TPU v7x, 512 devices: a whole 4x4x16 slice. The times are simulated.
512 devices in a mesh: ctx: 16 (over z), ch: 32 (over x, y, core).
Axes of the slice: x: 4, y: 4, z: 16, core: 2. Of those that a mesh axis runs over, the one named last changes fastest.
Arguments:
- features: bfloat16 [2, 16, 128, 3, 4096], P(None, 'ctx', None, None, 'ch'), may hold values from -6 to 6
- short_weight: bfloat16 [7, 3, 4096], P(None, None, 'ch'), may hold values from -2 to 2
- long_filter: bfloat16 [2, 16, 128, 4096], P(None, 'ctx', None, 'ch'), may hold values from -0.125 to 0.125
- skip_gain: float32 [4096], P('ch'), may hold values from -4 to 4
- out_weight: bfloat16 [4096, 4096], P('ch'), may hold values from -0.1875 to 0.1875
Outputs:
- mixed: bfloat16 [2, 16, 128, 4096], P(None, 'ctx', None, 'ch')
All inputs are finite; a program needn't handle non-finite values.
Results may differ from a plain program's by a relative error of at most 0.015.
Values may be sent and summed in bfloat16 or wider, within the bound.
No kernel may reach another device: no remote copies, remote signals or barrier semaphores. Data moves between devices by JAX's collectives and lax.ppermute only.
A program may use at most 64 MiB of HBM per device.

v0:
```python
import math

import jax
import jax.numpy as jnp
from jax import lax
from jax.sharding import PartitionSpec as P


def from_behind(value, axis, steps):
    count = lax.axis_size(axis)
    initial, last = (max(0, -steps), min(count, count - steps))
    return lax.ppermute(value, axis, [(source, source + steps) for source in range(initial, last)])


def transform_tables(length):
    period = 2 * length
    indices = jnp.arange(period, dtype=jnp.int32)
    phases = indices[:, None] * indices[None, :] % period
    angles = phases.astype(jnp.float32) * (2.0 * math.pi / period)
    cosine = jnp.cos(angles)
    sine_table = jnp.sin(angles)
    forward_full = jnp.concatenate([cosine, -sine_table], axis=0)
    forward_data = forward_full[:, :length]
    inverse = jnp.concatenate([cosine[:length], -sine_table[:length]], axis=1) / period
    return (forward_full, forward_data, inverse)


def complex_product(first, second):
    middle = first.shape[-2] // 2
    real_a = first[..., :middle, :]
    imag_a = first[..., middle:, :]
    real_b = second[..., :middle, :]
    imag_b = second[..., middle:, :]
    return jnp.concatenate(
        [real_a * real_b - imag_a * imag_b, real_a * imag_b + imag_a * real_b], axis=-2
    )


def featurize(tokens, before, kernel):
    extended = jnp.concatenate([before, tokens], axis=0).astype(jnp.float32)
    length = tokens.shape[0]
    margin_rows = kernel.shape[0] - 1
    summed = jnp.zeros(tokens.shape, jnp.float32)
    for offset in range(kernel.shape[0]):
        summed = (
            summed
            + kernel[offset].astype(jnp.float32)
            * extended[margin_rows - offset : margin_rows - offset + length]
        )
    return summed


def ordered(blocks):
    return jnp.concatenate([blocks[0], jnp.flip(blocks[1], axis=0)], axis=0)


def local(features, short_weight, long_filter, skip_gain, out_weight):
    pair_count = lax.axis_size("ctx")
    blocks_all = 2 * pair_count
    position = lax.axis_index("ctx")
    length = features.shape[2]
    margin_rows = short_weight.shape[0] - 1
    trailing = features[:, 0, length - margin_rows :]
    from_before = from_behind(trailing[0], "ctx", 1)
    from_after = from_behind(trailing[1], "ctx", -1)
    second_rim = jnp.where(position == pair_count - 1, trailing[0], from_after)
    first_feat = featurize(features[0, 0], from_before, short_weight)
    second_feat = featurize(features[1, 0], second_rim, short_weight)
    featured = jnp.stack([first_feat, second_feat], axis=0)
    queries = featured[:, :, 0]
    gated_keys = (featured[:, :, 1] * featured[:, :, 2]).astype(jnp.bfloat16)
    forward_full, forward_data, inverse = transform_tables(length)
    precise = lax.Precision.HIGHEST
    gathered = lax.all_gather(long_filter, "ctx", axis=1, tiled=True)
    lag_order = ordered(gathered)
    padded = jnp.concatenate(
        [jnp.zeros((1,) + lag_order.shape[1:], lag_order.dtype), lag_order], axis=0
    )
    lag_spectra = jnp.einsum(
        "fn,knc->kfc", forward_data, padded.astype(jnp.float32), precision=precise
    )
    frequency = jnp.arange(4 * length, dtype=jnp.int32) % (2 * length)
    parity = jnp.where(frequency % 2 == 0, 1.0, -1.0).astype(jnp.float32)[:, None]
    responses = lag_spectra[1:] + parity * lag_spectra[:-1]
    targets = jnp.stack([position, blocks_all - 1 - position])

    def absorb(totals, spectrum, source):
        for target_slot in range(2):
            distance = targets[target_slot] - source
            clamped = jnp.maximum(distance, 0)
            response = lax.dynamic_index_in_dim(responses, clamped, 0, keepdims=False)
            contribution = complex_product(response, spectrum)
            totals = totals.at[target_slot].add(jnp.where(distance >= 0, contribution, 0.0))
        return totals

    zeroed = jnp.zeros((2, 4 * length, gated_keys.shape[-1]), jnp.float32)

    def transform_block(values):
        return jnp.dot(forward_data, values.astype(jnp.float32), precision=precise)

    totals = zeroed
    shards = lax.all_gather(gated_keys[:, None], "ctx", axis=1, tiled=True)

    def advance(running, offset):
        couple = lax.dynamic_index_in_dim(shards, offset, 1, keepdims=False)
        running = absorb(running, transform_block(couple[0]), offset)
        running = absorb(running, transform_block(couple[1]), blocks_all - 1 - offset)
        return (running, None)

    totals, unused = lax.scan(advance, totals, jnp.arange(shards.shape[1], dtype=jnp.int32))
    convolved = jnp.einsum("tf,hfc->htc", inverse, totals, precision=precise)
    activated = (queries * (convolved + skip_gain * gated_keys.astype(jnp.float32))).astype(
        jnp.bfloat16
    )
    token_rows = activated.reshape(2 * length, activated.shape[-1])
    channels = token_rows.shape[1]
    owned = lax.psum_scatter(
        lax.dot_general(
            out_weight, token_rows, (((0,), (1,)), ((), ())), preferred_element_type=jnp.float32
        ).astype(jnp.bfloat16),
        "ch",
        scatter_dimension=0,
        tiled=True,
    ).astype(jnp.float32)
    result = owned.T
    return result.astype(jnp.bfloat16).reshape(2, 1, length, channels)


def solution(mesh):
    in_specs = (
        P(None, "ctx", None, None, "ch"),
        P(None, None, "ch"),
        P(None, "ctx", None, "ch"),
        P("ch"),
        P("ch", None),
    )
    out_specs = P(None, "ctx", None, "ch")
    return jax.shard_map(local, mesh=mesh, in_specs=in_specs, out_specs=out_specs, check_vma=False)
```

profile of v0, /device:TPU:1, one launch (start us, length us, event | category | flops | bytes accessed | tf_op | source)
XLA Modules:
  0.0 414.4 jit_solution(9419086972166073403)
XLA Ops:
  6.5 1.7 copy.15
  9.0 4.3 %collective-permute-start = (bf16[6,3,128]{2,0,1:T(8,128)(2,1)S(1)}, bf16[6,3,128]{2,0,1:T(8,128)(2,1)S(1)}, u32[]{:S(2)}, u32[]{:S(2)}) collective-permute-start(bf16[6,3,128]{2,0,1:T(8,128)(2,1)S(1)} %get-tuple-element.184), channel_id=1, source_target_pairs={{0,32},{32,64},{64,96},{96,128},{128,160},{160,192},{192,224},{224... | collective-permute-start | bytes 13832 | tf_op jit(solution)/shard_map/ppermute | solution.py:12
  13.3 1.3 collective-permute-start.1
  16.6 1.3 collective-permute-done.1
  21.9 53.2 %all-gather.4.cloned.1.call-done = bf16[2,16,128,128]{2,3,1,0:T(8,128)(2,1)} async-done(((bf16[2,1,128,128]{2,3,1,0:T(8,128)(2,1)}), bf16[2,16,128,128]{2,3,1,0:T(8,128)(2,1)}) %all-gather.4.cloned.1.call-update) | async-done | bytes 1048592 | tf_op jit(solution)/shard_map/all_gather | solution.py:74
  75.1 1.3 slice_bitcast_fusion.1
  76.4 3.7 convolution_bitcast_fusion.2
  80.1 4.5 %fusion.7 = f32[32,512,128]{1,2,0:T(8,128)} fusion(f32[33,512,128]{1,2,0:T(8,128)S(1)} %convolution_bitcast_fusion.2, f32[512]{0:T(512)S(1)} %fusion.56), kind=kLoop, calls=%fused_computation.35 | loop fusion | flops 4194304 | bytes 25167872 | tf_op jit(solution)/shard_map/add | solution.py:84
  84.7 60.3 %all-gather.6.cloned.1.call-done = bf16[2,2048,1,128]{3,1,0,2:T(8,128)(2,1)} async-done(((bf16[2,128,1,128]{3,1,0,2:T(8,128)(2,1)}), bf16[2,2048,1,128]{3,1,0,2:T(8,128)(2,1)}) %all-gather.6.cloned.1.call-update) | async-done | bytes 1048592 | tf_op jit(solution)/shard_map/all_gather | solution.py:102
  145.0 149.5 %while.16 = (s32[]{:T(128)}, f32[2,512,128]{1,2,0:T(8,128)S(1)}, s32[16]{0:T(128)S(1)}, s32[]{:T(128)}, f32[32,512,128]{1,2,0:T(8,128)}, /*index=5*/bf16[2,16,12...) while((s32[]{:T(128)}, f32[2,512,128]{1,2,0:T(8,128)S(1)}, ...), condition=%wide.region_1.2_spmd, body=%wide.region_0.1_spmd.sunk | while | flops 202899456 | bytes 6881675 | solution.py:110
  149.9 1.2 subtract_bitcast_fusion.6
  153.0 1.2 subtract_bitcast_fusion.7
  159.3 1.2 subtract_bitcast_fusion.6
  162.4 1.2 subtract_bitcast_fusion.7
  168.6 1.2 subtract_bitcast_fusion.6
  171.7 1.2 subtract_bitcast_fusion.7
  178.0 1.2 subtract_bitcast_fusion.6
  181.1 1.2 subtract_bitcast_fusion.7
  187.3 1.2 subtract_bitcast_fusion.6
  190.4 1.2 subtract_bitcast_fusion.7
  196.7 1.2 subtract_bitcast_fusion.6
  198.7 1.1 convolution_bitcast_fusion.7
  199.7 1.2 subtract_bitcast_fusion.7
  206.0 1.2 subtract_bitcast_fusion.6
  209.1 1.2 subtract_bitcast_fusion.7
  215.3 1.2 subtract_bitcast_fusion.6
  217.3 1.1 convolution_bitcast_fusion.7
  218.4 1.2 subtract_bitcast_fusion.7
  224.7 1.2 subtract_bitcast_fusion.6
  226.7 1.1 convolution_bitcast_fusion.7
  227.8 1.2 subtract_bitcast_fusion.7
  234.0 1.2 subtract_bitcast_fusion.6
  237.1 1.2 subtract_bitcast_fusion.7
  243.4 1.2 subtract_bitcast_fusion.6
  246.5 1.2 subtract_bitcast_fusion.7
  252.7 1.2 subtract_bitcast_fusion.6
  255.8 1.2 subtract_bitcast_fusion.7
  262.1 1.2 subtract_bitcast_fusion.6
  265.2 1.2 subtract_bitcast_fusion.7
  271.4 1.2 subtract_bitcast_fusion.6
  274.5 1.2 subtract_bitcast_fusion.7
  280.8 1.2 subtract_bitcast_fusion.6
  283.8 1.2 subtract_bitcast_fusion.7
  290.1 1.2 subtract_bitcast_fusion.6
  293.2 1.2 subtract_bitcast_fusion.7
  295.9 2.5 copy.19
  298.4 107.8 %reduce-scatter.4.cloned.1.call-done = bf16[128,256]{1,0:T(8,128)(2,1)} async-done(((bf16[4096,256]{1,0:T(8,128)(2,1)}), bf16[128,256]{1,0:T(8,128)(2,1)}) %reduce-scatter.4.cloned.1.call-update) | async-done | bytes 65552
  406.3 1.6 copy.20
  (147 shorter events, 53.1 us)
Async XLA Ops:
  6.5 288.7 %copy-start = (bf16[128,4096]{1,0:T(8,128)(2,1)S(1)}, bf16[128,4096]{1,0:T(8,128)(2,1)}, u32[]{:S(2)}) copy-start(bf16[128,4096]{1,0:T(8,128)(2,1)} %param.19) | copy-start | bytes 3145732
  6.5 68.6 %all-gather.4.cloned.1.call-start = ((), (), s32[]{:S(2)}) async-start(), calls=%async_computation.1 | async-start | bytes 1114112 | tf_op jit(solution)/shard_map/all_gather | solution.py:74
  8.2 136.7 %all-gather.6.cloned.1.call-start = ((), (), s32[]{:S(2)}) async-start(), calls=%async_computation.2 | async-start | bytes 1114112 | tf_op jit(solution)/shard_map/all_gather | solution.py:102
  9.0 9.6 %collective-permute-start = (bf16[6,3,128]{2,0,1:T(8,128)(2,1)S(1)}, bf16[6,3,128]{2,0,1:T(8,128)(2,1)S(1)}, u32[]{:S(2)}, u32[]{:S(2)}) collective-permute-start(bf16[6,3,128]{2,0,1:T(8,128)(2,1)S(1)} %get-tuple-element.184), channel_id=1, source_target_pairs={{0,32},{32,64},{64,96},{96,128},{128,160},{160,192},{192,224},{224... | collective-permute-start | bytes 13832 | tf_op jit(solution)/shard_map/ppermute | solution.py:12
  13.3 4.6 %collective-permute-start.1 = (bf16[6,3,128]{2,0,1:T(8,128)(2,1)S(1)}, bf16[6,3,128]{2,0,1:T(8,128)(2,1)S(1)}, u32[]{:S(2)}, u32[]{:S(2)}) collective-permute-start(bf16[6,3,128]{2,0,1:T(8,128)(2,1)S(1)} %get-tuple-element.183), channel_id=1, source_target_pairs={{32,0},{64,32},{96,64},{128,96},{160,128},{192,160},{224,192},{256... | collective-permute-start | bytes 13832 | tf_op jit(solution)/shard_map/ppermute | solution.py:12
  19.7 386.6 %reduce-scatter.4.cloned.1.call-start = ((), (), s32[]{:S(2)}) async-start(), calls=%async_computation.3 | async-start | bytes 2162688
  145.0 149.5 %copy-start.1 = (bf16[2,128,1,128]{3,1,0,2:T(8,128)(2,1)S(1)}, bf16[2,128,1,128]{3,1,0,2:T(8,128)(2,1)}, u32[]{:S(2)}) copy-start(bf16[2,128,1,128]{3,1,0,2:T(8,128)(2,1)} %fusion.44) | copy-start | bytes 196612
  145.0 149.5 %copy-start.2 = (f32[128]{0:T(128)S(1)}, f32[128]{0:T(128)}, u32[]{:S(2)}) copy-start(f32[128]{0:T(128)} %param.18) | copy-start | bytes 1540
Sparse Core Ops, SparseCore 0:
  9.4 65.6 all-gather.3
  77.2 67.7 all-gather.5
  298.6 107.6 reduce-scatter.3
where the time goes:
time: 419 us; the launch traced here: 414 us
  waiting for transfers between devices  223 us (53%)
  loops' own time  64 us (15%)
  other arithmetic  51 us (12%)
  matrix products  39.4 us (9%)
  local copies, waits for them, and re-layouts  18.2 us (4%)
  between operations  13.3 us (3%)
  starting transfers between devices  5.72 us (1%)
    unnamed x4, waiting for transfers between devices  108 us
    another operation x1, loops' own time, local(): lax.scan(advance, totals, jnp.arange(shards.shape[1], dtype=jnp.int32))  64 us
    all_gather x1, waiting for transfers between devices, local(): shards = lax.all_gather(gated_keys[:, None], 'ctx', axis=1, tiled=True)  60.3 us
    all_gather x1, waiting for transfers between devices, local(): gathered = lax.all_gather(long_filter, 'ctx', axis=1, tiled=True)  53.2 us
    concatenate x32, other arithmetic, complex_product(): jnp.concatenate([real_a * real_b - imag_a * imag_b, real_a * imag_b + ima...  37.2 us
    dot_general x32, matrix products, transform_block(): return jnp.dot(forward_data, values.astype(jnp.float32), precision=precise)  34.4 us
    dynamic_slice x16, local copies, waits for them, and re-layouts, local(): lax.scan(advance, totals, jnp.arange(shards.shape[1], dtype=jnp.int32))  9.38 us
  transfers between devices with their start and end apart: 5, of which 4 were waited for; matrix products, arithmetic and copies ran while one was open for 4% of the time, Pallas kernels for 0%

commit v1 on v0

v1 whole, which is shorter than its diff:
```python
import math

import jax
import jax.numpy as jnp
import numpy as np
from jax import lax
from jax.experimental import pallas as pl
from jax.experimental.pallas import tpu as pltpu
from jax.sharding import Mesh, PartitionSpec as P

INTERPRET = False
LANES = 128
PERIOD = 2 * LANES


def tables():
    t = np.arange(LANES)[:, None]
    k = np.arange(LANES)[None, :]
    angle = 2.0 * math.pi * ((t * k) % PERIOD) / PERIOD
    sign = np.where(t % 2 == 0, 1.0, -1.0)
    cosine, sine = np.cos(angle), -np.sin(angle)
    forward = np.concatenate([cosine, np.where(k == 0, sign, sine)], axis=1)
    scale = np.where(k == 0, 1.0, 2.0) / PERIOD
    inverse = np.concatenate(
        [cosine * scale, np.where(k == 0, sign / PERIOD, sine * scale)], axis=1
    ).T
    high = forward.astype(jnp.bfloat16)
    low = (forward - high.astype(np.float64)).astype(jnp.bfloat16)
    return np.stack([high, low]), inverse.astype(np.float32)


def pack_kernel(index_ref, features_ref, filter_ref, taps_ref, gain_ref, out_ref, weights_ref, rows, turned):
    groups = out_ref.shape[0]
    channels = LANES // groups
    streams = features_ref.shape[1]
    for half in range(2):
        for stream in range(streams):
            tile = features_ref[half, stream].astype(jnp.float32).T.astype(jnp.bfloat16)
            out_ref[:, half * streams + stream] = tile.reshape(groups, channels, LANES)
        tile = filter_ref[half].astype(jnp.float32).T.astype(jnp.bfloat16)
        out_ref[:, 2 * streams + half] = tile.reshape(groups, channels, LANES)
    rows[...] = jnp.zeros_like(rows)
    taps = taps_ref.shape[1]
    for stream in range(streams):
        rows[stream * 8 : stream * 8 + taps] = taps_ref[stream].astype(jnp.float32)
    rows[streams * 8 : streams * 8 + 1] = gain_ref[...]
    turned[...] = rows[...].T
    first = pl.multiple_of(index_ref[0] * channels, channels)
    weights_ref[...] = turned[pl.ds(first, channels)]


def mix_kernel(packed_ref, weights_ref, forward_ref, inverse_ref, out_ref, query, keys, lags, key_spec, lag_spec, resp, total):
    pairs = packed_ref.shape[0]
    blocks = 2 * pairs
    channels = packed_ref.shape[2]
    taps = 7
    lane = lax.broadcasted_iota(jnp.int32, (channels, LANES), 1)

    def place(block):
        return (block, 0) if block < pairs else (blocks - 1 - block, 1)

    def span(block):
        return slice(block * channels, (block + 1) * channels)

    def column(index):
        return jnp.broadcast_to(weights_ref[:, index : index + 1], (channels, LANES))

    for block in range(blocks):
        source, half = place(block)
        lags[span(block)] = packed_ref[source, 6 + half]
    for stream in (1, 2, 0):
        weight = [column(stream * 8 + i) for i in range(taps)]
        turned_before = [jnp.zeros((channels, LANES), jnp.float32)] * taps
        for block in range(blocks):
            source, half = place(block)
            value = packed_ref[source, half * 3 + stream].astype(jnp.float32)
            summed = weight[0] * value
            turned = [value]
            for i in range(1, taps):
                rolled = pltpu.roll(value, i, 1)
                turned.append(rolled)
                summed = summed + weight[i] * jnp.where(lane >= i, rolled, turned_before[i])
            turned_before = turned
            if stream == 1:
                total[span(block), :LANES] = summed
            elif stream == 2:
                keys[span(block)] = (total[span(block), :LANES] * summed).astype(jnp.bfloat16)
            else:
                query[span(block)] = summed

    def transform(values):
        return jnp.dot(values, forward_ref[0], preferred_element_type=jnp.float32) + jnp.dot(
            values, forward_ref[1], preferred_element_type=jnp.float32
        )

    key_spec[...] = transform(keys[...])
    lag_spec[...] = transform(lags[...])
    parity = jnp.where(lane % 2 == 0, 1.0, -1.0).astype(jnp.float32)
    for block in range(blocks):
        real = lag_spec[span(block), :LANES]
        imag = lag_spec[span(block), LANES:]
        if block:
            real = real + parity * lag_spec[span(block - 1), :LANES]
            imag = imag + parity * lag_spec[span(block - 1), LANES:]
        resp[0, span(block)] = real
        resp[1, span(block)] = jnp.where(lane == 0, 0.0, imag)
        resp[2, span(block)] = jnp.where(lane == 0, imag, real)
    group = 4
    for base in range(0, blocks, group):
        sums = [[None, None] for _ in range(group)]
        for block in range(base + group):
            real = key_spec[span(block), :LANES]
            imag = key_spec[span(block), LANES:]
            for j in range(group):
                gap = base + j - block
                if gap < 0:
                    continue
                first = resp[0, span(gap)]
                cross = resp[1, span(gap)]
                second = resp[2, span(gap)]
                out_real = real * first - imag * cross
                out_imag = real * cross + imag * second
                if sums[j][0] is None:
                    sums[j] = [out_real, out_imag]
                else:
                    sums[j] = [sums[j][0] + out_real, sums[j][1] + out_imag]
        for j in range(group):
            total[span(base + j), :LANES] = sums[j][0]
            total[span(base + j), LANES:] = sums[j][1]
    convolved = jnp.dot(
        total[...], inverse_ref[...], preferred_element_type=jnp.float32, precision=lax.Precision.HIGHEST
    )
    total[:, :LANES] = convolved
    gain = column(24)
    for block in range(blocks):
        target, half = place(block)
        inner = total[span(block), :LANES] + gain * keys[span(block)].astype(jnp.float32)
        out_ref[target, half] = (query[span(block)] * inner).astype(jnp.bfloat16)


def project_kernel(index_ref, own_ref, other_ref, own_weight_ref, other_weight_ref, out_ref):
    chips, rows, width = out_ref.shape
    depth = own_weight_ref.shape[0]
    core = index_ref[0]
    lhs = []
    for half in range(2):
        parts = [
            ref[:, half].reshape(depth, LANES).astype(jnp.float32).T.astype(jnp.bfloat16)
            for ref in (own_ref, other_ref)
        ]
        lhs.append(jnp.concatenate(parts, axis=1))
    lhs = jnp.concatenate(lhs, axis=0)
    for chip in range(chips):
        columns = pl.ds(pl.multiple_of((2 * chip + core) * width, width), width)
        weight = jnp.concatenate([own_weight_ref[:, columns], other_weight_ref[:, columns]], axis=0)
        out_ref[chip] = jnp.dot(lhs, weight, preferred_element_type=jnp.float32).astype(jnp.bfloat16)


def local(features, short_weight, long_filter, skip_gain, out_weight):
    pairs = lax.axis_size("ctx")
    chips = lax.axis_size("chip")
    length = features.shape[2]
    width = features.shape[4]
    channels = width // pairs
    position = lax.axis_index("ctx").astype(jnp.int32).reshape(1)
    core = lax.axis_index("core").astype(jnp.int32).reshape(1)
    other_weight = lax.ppermute(out_weight, "core", [(0, 1), (1, 0)])
    tiles = jnp.transpose(features, (0, 1, 3, 2, 4)).reshape(2, 3, length, width)
    taps = jnp.transpose(short_weight, (1, 0, 2))
    scalars = pl.BlockSpec(memory_space=pltpu.SMEM)
    vmem = pl.BlockSpec(memory_space=pltpu.VMEM)
    packed, weights = pl.pallas_call(
        pack_kernel,
        out_shape=(
            jax.ShapeDtypeStruct((pairs, 8, channels, length), jnp.bfloat16),
            jax.ShapeDtypeStruct((channels, LANES), jnp.float32),
        ),
        in_specs=[scalars] + [vmem] * 4,
        out_specs=(vmem, vmem),
        scratch_shapes=[pltpu.VMEM((LANES, LANES), jnp.float32)] * 2,
        cost_estimate=pl.CostEstimate(flops=1000000, bytes_accessed=600000, transcendentals=0),
        interpret=INTERPRET,
    )(position, tiles, long_filter.reshape(2, length, width), taps, skip_gain.reshape(1, width))
    packed = lax.all_to_all(packed, "ctx", 0, 0, tiled=True)
    forward, inverse = tables()
    rows = 2 * pairs * channels
    activated = pl.pallas_call(
        mix_kernel,
        out_shape=jax.ShapeDtypeStruct((pairs, 2, channels, length), jnp.bfloat16),
        in_specs=[vmem] * 4,
        out_specs=vmem,
        scratch_shapes=[
            pltpu.VMEM((rows, LANES), jnp.float32),
            pltpu.VMEM((rows, LANES), jnp.bfloat16),
            pltpu.VMEM((rows, LANES), jnp.bfloat16),
            pltpu.VMEM((rows, PERIOD), jnp.float32),
            pltpu.VMEM((rows, PERIOD), jnp.float32),
            pltpu.VMEM((3, rows, LANES), jnp.float32),
            pltpu.VMEM((rows, PERIOD), jnp.float32),
        ],
        cost_estimate=pl.CostEstimate(flops=100000000, bytes_accessed=600000, transcendentals=0),
        interpret=INTERPRET,
    )(packed, weights, jnp.asarray(forward), jnp.asarray(inverse))
    own = lax.all_to_all(activated, "ctx", 0, 0, tiled=True)
    other = lax.ppermute(own, "core", [(0, 1), (1, 0)])
    partial = pl.pallas_call(
        project_kernel,
        out_shape=jax.ShapeDtypeStruct((chips, 2 * length, width), jnp.bfloat16),
        in_specs=[scalars] + [vmem] * 4,
        out_specs=vmem,
        cost_estimate=pl.CostEstimate(flops=268435456, bytes_accessed=3300000, transcendentals=0),
        interpret=INTERPRET,
    )(core, own, other, out_weight, other_weight)
    shares = lax.all_to_all(partial, "chip", 0, 0, tiled=True)
    mixed = jnp.sum(shares.astype(jnp.float32), axis=0).astype(jnp.bfloat16)
    return mixed.reshape(2, 1, length, width)


def solution(mesh):
    pairs, parts = mesh.shape["ctx"], mesh.shape["ch"]
    split = Mesh(mesh.devices.reshape(pairs, parts // 2, 2), ("ctx", "chip", "core"))
    ch = ("chip", "core")
    in_specs = (
        P(None, "ctx", None, None, ch),
        P(None, None, ch),
        P(None, "ctx", None, ch),
        P(ch),
        P(ch, None),
    )
    return jax.shard_map(
        local, mesh=split, in_specs=in_specs, out_specs=P(None, "ctx", None, ch), check_vma=False
    )
```

time: 419 us -> 90.1 us (0.22)
  waiting for transfers between devices: 223 us -> 11.8 us
  loops' own time: 64 us -> 0 us
  other arithmetic: 51 us -> 0.77 us
  blocking collectives: 0 us -> 44.6 us
  matrix products: 39.4 us -> 0 us
  starting transfers between devices: 5.72 us -> 22.7 us
  local copies, waits for them, and re-layouts: 18.2 us -> 1.33 us
  between operations: 13.3 us -> 0.05 us
  Pallas kernels: 0 us -> 8.38 us
    all_gather x2 -> x0, waiting for transfers between devices: 114 us -> none  [the longest x1 60.3 us: local(): shards = lax.all_gather(gated_keys[:, None], 'ctx', axis=1, tiled=True)]
    unnamed x4 -> x0, waiting for transfers between devices: 108 us -> none
    another operation x1 -> x0, loops' own time: 64 us -> none  [local(): lax.scan(advance, totals, jnp.arange(shards.shape[1], dtype=jnp.int32))]
    all_to_all x0 -> x2, blocking collectives: none -> 44.6 us  [the longest x1 22.8 us: local(): shares = lax.all_to_all(partial, 'chip', 0, 0, tiled=True)]
    dot_general x35 -> x0, matrix products: 39.4 us -> none  [the longest x32 34.4 us: transform_block(): return jnp.dot(forward_data, values.astype(jnp.float32), precision=precise)]
    concatenate x33 -> x0, other arithmetic: 37.3 us -> none  [the longest x32 37.2 us: complex_product(): jnp.concatenate([real_a * real_b - imag_a * imag_b, real_a * imag_b + ima...]
    all_to_all x0 -> x1, starting transfers between devices: none -> 15.7 us  [local(): packed = lax.all_to_all(packed, 'ctx', 0, 0, tiled=True)]
    all_to_all x0 -> x1, waiting for transfers between devices: none -> 10.9 us  [local(): packed = lax.all_to_all(packed, 'ctx', 0, 0, tiled=True)]
  transfers between devices with their start and end apart: 5 -> 3, of which waited for: 4 -> 2; matrix products, arithmetic and copies ran while one was open for 4% -> 0% of each run, Pallas kernels for 0% -> 4%
where the time goes in v1:
time: 90.1 us; the launch traced here: 89.6 us
  blocking collectives  44.6 us (50%)
  starting transfers between devices  22.7 us (25%)
  waiting for transfers between devices  11.8 us (13%)
  Pallas kernels  8.38 us (9%)
  local copies, waits for them, and re-layouts  1.33 us (1%)
    all_to_all x1, blocking collectives, local(): shares = lax.all_to_all(partial, 'chip', 0, 0, tiled=True)  22.8 us
    all_to_all x1, blocking collectives, local(): own = lax.all_to_all(activated, 'ctx', 0, 0, tiled=True)  21.9 us
    all_to_all x1, starting transfers between devices, local(): packed = lax.all_to_all(packed, 'ctx', 0, 0, tiled=True)  15.7 us
    all_to_all x1, waiting for transfers between devices, local(): packed = lax.all_to_all(packed, 'ctx', 0, 0, tiled=True)  10.9 us
    ppermute x1, starting transfers between devices, local(): other = lax.ppermute(own, 'core', [(0, 1), (1, 0)])  4.08 us
    pallas_call x1, Pallas kernels, local(): pl.pallas_call(project_kernel, out_shape=jax.ShapeDtypeStruct((chips, 2 *...  3.42 us
    pallas_call x1, Pallas kernels, local(): pl.pallas_call(mix_kernel, out_shape=jax.ShapeDtypeStruct((pairs, 2, chan...  3.15 us
    ppermute x1, starting transfers between devices, local(): other_weight = lax.ppermute(out_weight, 'core', [(0, 1), (1, 0)])  2.87 us
  transfers between devices with their start and end apart: 3, of which 2 were waited for; matrix products, arithmetic and copies ran while one was open for 0% of the time, Pallas kernels for 4%

profile of v1, /device:TPU:1, one launch (start us, length us, event | category | flops | bytes accessed | tf_op | source)
XLA Modules:
  0.0 89.6 jit_solution(1804494797660313140)
XLA Ops:
  0.0 1.8 %shard_map.73 = (bf16[16,8,8,128]{3,2,1,0:T(8,128)(2,1)}, f32[8,128]{1,0:T(8,128)}) custom-call(s32[1]{0:T(128)} %bitcast.1.index_ref, bf16[2,3,128,128]{3,2,1,0:T(8,128)(2,1)} %bitcast.11, bf16[2,128,128]{2,1,0:T(8,128)(2,1)} %bitcast.12, bf16[3,7,128]{2,1,0:T(8,128)(2,1)} %bitcast.13, f32[1,128]{1,0:T(1,128)} %bitcast.14), custom_call_target="tpu_custom_call" | custom-call | flops 1000000 | bytes 600000 | tf_op jit(solution)/shard_map/pallas_call | solution.py:172
  1.8 15.7 %all-to-all-start = ((bf16[16,8,8,128]{3,2,1,0:T(8,128)(2,1)}), bf16[16,8,8,128]{3,2,1,0:T(8,128)(2,1)S(1)}, u32[]{:S(2)}, u32[]{:S(2)}) async-start(bf16[16,8,8,128]{3,2,1,0:T(8,128)(2,1)} %get-tuple-element.7), calls=%async_computation | async-start | bytes 524288 | tf_op jit(solution)/shard_map/all_to_all | solution.py:184
  17.6 2.9 %collective-permute-start.1 = (bf16[128,4096]{1,0:T(8,128)(2,1)}, bf16[128,4096]{1,0:T(8,128)(2,1)S(1)}, u32[]{:S(2)}, u32[]{:S(2)}) collective-permute-start(bf16[128,4096]{1,0:T(8,128)(2,1)} %own_weight_ref.1), channel_id=1, source_target_pairs={{0,1},{1,0},{2,3},{3,2},{4,5},{5,4},{6,7},{7,6},{8,9},{9,8},{10,11... | collective-permute-start | bytes 3145736 | tf_op jit(solution)/shard_map/ppermute | solution.py:167
  20.4 10.9 %all-to-all-done.packed_ref = bf16[16,8,8,128]{3,2,1,0:T(8,128)(2,1)S(1)} async-done(((bf16[16,8,8,128]{3,2,1,0:T(8,128)(2,1)}), bf16[16,8,8,128]{3,2,1,0:T(8,128)(2,1)S(1)}, u32[]{:S(2)}, u32[]{:S(2)}) %all-to-all-start) | async-done | bytes 262176 | tf_op jit(solution)/shard_map/all_to_all | solution.py:184
  31.3 0.0 copy-start
  31.3 0.7 copy-done
  32.0 3.1 %shard_map.74 = bf16[16,2,8,128]{3,2,1,0:T(8,128)(2,1)} custom-call(bf16[16,8,8,128]{3,2,1,0:T(8,128)(2,1)} %copy-done, f32[8,128]{1,0:T(8,128)} %get-tuple-element.8.weights_ref, bf16[2,128,256]{2,1,0:T(8,128)(2,1)} %constant.17.clone.forward_ref, f32[256,128]{1,0:T(8,128)} %constant.18.clone.inverse_ref), custom_call_target="tpu_custom_call" | custom-call | flops 100000000 | bytes 600000 | tf_op jit(solution)/shard_map/pallas_call | solution.py:187
  35.2 21.9 %all_to_all.15.own_ref = bf16[16,2,8,128]{3,2,1,0:T(8,128)(2,1)S(1)} all-to-all(bf16[16,2,8,128]{3,2,1,0:T(8,128)(2,1)} %shard_map.74), channel_id=1, replica_groups=mesh['ctx'=16,'chip'=16,'core'=2] {'ctx'}, dimensions={0} | all-to-all | bytes 131072 | tf_op jit(solution)/shard_map/all_to_all | solution.py:204
  57.1 0.0 copy-start.2
  57.1 4.1 %collective-permute-start = (bf16[16,2,8,128]{3,2,1,0:T(8,128)(2,1)S(1)}, bf16[16,2,8,128]{3,2,1,0:T(8,128)(2,1)S(1)}, u32[]{:S(2)}, u32[]{:S(2)}) collective-permute-start(bf16[16,2,8,128]{3,2,1,0:T(8,128)(2,1)S(1)} %all_to_all.15.own_ref), channel_id=1, source_target_pairs={{0,1},{1,0},{2,3},{3,2},{4,5},{5,4},{6,7},{7,6},{8,9},{9,8},{10,11... | collective-permute-start | bytes 196616 | tf_op jit(solution)/shard_map/ppermute | solution.py:205
  61.2 0.0 collective-permute-done.1.other_weight_ref
  61.2 0.0 copy-start.1
  61.2 0.9 collective-permute-done.other_ref
  62.0 0.0 copy-start.3
  62.0 0.0 copy-done.2
  62.0 0.1 copy-done.1
  62.1 0.5 copy-done.3
  62.7 3.4 %shard_map.75 = bf16[16,256,128]{2,1,0:T(8,128)(2,1)} custom-call(s32[1]{0:T(128)} %bitcast.index_ref, bf16[16,2,8,128]{3,2,1,0:T(8,128)(2,1)} %copy-done.2, bf16[16,2,8,128]{3,2,1,0:T(8,128)(2,1)} %copy-done.3, bf16[128,4096]{1,0:T(8,128)(2,1)} %own_weight_ref.1, bf16[128,4096]{1,0:T(8,128)(2,1)} %copy-done.1), custom_call_target="tpu_custom_call" | custom-call | flops 268435456 | bytes 3300000 | tf_op jit(solution)/shard_map/pallas_call | solution.py:206
  66.1 22.8 %all_to_all.16 = bf16[16,256,128]{2,1,0:T(8,128)(2,1)S(1)} all-to-all(bf16[16,256,128]{2,1,0:T(8,128)(2,1)} %shard_map.75), channel_id=1, replica_groups=mesh['ctx'=16,'chip'=16,'core'=2] {'chip'}, dimensions={0} | all-to-all | bytes 2097152 | tf_op jit(solution)/shard_map/all_to_all | solution.py:214
  88.8 0.8 reduce_sum.12
Async XLA Ops:
  1.8 29.5 %all-to-all-start = ((bf16[16,8,8,128]{3,2,1,0:T(8,128)(2,1)}), bf16[16,8,8,128]{3,2,1,0:T(8,128)(2,1)S(1)}, u32[]{:S(2)}, u32[]{:S(2)}) async-start(bf16[16,8,8,128]{3,2,1,0:T(8,128)(2,1)} %get-tuple-element.7), calls=%async_computation | async-start | bytes 524288 | tf_op jit(solution)/shard_map/all_to_all | solution.py:184
  17.6 43.6 %collective-permute-start.1 = (bf16[128,4096]{1,0:T(8,128)(2,1)}, bf16[128,4096]{1,0:T(8,128)(2,1)S(1)}, u32[]{:S(2)}, u32[]{:S(2)}) collective-permute-start(bf16[128,4096]{1,0:T(8,128)(2,1)} %own_weight_ref.1), channel_id=1, source_target_pairs={{0,1},{1,0},{2,3},{3,2},{4,5},{5,4},{6,7},{7,6},{8,9},{9,8},{10,11... | collective-permute-start | bytes 3145736 | tf_op jit(solution)/shard_map/ppermute | solution.py:167
  31.3 0.7 copy-start
  57.1 5.0 %copy-start.2 = (bf16[16,2,8,128]{3,2,1,0:T(8,128)(2,1)}, bf16[16,2,8,128]{3,2,1,0:T(8,128)(2,1)S(1)}, u32[]{:S(2)}) copy-start(bf16[16,2,8,128]{3,2,1,0:T(8,128)(2,1)S(1)} %all_to_all.15.own_ref) | copy-start | bytes 196612
  57.1 5.0 %collective-permute-start = (bf16[16,2,8,128]{3,2,1,0:T(8,128)(2,1)S(1)}, bf16[16,2,8,128]{3,2,1,0:T(8,128)(2,1)S(1)}, u32[]{:S(2)}, u32[]{:S(2)}) collective-permute-start(bf16[16,2,8,128]{3,2,1,0:T(8,128)(2,1)S(1)} %all_to_all.15.own_ref), channel_id=1, source_target_pairs={{0,1},{1,0},{2,3},{3,2},{4,5},{5,4},{6,7},{7,6},{8,9},{9,8},{10,11... | collective-permute-start | bytes 196616 | tf_op jit(solution)/shard_map/ppermute | solution.py:205
  61.2 1.0 %copy-start.1 = (bf16[128,4096]{1,0:T(8,128)(2,1)}, bf16[128,4096]{1,0:T(8,128)(2,1)S(1)}, u32[]{:S(2)}) copy-start(bf16[128,4096]{1,0:T(8,128)(2,1)S(1)} %collective-permute-done.1.other_weight_ref) | copy-start | bytes 3145732
  62.0 0.6 copy-start.3

commit v2 on v1

--- a/solution.py
+++ b/solution.py
@@ -9,8 +9,13 @@
 from jax.sharding import Mesh, PartitionSpec as P
 
 INTERPRET = False
+MIB = 2**20
 LANES = 128
 PERIOD = 2 * LANES
+
+
+def in_hbm(value):
+    return pltpu.with_memory_space_constraint(value, pltpu.HBM)
 
 
 def tables():
@@ -29,18 +34,35 @@
     return np.stack([high, low]), inverse.astype(np.float32)
 
 
-def pack_kernel(index_ref, features_ref, filter_ref, taps_ref, gain_ref, out_ref, weights_ref, rows, turned):
+def pack_kernel(
+    index_ref, features_hbm, filter_hbm, taps_hbm, gain_hbm, out_ref, weights_ref,
+    features_ref, filter_ref, taps_ref, gain_ref, rows, turned, sems,
+):
     groups = out_ref.shape[0]
     channels = LANES // groups
     streams = features_ref.shape[1]
+    copies = [
+        pltpu.make_async_copy(features_hbm.at[0], features_ref.at[0], sems.at[0]),
+        pltpu.make_async_copy(features_hbm.at[1], features_ref.at[1], sems.at[1]),
+        pltpu.make_async_copy(filter_hbm, filter_ref, sems.at[2]),
+        pltpu.make_async_copy(taps_hbm, taps_ref, sems.at[3]),
+        pltpu.make_async_copy(gain_hbm, gain_ref, sems.at[4]),
+    ]
+    for copy in copies:
+        copy.start()
     for half in range(2):
+        copies[half].wait()
         for stream in range(streams):
             tile = features_ref[half, stream].astype(jnp.float32).T.astype(jnp.bfloat16)
             out_ref[:, half * streams + stream] = tile.reshape(groups, channels, LANES)
+    copies[2].wait()
+    for half in range(2):
         tile = filter_ref[half].astype(jnp.float32).T.astype(jnp.bfloat16)
         out_ref[:, 2 * streams + half] = tile.reshape(groups, channels, LANES)
     rows[...] = jnp.zeros_like(rows)
     taps = taps_ref.shape[1]
+    copies[3].wait()
+    copies[4].wait()
     for stream in range(streams):
         rows[stream * 8 : stream * 8 + taps] = taps_ref[stream].astype(jnp.float32)
     rows[streams * 8 : streams * 8 + 1] = gain_ref[...]
@@ -49,7 +71,14 @@
     weights_ref[...] = turned[pl.ds(first, channels)]
 
 
-def mix_kernel(packed_ref, weights_ref, forward_ref, inverse_ref, out_ref, query, keys, lags, key_spec, lag_spec, resp, total):
+def mix_kernel(
+    packed_ref, weights_ref, forward_hbm, inverse_hbm, out_ref,
+    query, keys, lags, key_spec, lag_spec, resp, total, forward_ref, inverse_ref, sems,
+):
+    forward_copy = pltpu.make_async_copy(forward_hbm, forward_ref, sems.at[0])
+    inverse_copy = pltpu.make_async_copy(inverse_hbm, inverse_ref, sems.at[1])
+    forward_copy.start()
+    inverse_copy.start()
     pairs = packed_ref.shape[0]
     blocks = 2 * pairs
     channels = packed_ref.shape[2]
@@ -93,6 +122,7 @@
             values, forward_ref[1], preferred_element_type=jnp.float32
         )
 
+    forward_copy.wait()
     key_spec[...] = transform(keys[...])
     lag_spec[...] = transform(lags[...])
     parity = jnp.where(lane % 2 == 0, 1.0, -1.0).astype(jnp.float32)
@@ -127,6 +157,7 @@
         for j in range(group):
             total[span(base + j), :LANES] = sums[j][0]
             total[span(base + j), LANES:] = sums[j][1]
+    inverse_copy.wait()
     convolved = jnp.dot(
         total[...], inverse_ref[...], preferred_element_type=jnp.float32, precision=lax.Precision.HIGHEST
     )
@@ -169,25 +200,41 @@
     taps = jnp.transpose(short_weight, (1, 0, 2))
     scalars = pl.BlockSpec(memory_space=pltpu.SMEM)
     vmem = pl.BlockSpec(memory_space=pltpu.VMEM)
+    hbm = pl.BlockSpec(memory_space=pltpu.HBM)
     packed, weights = pl.pallas_call(
         pack_kernel,
         out_shape=(
-            jax.ShapeDtypeStruct((pairs, 8, channels, length), jnp.bfloat16),
-            jax.ShapeDtypeStruct((channels, LANES), jnp.float32),
+            pltpu.VMEM((pairs, 8, channels, length), jnp.bfloat16),
+            pltpu.VMEM((channels, LANES), jnp.float32),
         ),
-        in_specs=[scalars] + [vmem] * 4,
+        in_specs=[scalars] + [hbm] * 4,
         out_specs=(vmem, vmem),
-        scratch_shapes=[pltpu.VMEM((LANES, LANES), jnp.float32)] * 2,
+        scratch_shapes=[
+            pltpu.VMEM((2, 3, length, width), jnp.bfloat16),
+            pltpu.VMEM((2, length, width), jnp.bfloat16),
+            pltpu.VMEM(taps.shape, jnp.bfloat16),
+            pltpu.VMEM((1, width), jnp.float32),
+            pltpu.VMEM((LANES, LANES), jnp.float32),
+            pltpu.VMEM((LANES, LANES), jnp.float32),
+            pltpu.SemaphoreType.DMA((5,)),
+        ],
+        compiler_params=pltpu.CompilerParams(vmem_limit_bytes=4 * MIB),
         cost_estimate=pl.CostEstimate(flops=1000000, bytes_accessed=600000, transcendentals=0),
         interpret=INTERPRET,
-    )(position, tiles, long_filter.reshape(2, length, width), taps, skip_gain.reshape(1, width))
+    )(
+        position,
+        in_hbm(tiles),
+        in_hbm(long_filter.reshape(2, length, width)),
+        in_hbm(taps),
+        in_hbm(skip_gain.reshape(1, width)),
+    )
     packed = lax.all_to_all(packed, "ctx", 0, 0, tiled=True)
     forward, inverse = tables()
     rows = 2 * pairs * channels
     activated = pl.pallas_call(
         mix_kernel,
-        out_shape=jax.ShapeDtypeStruct((pairs, 2, channels, length), jnp.bfloat16),
-        in_specs=[vmem] * 4,
+        out_shape=pltpu.VMEM((pairs, 2, channels, length), jnp.bfloat16),
+        in_specs=[vmem] * 2 + [hbm] * 2,
         out_specs=vmem,
         scratch_shapes=[
             pltpu.VMEM((rows, LANES), jnp.float32),
@@ -197,17 +244,27 @@
             pltpu.VMEM((rows, PERIOD), jnp.float32),
             pltpu.VMEM((3, rows, LANES), jnp.float32),
             pltpu.VMEM((rows, PERIOD), jnp.float32),
+            pltpu.VMEM(forward.shape, jnp.bfloat16),
+            pltpu.VMEM(inverse.shape, jnp.float32),
+            pltpu.SemaphoreType.DMA((2,)),
         ],
+        compiler_params=pltpu.CompilerParams(vmem_limit_bytes=6 * MIB),
         cost_estimate=pl.CostEstimate(flops=100000000, bytes_accessed=600000, transcendentals=0),
         interpret=INTERPRET,
-    )(packed, weights, jnp.asarray(forward), jnp.asarray(inverse))
+    )(
+        packed,
+        weights,
+        in_hbm(jnp.asarray(forward)),
+        in_hbm(jnp.asarray(inverse)),
+    )
     own = lax.all_to_all(activated, "ctx", 0, 0, tiled=True)
     other = lax.ppermute(own, "core", [(0, 1), (1, 0)])
     partial = pl.pallas_call(
         project_kernel,
-        out_shape=jax.ShapeDtypeStruct((chips, 2 * length, width), jnp.bfloat16),
+        out_shape=pltpu.VMEM((chips, 2 * length, width), jnp.bfloat16),
         in_specs=[scalars] + [vmem] * 4,
         out_specs=vmem,
+        compiler_params=pltpu.CompilerParams(vmem_limit_bytes=8 * MIB),
         cost_estimate=pl.CostEstimate(flops=268435456, bytes_accessed=3300000, transcendentals=0),
         interpret=INTERPRET,
     )(core, own, other, out_weight, other_weight)

time: 90.1 us -> 85.2 us (0.946)
  Pallas kernels: 8.38 us -> 5.31 us
  local copies, waits for them, and re-layouts: 1.33 us -> 0.01 us
    pallas_call x3, Pallas kernels: 8.38 us -> 5.31 us  [the longest x1 2.52 us: local(): pl.pallas_call(mix_kernel, out_shape=pltpu.VMEM((pairs, 2, channels, leng...]
    unnamed x8 -> x2, local copies, waits for them, and re-layouts: 1.33 us -> 0.01 us
  transfers between devices with their start and end apart: 3 -> 3, of which waited for: 2 -> 2; matrix products, arithmetic and copies ran while one was open for 0% -> 0% of each run, Pallas kernels for 4% -> 3%
where the time goes in v2:
time: 85.2 us; the launch traced here: 84.8 us
  blocking collectives  44.2 us (52%)
  starting transfers between devices  22.7 us (27%)
  waiting for transfers between devices  11.8 us (14%)
  Pallas kernels  5.31 us (6%)
    all_to_all x1, blocking collectives, local(): shares = lax.all_to_all(partial, 'chip', 0, 0, tiled=True)  22.6 us
    all_to_all x1, blocking collectives, local(): own = lax.all_to_all(activated, 'ctx', 0, 0, tiled=True)  21.7 us
    all_to_all x1, starting transfers between devices, local(): packed = lax.all_to_all(packed, 'ctx', 0, 0, tiled=True)  15.7 us
    all_to_all x1, waiting for transfers between devices, local(): packed = lax.all_to_all(packed, 'ctx', 0, 0, tiled=True)  10.9 us
    ppermute x1, starting transfers between devices, local(): other = lax.ppermute(own, 'core', [(0, 1), (1, 0)])  4.09 us
    ppermute x1, starting transfers between devices, local(): other_weight = lax.ppermute(out_weight, 'core', [(0, 1), (1, 0)])  2.87 us
    pallas_call x1, Pallas kernels, local(): pl.pallas_call(mix_kernel, out_shape=pltpu.VMEM((pairs, 2, channels, leng...  2.52 us
    pallas_call x1, Pallas kernels, local(): pl.pallas_call(pack_kernel, out_shape=(pltpu.VMEM((pairs, 8, channels, le...  2.04 us
  transfers between devices with their start and end apart: 3, of which 2 were waited for; matrix products, arithmetic and copies ran while one was open for 0% of the time, Pallas kernels for 3%

profile of v2, /device:TPU:1, one launch (start us, length us, event | category | flops | bytes accessed | tf_op | source)
XLA Modules:
  0.0 84.8 jit_solution(9289677072785366265)
XLA Ops:
  0.0 0.0 copy-start
  0.0 2.0 %shard_map.73 = (bf16[16,8,8,128]{3,2,1,0:T(8,128)(2,1)}, f32[8,128]{1,0:T(8,128)S(1)}) custom-call(s32[1]{0:T(128)} %bitcast.1.index_ref, bf16[2,3,128,128]{3,2,1,0:T(8,128)(2,1)} %bitcast.11, bf16[2,128,128]{2,1,0:T(8,128)(2,1)} %bitcast.12, bf16[3,7,128]{2,1,0:T(8,128)(2,1)} %bitcast.13, f32[1,128]{1,0:T(1,128)} %bitcast.14), custom_call_target="tpu_custom_call" | custom-call | flops 1000000 | bytes 600000 | tf_op jit(solution)/shard_map/pallas_call | solution.py:204
  2.0 15.7 %all-to-all-start = ((bf16[16,8,8,128]{3,2,1,0:T(8,128)(2,1)}), bf16[16,8,8,128]{3,2,1,0:T(8,128)(2,1)S(1)}, u32[]{:S(2)}, u32[]{:S(2)}) async-start(bf16[16,8,8,128]{3,2,1,0:T(8,128)(2,1)} %get-tuple-element.7), calls=%async_computation | async-start | bytes 524288 | tf_op jit(solution)/shard_map/all_to_all | solution.py:231
  17.8 2.9 %collective-permute-start.1 = (bf16[128,4096]{1,0:T(8,128)(2,1)}, bf16[128,4096]{1,0:T(8,128)(2,1)S(1)}, u32[]{:S(2)}, u32[]{:S(2)}) collective-permute-start(bf16[128,4096]{1,0:T(8,128)(2,1)} %own_weight_ref.1), channel_id=1, source_target_pairs={{0,1},{1,0},{2,3},{3,2},{4,5},{5,4},{6,7},{7,6},{8,9},{9,8},{10,11... | collective-permute-start | bytes 3145736 | tf_op jit(solution)/shard_map/ppermute | solution.py:198
  20.7 10.9 %all-to-all-done.packed_ref = bf16[16,8,8,128]{3,2,1,0:T(8,128)(2,1)S(1)} async-done(((bf16[16,8,8,128]{3,2,1,0:T(8,128)(2,1)}), bf16[16,8,8,128]{3,2,1,0:T(8,128)(2,1)S(1)}, u32[]{:S(2)}, u32[]{:S(2)}) %all-to-all-start) | async-done | bytes 262176 | tf_op jit(solution)/shard_map/all_to_all | solution.py:231
  31.6 2.5 %shard_map.74 = bf16[16,2,8,128]{3,2,1,0:T(8,128)(2,1)S(1)} custom-call(bf16[16,8,8,128]{3,2,1,0:T(8,128)(2,1)S(1)} %all-to-all-done.packed_ref, f32[8,128]{1,0:T(8,128)S(1)} %get-tuple-element.8.weights_ref, bf16[2,128,256]{2,1,0:T(8,128)(2,1)} %constant.17.clone.forward_hbm, f32[256,128]{1,0:T(8,128)} %constant.18.clone.inverse_hbm), custom_call_target="tpu_custom_call" | custom-call | flops 100000000 | bytes 600000 | tf_op jit(solution)/shard_map/pallas_call | solution.py:234
  34.1 21.7 %all_to_all.15.own_ref = bf16[16,2,8,128]{3,2,1,0:T(8,128)(2,1)S(1)} all-to-all(bf16[16,2,8,128]{3,2,1,0:T(8,128)(2,1)S(1)} %shard_map.74), channel_id=1, replica_groups=mesh['ctx'=16,'chip'=16,'core'=2] {'ctx'}, dimensions={0} | all-to-all | bytes 131072 | tf_op jit(solution)/shard_map/all_to_all | solution.py:260
  55.8 4.1 %collective-permute-start = (bf16[16,2,8,128]{3,2,1,0:T(8,128)(2,1)S(1)}, bf16[16,2,8,128]{3,2,1,0:T(8,128)(2,1)S(1)}, u32[]{:S(2)}, u32[]{:S(2)}) collective-permute-start(bf16[16,2,8,128]{3,2,1,0:T(8,128)(2,1)S(1)} %all_to_all.15.own_ref), channel_id=1, source_target_pairs={{0,1},{1,0},{2,3},{3,2},{4,5},{5,4},{6,7},{7,6},{8,9},{9,8},{10,11... | collective-permute-start | bytes 196616 | tf_op jit(solution)/shard_map/ppermute | solution.py:261
  59.9 0.0 collective-permute-done.1.other_weight_ref
  59.9 0.9 %collective-permute-done.other_ref = bf16[16,2,8,128]{3,2,1,0:T(8,128)(2,1)S(1)} collective-permute-done((bf16[16,2,8,128]{3,2,1,0:T(8,128)(2,1)S(1)}, bf16[16,2,8,128]{3,2,1,0:T(8,128)(2,1)S(1)}, u32[]{:S(2)}, u32[]{:S(2)}) %collective-permute-start) | collective-permute-done | bytes 65568 | tf_op jit(solution)/shard_map/ppermute | solution.py:261
  60.7 0.0 copy-done
  60.8 0.8 shard_map.75
  61.5 22.6 %all_to_all.16 = bf16[16,256,128]{2,1,0:T(8,128)(2,1)S(1)} all-to-all(bf16[16,256,128]{2,1,0:T(8,128)(2,1)S(1)} %shard_map.75), channel_id=1, replica_groups=mesh['ctx'=16,'chip'=16,'core'=2] {'chip'}, dimensions={0} | all-to-all | bytes 2097152 | tf_op jit(solution)/shard_map/all_to_all | solution.py:271
  84.1 0.8 reduce_sum.12
Async XLA Ops:
  0.0 60.8 %copy-start = (bf16[128,4096]{1,0:T(8,128)(2,1)S(1)}, bf16[128,4096]{1,0:T(8,128)(2,1)}, u32[]{:S(2)}) copy-start(bf16[128,4096]{1,0:T(8,128)(2,1)} %own_weight_ref.1) | copy-start | bytes 3145732
  2.0 29.5 %all-to-all-start = ((bf16[16,8,8,128]{3,2,1,0:T(8,128)(2,1)}), bf16[16,8,8,128]{3,2,1,0:T(8,128)(2,1)S(1)}, u32[]{:S(2)}, u32[]{:S(2)}) async-start(bf16[16,8,8,128]{3,2,1,0:T(8,128)(2,1)} %get-tuple-element.7), calls=%async_computation | async-start | bytes 524288 | tf_op jit(solution)/shard_map/all_to_all | solution.py:231
  17.8 42.1 %collective-permute-start.1 = (bf16[128,4096]{1,0:T(8,128)(2,1)}, bf16[128,4096]{1,0:T(8,128)(2,1)S(1)}, u32[]{:S(2)}, u32[]{:S(2)}) collective-permute-start(bf16[128,4096]{1,0:T(8,128)(2,1)} %own_weight_ref.1), channel_id=1, source_target_pairs={{0,1},{1,0},{2,3},{3,2},{4,5},{5,4},{6,7},{7,6},{8,9},{9,8},{10,11... | collective-permute-start | bytes 3145736 | tf_op jit(solution)/shard_map/ppermute | solution.py:198
  55.8 5.0 %collective-permute-start = (bf16[16,2,8,128]{3,2,1,0:T(8,128)(2,1)S(1)}, bf16[16,2,8,128]{3,2,1,0:T(8,128)(2,1)S(1)}, u32[]{:S(2)}, u32[]{:S(2)}) collective-permute-start(bf16[16,2,8,128]{3,2,1,0:T(8,128)(2,1)S(1)} %all_to_all.15.own_ref), channel_id=1, source_target_pairs={{0,1},{1,0},{2,3},{3,2},{4,5},{5,4},{6,7},{7,6},{8,9},{9,8},{10,11... | collective-permute-start | bytes 196616 | tf_op jit(solution)/shard_map/ppermute | solution.py:261

commit v3 on v2

--- a/solution.py
+++ b/solution.py
@@ -86,7 +86,8 @@
     lane = lax.broadcasted_iota(jnp.int32, (channels, LANES), 1)
 
     def place(block):
-        return (block, 0) if block < pairs else (blocks - 1 - block, 1)
+        owner, half = (block, 0) if block < pairs else (blocks - 1 - block, 1)
+        return (owner + pairs // 2) % pairs, half
 
     def span(block):
         return slice(block * channels, (block + 1) * channels)
@@ -169,15 +170,15 @@
         out_ref[target, half] = (query[span(block)] * inner).astype(jnp.bfloat16)
 
 
-def project_kernel(index_ref, own_ref, other_ref, own_weight_ref, other_weight_ref, out_ref):
+def project_kernel(index_ref, both_ref, own_weight_ref, other_weight_ref, out_ref):
     chips, rows, width = out_ref.shape
     depth = own_weight_ref.shape[0]
     core = index_ref[0]
     lhs = []
     for half in range(2):
         parts = [
-            ref[:, half].reshape(depth, LANES).astype(jnp.float32).T.astype(jnp.bfloat16)
-            for ref in (own_ref, other_ref)
+            both_ref[which, :, half].reshape(depth, LANES).astype(jnp.float32).T.astype(jnp.bfloat16)
+            for which in (core, 1 - core)
         ]
         lhs.append(jnp.concatenate(parts, axis=1))
     lhs = jnp.concatenate(lhs, axis=0)
@@ -193,7 +194,8 @@
     length = features.shape[2]
     width = features.shape[4]
     channels = width // pairs
-    position = lax.axis_index("ctx").astype(jnp.int32).reshape(1)
+    order = [[(place + pairs // 2) % pairs for place in range(pairs)]]
+    position = ((lax.axis_index("ctx") + pairs // 2) % pairs).astype(jnp.int32).reshape(1)
     core = lax.axis_index("core").astype(jnp.int32).reshape(1)
     other_weight = lax.ppermute(out_weight, "core", [(0, 1), (1, 0)])
     tiles = jnp.transpose(features, (0, 1, 3, 2, 4)).reshape(2, 3, length, width)
@@ -228,7 +230,7 @@
         in_hbm(taps),
         in_hbm(skip_gain.reshape(1, width)),
     )
-    packed = lax.all_to_all(packed, "ctx", 0, 0, tiled=True)
+    packed = lax.all_to_all(packed, "ctx", 0, 0, tiled=True, axis_index_groups=order)
     forward, inverse = tables()
     rows = 2 * pairs * channels
     activated = pl.pallas_call(
@@ -257,17 +259,17 @@
         in_hbm(jnp.asarray(forward)),
         in_hbm(jnp.asarray(inverse)),
     )
-    own = lax.all_to_all(activated, "ctx", 0, 0, tiled=True)
-    other = lax.ppermute(own, "core", [(0, 1), (1, 0)])
+    own = lax.all_to_all(activated, "ctx", 0, 0, tiled=True, axis_index_groups=order)
+    both = lax.all_gather(own, "core", axis=0)
     partial = pl.pallas_call(
         project_kernel,
         out_shape=pltpu.VMEM((chips, 2 * length, width), jnp.bfloat16),
-        in_specs=[scalars] + [vmem] * 4,
+        in_specs=[scalars] + [vmem] * 3,
         out_specs=vmem,
         compiler_params=pltpu.CompilerParams(vmem_limit_bytes=8 * MIB),
         cost_estimate=pl.CostEstimate(flops=268435456, bytes_accessed=3300000, transcendentals=0),
         interpret=INTERPRET,
-    )(core, own, other, out_weight, other_weight)
+    )(core, both, out_weight, other_weight)
     shares = lax.all_to_all(partial, "chip", 0, 0, tiled=True)
     mixed = jnp.sum(shares.astype(jnp.float32), axis=0).astype(jnp.bfloat16)
     return mixed.reshape(2, 1, length, width)

time: 85.2 us -> 79.5 us (0.933)
  blocking collectives: 44.2 us -> 25.9 us
  starting transfers between devices: 22.7 us -> 33.9 us
    all_to_all x1 -> x0, blocking collectives: 21.7 us -> none  [local(): own = lax.all_to_all(activated, 'ctx', 0, 0, tiled=True)]
    all_to_all x1 -> x2, starting transfers between devices: 15.7 us -> 30.7 us  [the longest x1 19.1 us: local(): lax.all_to_all(packed, 'ctx', 0, 0, tiled=True, axis_index_groups=order)]
    ppermute x1 -> x0, starting transfers between devices: 4.09 us -> none  [local(): other = lax.ppermute(own, 'core', [(0, 1), (1, 0)])]
    all_gather x0 -> x1, blocking collectives: none -> 3.38 us  [local(): both = lax.all_gather(own, 'core', axis=0)]
    all_to_all x1 -> x2, waiting for transfers between devices: 10.9 us -> 12.5 us  [the longest x1 9.34 us: local(): lax.all_to_all(packed, 'ctx', 0, 0, tiled=True, axis_index_groups=order)]
    ppermute x1 -> x0, waiting for transfers between devices: 0.87 us -> none  [local(): other = lax.ppermute(own, 'core', [(0, 1), (1, 0)])]
  transfers between devices with their start and end apart: 3 -> 3, of which waited for: 2 -> 2; matrix products, arithmetic and copies ran while one was open for 0% -> 0% of each run, Pallas kernels for 3% -> 4%
where the time goes in v3:
time: 79.5 us; the launch traced here: 79.1 us
  starting transfers between devices  33.9 us (43%)
  blocking collectives  25.9 us (33%)
  waiting for transfers between devices  12.5 us (16%)
  Pallas kernels  5.92 us (7%)
    all_to_all x1, blocking collectives, local(): shares = lax.all_to_all(partial, 'chip', 0, 0, tiled=True)  22.6 us
    all_to_all x1, starting transfers between devices, local(): lax.all_to_all(packed, 'ctx', 0, 0, tiled=True, axis_index_groups=order)  19.1 us
    all_to_all x1, starting transfers between devices, local(): lax.all_to_all(activated, 'ctx', 0, 0, tiled=True, axis_index_groups=order)  11.6 us
    all_to_all x1, waiting for transfers between devices, local(): lax.all_to_all(packed, 'ctx', 0, 0, tiled=True, axis_index_groups=order)  9.34 us
    all_gather x1, blocking collectives, local(): both = lax.all_gather(own, 'core', axis=0)  3.38 us
    all_to_all x1, waiting for transfers between devices, local(): lax.all_to_all(activated, 'ctx', 0, 0, tiled=True, axis_index_groups=order)  3.16 us
    ppermute x1, starting transfers between devices, local(): other_weight = lax.ppermute(out_weight, 'core', [(0, 1), (1, 0)])  3.13 us
    pallas_call x1, Pallas kernels, local(): pl.pallas_call(mix_kernel, out_shape=pltpu.VMEM((pairs, 2, channels, leng...  3.12 us
  transfers between devices with their start and end apart: 3, of which 2 were waited for; matrix products, arithmetic and copies ran while one was open for 0% of the time, Pallas kernels for 4%

profile of v3, /device:TPU:1, one launch (start us, length us, event | category | flops | bytes accessed | tf_op | source)
XLA Modules:
  0.0 79.1 jit_solution(16861222647161732214)
XLA Ops:
  0.0 0.0 copy-start
  0.0 2.0 %shard_map.73 = (bf16[16,8,8,128]{3,2,1,0:T(8,128)(2,1)}, f32[8,128]{1,0:T(8,128)S(1)}) custom-call(s32[1]{0:T(128)} %bitcast.1.index_ref, bf16[2,3,128,128]{3,2,1,0:T(8,128)(2,1)} %bitcast.13, bf16[2,128,128]{2,1,0:T(8,128)(2,1)} %bitcast.14, bf16[3,7,128]{2,1,0:T(8,128)(2,1)} %bitcast.15, f32[1,128]{1,0:T(1,128)} %bitcast.16), custom_call_target="tpu_custom_call" | custom-call | flops 1000000 | bytes 600000 | tf_op jit(solution)/shard_map/pallas_call | solution.py:206
  2.0 19.1 %all-to-all-start = ((bf16[16,8,8,128]{3,2,1,0:T(8,128)(2,1)}), bf16[16,8,8,128]{3,2,1,0:T(8,128)(2,1)S(1)}, u32[]{:S(2)}, u32[]{:S(2)}) async-start(bf16[16,8,8,128]{3,2,1,0:T(8,128)(2,1)} %get-tuple-element.7), calls=%async_computation | async-start | bytes 524288 | tf_op jit(solution)/shard_map/all_to_all | solution.py:233
  21.2 3.1 %collective-permute-start = (bf16[128,4096]{1,0:T(8,128)(2,1)}, bf16[128,4096]{1,0:T(8,128)(2,1)S(1)}, u32[]{:S(2)}, u32[]{:S(2)}) collective-permute-start(bf16[128,4096]{1,0:T(8,128)(2,1)} %own_weight_ref.1), channel_id=1, source_target_pairs={{0,1},{1,0},{2,3},{3,2},{4,5},{5,4},{6,7},{7,6},{8,9},{9,8},{10,11... | collective-permute-start | bytes 3145736 | tf_op jit(solution)/shard_map/ppermute | solution.py:200
  24.3 9.3 %all-to-all-done.packed_ref = bf16[16,8,8,128]{3,2,1,0:T(8,128)(2,1)S(1)} async-done(((bf16[16,8,8,128]{3,2,1,0:T(8,128)(2,1)}), bf16[16,8,8,128]{3,2,1,0:T(8,128)(2,1)S(1)}, u32[]{:S(2)}, u32[]{:S(2)}) %all-to-all-start) | async-done | bytes 262176 | tf_op jit(solution)/shard_map/all_to_all | solution.py:233
  33.7 3.1 %shard_map.74 = bf16[16,2,8,128]{3,2,1,0:T(8,128)(2,1)} custom-call(bf16[16,8,8,128]{3,2,1,0:T(8,128)(2,1)S(1)} %all-to-all-done.packed_ref, f32[8,128]{1,0:T(8,128)S(1)} %get-tuple-element.8.weights_ref, bf16[2,128,256]{2,1,0:T(8,128)(2,1)} %constant.32.clone.forward_hbm, f32[256,128]{1,0:T(8,128)} %constant.33.clone.inverse_hbm), custom_call_target="tpu_custom_call" | custom-call | flops 100000000 | bytes 600000 | tf_op jit(solution)/shard_map/pallas_call | solution.py:236
  36.8 11.6 %all-to-all-start.1 = ((bf16[16,2,8,128]{3,2,1,0:T(8,128)(2,1)}), bf16[16,2,8,128]{3,2,1,0:T(8,128)(2,1)S(1)}, u32[]{:S(2)}, u32[]{:S(2)}) async-start(bf16[16,2,8,128]{3,2,1,0:T(8,128)(2,1)} %shard_map.74), calls=%async_computation.1 | async-start | bytes 131072 | tf_op jit(solution)/shard_map/all_to_all | solution.py:262
  48.4 3.2 %all-to-all-done.1 = bf16[16,2,8,128]{3,2,1,0:T(8,128)(2,1)S(1)} async-done(((bf16[16,2,8,128]{3,2,1,0:T(8,128)(2,1)}), bf16[16,2,8,128]{3,2,1,0:T(8,128)(2,1)S(1)}, u32[]{:S(2)}, u32[]{:S(2)}) %all-to-all-start.1) | async-done | bytes 65568 | tf_op jit(solution)/shard_map/all_to_all | solution.py:262
  51.6 3.4 %all-gather = bf16[32,2,8,128]{3,2,1,0:T(8,128)(2,1)S(1)} all-gather(bf16[16,2,8,128]{3,2,1,0:T(8,128)(2,1)S(1)} %all-to-all-done.1), channel_id=2, replica_groups=mesh['ctx'=16,'chip'=16,'core'=2] {'core'}, dimensions={0}, use_global_device_ids=true | all-gather | bytes 196608 | tf_op jit(solution)/shard_map/all_gather | solution.py:263
  55.0 0.0 collective-permute-done.other_weight_ref
  55.0 0.0 copy-done
  55.0 0.8 shard_map.75
  55.7 22.6 %all_to_all.15 = bf16[16,256,128]{2,1,0:T(8,128)(2,1)S(1)} all-to-all(bf16[16,256,128]{2,1,0:T(8,128)(2,1)S(1)} %shard_map.75), channel_id=1, replica_groups=mesh['ctx'=16,'chip'=16,'core'=2] {'chip'}, dimensions={0} | all-to-all | bytes 2097152 | tf_op jit(solution)/shard_map/all_to_all | solution.py:273
  78.3 0.8 reduce_sum.12
Async XLA Ops:
  0.0 55.0 %copy-start = (bf16[128,4096]{1,0:T(8,128)(2,1)S(1)}, bf16[128,4096]{1,0:T(8,128)(2,1)}, u32[]{:S(2)}) copy-start(bf16[128,4096]{1,0:T(8,128)(2,1)} %own_weight_ref.1) | copy-start | bytes 3145732
  2.0 31.6 %all-to-all-start = ((bf16[16,8,8,128]{3,2,1,0:T(8,128)(2,1)}), bf16[16,8,8,128]{3,2,1,0:T(8,128)(2,1)S(1)}, u32[]{:S(2)}, u32[]{:S(2)}) async-start(bf16[16,8,8,128]{3,2,1,0:T(8,128)(2,1)} %get-tuple-element.7), calls=%async_computation | async-start | bytes 524288 | tf_op jit(solution)/shard_map/all_to_all | solution.py:233
  21.2 33.8 %collective-permute-start = (bf16[128,4096]{1,0:T(8,128)(2,1)}, bf16[128,4096]{1,0:T(8,128)(2,1)S(1)}, u32[]{:S(2)}, u32[]{:S(2)}) collective-permute-start(bf16[128,4096]{1,0:T(8,128)(2,1)} %own_weight_ref.1), channel_id=1, source_target_pairs={{0,1},{1,0},{2,3},{3,2},{4,5},{5,4},{6,7},{7,6},{8,9},{9,8},{10,11... | collective-permute-start | bytes 3145736 | tf_op jit(solution)/shard_map/ppermute | solution.py:200
  36.8 14.8 %all-to-all-start.1 = ((bf16[16,2,8,128]{3,2,1,0:T(8,128)(2,1)}), bf16[16,2,8,128]{3,2,1,0:T(8,128)(2,1)S(1)}, u32[]{:S(2)}, u32[]{:S(2)}) async-start(bf16[16,2,8,128]{3,2,1,0:T(8,128)(2,1)} %shard_map.74), calls=%async_computation.1 | async-start | bytes 131072 | tf_op jit(solution)/shard_map/all_to_all | solution.py:262

commit v4 on v3

--- a/solution.py
+++ b/solution.py
@@ -35,33 +35,51 @@
 
 
 def pack_kernel(
-    index_ref, features_hbm, filter_hbm, taps_hbm, gain_hbm, out_ref, weights_ref,
-    features_ref, filter_ref, taps_ref, gain_ref, rows, turned, sems,
+    index_ref, features_hbm, filter_hbm, taps_hbm, gain_hbm, out_ref, weights_ref, query_ref,
+    features_ref, filter_ref, taps_ref, gain_ref, extended, edges, rows, turned, sems,
 ):
     groups = out_ref.shape[0]
     channels = LANES // groups
     streams = features_ref.shape[1]
+    taps = taps_ref.shape[1]
+    rim = taps - 1
     copies = [
+        pltpu.make_async_copy(taps_hbm, taps_ref, sems.at[3]),
         pltpu.make_async_copy(features_hbm.at[0], features_ref.at[0], sems.at[0]),
         pltpu.make_async_copy(features_hbm.at[1], features_ref.at[1], sems.at[1]),
         pltpu.make_async_copy(filter_hbm, filter_ref, sems.at[2]),
-        pltpu.make_async_copy(taps_hbm, taps_ref, sems.at[3]),
         pltpu.make_async_copy(gain_hbm, gain_ref, sems.at[4]),
     ]
     for copy in copies:
         copy.start()
+
+    def put(row, tile):
+        out_ref[:, row] = tile.T.astype(jnp.bfloat16).reshape(groups, channels, LANES)
+
+    extended[:, :8] = jnp.zeros((streams, 8, LANES), jnp.float32)
+    edges[...] = jnp.zeros_like(edges)
+    rows[...] = jnp.zeros_like(rows)
+    copies[0].wait()
     for half in range(2):
-        copies[half].wait()
+        copies[1 + half].wait()
+        featured = []
         for stream in range(streams):
-            tile = features_ref[half, stream].astype(jnp.float32).T.astype(jnp.bfloat16)
-            out_ref[:, half * streams + stream] = tile.reshape(groups, channels, LANES)
-    copies[2].wait()
+            value = features_ref[half, stream].astype(jnp.float32)
+            extended[stream, 8:] = value
+            base = 2 * rim * (half * streams + stream)
+            edges[base : base + rim] = extended[stream, 8 + LANES - rim : 8 + LANES]
+            edges[base + rim : base + 2 * rim] = extended[stream, 8 : 8 + rim]
+            summed = taps_ref[stream, 0:1].astype(jnp.float32) * value
+            for i in range(1, taps):
+                weight = taps_ref[stream, i : i + 1].astype(jnp.float32)
+                summed = summed + weight * extended[stream, 8 - i : 8 - i + LANES]
+            featured.append(summed)
+        query_ref[half] = featured[0]
+        put(half, featured[1] * featured[2])
+    copies[3].wait()
     for half in range(2):
-        tile = filter_ref[half].astype(jnp.float32).T.astype(jnp.bfloat16)
-        out_ref[:, 2 * streams + half] = tile.reshape(groups, channels, LANES)
-    rows[...] = jnp.zeros_like(rows)
-    taps = taps_ref.shape[1]
-    copies[3].wait()
+        put(2 + half, filter_ref[half].astype(jnp.float32))
+    put(4, edges[...])
     copies[4].wait()
     for stream in range(streams):
         rows[stream * 8 : stream * 8 + taps] = taps_ref[stream].astype(jnp.float32)
@@ -82,7 +100,9 @@
     pairs = packed_ref.shape[0]
     blocks = 2 * pairs
     channels = packed_ref.shape[2]
-    taps = 7
+    streams, taps = 3, 7
+    rim = taps - 1
+    step = 2 * rim
     lane = lax.broadcasted_iota(jnp.int32, (channels, LANES), 1)
 
     def place(block):
@@ -97,26 +117,33 @@
 
     for block in range(blocks):
         source, half = place(block)
-        lags[span(block)] = packed_ref[source, 6 + half]
-    for stream in (1, 2, 0):
-        weight = [column(stream * 8 + i) for i in range(taps)]
-        turned_before = [jnp.zeros((channels, LANES), jnp.float32)] * taps
-        for block in range(blocks):
-            source, half = place(block)
-            value = packed_ref[source, half * 3 + stream].astype(jnp.float32)
-            summed = weight[0] * value
-            turned = [value]
-            for i in range(1, taps):
-                rolled = pltpu.roll(value, i, 1)
-                turned.append(rolled)
-                summed = summed + weight[i] * jnp.where(lane >= i, rolled, turned_before[i])
-            turned_before = turned
-            if stream == 1:
-                total[span(block), :LANES] = summed
-            elif stream == 2:
-                keys[span(block)] = (total[span(block), :LANES] * summed).astype(jnp.bfloat16)
-            else:
-                query[span(block)] = summed
+        lags[span(block)] = packed_ref[source, 2 + half]
+    stream_of = lane // step % streams
+    weight = [
+        jnp.where(stream_of == 0, column(i), jnp.where(stream_of == 1, column(8 + i), column(16 + i)))
+        for i in range(taps)
+    ]
+    tail = lane % step < rim
+    lower = lane < streams * step
+    edge = [packed_ref[place(owner)[0], 4].astype(jnp.float32) for owner in range(pairs)]
+    head = lane < rim
+    for owner in range(pairs):
+        before = edge[owner - 1] if owner else jnp.zeros_like(edge[0])
+        if owner + 1 < pairs:
+            after = edge[owner + 1]
+        else:
+            after = pltpu.roll(edge[owner], streams * step, 1)
+        value = jnp.where(tail, jnp.where(lower, before, after), edge[owner])
+        summed = weight[0] * value
+        for i in range(1, taps):
+            summed = summed + weight[i] * pltpu.roll(value, i, 1)
+        product = summed * pltpu.roll(summed, LANES - step, 1)
+        for half, block in ((0, owner), (1, blocks - 1 - owner)):
+            first = half * streams * step + rim
+            gated = pltpu.roll(product, LANES - first - step, 1)
+            whole = packed_ref[place(owner)[0], half].astype(jnp.float32)
+            keys[span(block)] = jnp.where(head, gated, whole).astype(jnp.bfloat16)
+            query[span(block)] = pltpu.roll(summed, LANES - first, 1)
 
     def transform(values):
         return jnp.dot(values, forward_ref[0], preferred_element_type=jnp.float32) + jnp.dot(
@@ -167,21 +194,23 @@
     for block in range(blocks):
         target, half = place(block)
         inner = total[span(block), :LANES] + gain * keys[span(block)].astype(jnp.float32)
-        out_ref[target, half] = (query[span(block)] * inner).astype(jnp.bfloat16)
+        out_ref[target, half] = jnp.where(head, query[span(block)] * inner, inner).astype(jnp.bfloat16)
+
+
+def activate_kernel(mixed_ref, query_ref, out_ref):
+    groups, halves, channels, length = mixed_ref.shape
+    rim = 6
+    token = lax.broadcasted_iota(jnp.int32, (length, LANES), 0)
+    for half in range(halves):
+        inner = mixed_ref[:, half].reshape(groups * channels, length).astype(jnp.float32).T
+        product = jnp.where(token < rim, inner, query_ref[half] * inner)
+        out_ref[half * length : (half + 1) * length] = product.astype(jnp.bfloat16)
 
 
 def project_kernel(index_ref, both_ref, own_weight_ref, other_weight_ref, out_ref):
-    chips, rows, width = out_ref.shape
-    depth = own_weight_ref.shape[0]
-    core = index_ref[0]
-    lhs = []
-    for half in range(2):
-        parts = [
-            both_ref[which, :, half].reshape(depth, LANES).astype(jnp.float32).T.astype(jnp.bfloat16)
-            for which in (core, 1 - core)
-        ]
-        lhs.append(jnp.concatenate(parts, axis=1))
-    lhs = jnp.concatenate(lhs, axis=0)
+    chips, _, width = out_ref.shape
+    core = index_ref[1]
+    lhs = jnp.concatenate([both_ref[core], both_ref[1 - core]], axis=1)
     for chip in range(chips):
         columns = pl.ds(pl.multiple_of((2 * chip + core) * width, width), width)
         weight = jnp.concatenate([own_weight_ref[:, columns], other_weight_ref[:, columns]], axis=0)
@@ -195,27 +224,29 @@
     width = features.shape[4]
     channels = width // pairs
     order = [[(place + pairs // 2) % pairs for place in range(pairs)]]
-    position = ((lax.axis_index("ctx") + pairs // 2) % pairs).astype(jnp.int32).reshape(1)
-    core = lax.axis_index("core").astype(jnp.int32).reshape(1)
-    other_weight = lax.ppermute(out_weight, "core", [(0, 1), (1, 0)])
+    position = (lax.axis_index("ctx") + pairs // 2) % pairs
+    index = jnp.stack([position, lax.axis_index("core")]).astype(jnp.int32)
     tiles = jnp.transpose(features, (0, 1, 3, 2, 4)).reshape(2, 3, length, width)
     taps = jnp.transpose(short_weight, (1, 0, 2))
     scalars = pl.BlockSpec(memory_space=pltpu.SMEM)
     vmem = pl.BlockSpec(memory_space=pltpu.VMEM)
     hbm = pl.BlockSpec(memory_space=pltpu.HBM)
-    packed, weights = pl.pallas_call(
+    packed, weights, query = pl.pallas_call(
         pack_kernel,
         out_shape=(
-            pltpu.VMEM((pairs, 8, channels, length), jnp.bfloat16),
+            pltpu.VMEM((pairs, 5, channels, length), jnp.bfloat16),
             pltpu.VMEM((channels, LANES), jnp.float32),
+            pltpu.VMEM((2, length, width), jnp.float32),
         ),
         in_specs=[scalars] + [hbm] * 4,
-        out_specs=(vmem, vmem),
+        out_specs=(vmem, vmem, vmem),
         scratch_shapes=[
             pltpu.VMEM((2, 3, length, width), jnp.bfloat16),
             pltpu.VMEM((2, length, width), jnp.bfloat16),
             pltpu.VMEM(taps.shape, jnp.bfloat16),
             pltpu.VMEM((1, width), jnp.float32),
+            pltpu.VMEM((3, 8 + length, width), jnp.float32),
+            pltpu.VMEM((LANES, LANES), jnp.float32),
             pltpu.VMEM((LANES, LANES), jnp.float32),
             pltpu.VMEM((LANES, LANES), jnp.float32),
             pltpu.SemaphoreType.DMA((5,)),
@@ -224,16 +255,17 @@
         cost_estimate=pl.CostEstimate(flops=1000000, bytes_accessed=600000, transcendentals=0),
         interpret=INTERPRET,
     )(
-        position,
+        index,
         in_hbm(tiles),
         in_hbm(long_filter.reshape(2, length, width)),
         in_hbm(taps),
         in_hbm(skip_gain.reshape(1, width)),
     )
     packed = lax.all_to_all(packed, "ctx", 0, 0, tiled=True, axis_index_groups=order)
+    other_weight = lax.ppermute(out_weight, "core", [(0, 1), (1, 0)])
     forward, inverse = tables()
     rows = 2 * pairs * channels
-    activated = pl.pallas_call(
+    mixed = pl.pallas_call(
         mix_kernel,
         out_shape=pltpu.VMEM((pairs, 2, channels, length), jnp.bfloat16),
         in_specs=[vmem] * 2 + [hbm] * 2,
@@ -259,8 +291,17 @@
         in_hbm(jnp.asarray(forward)),
         in_hbm(jnp.asarray(inverse)),
     )
-    own = lax.all_to_all(activated, "ctx", 0, 0, tiled=True, axis_index_groups=order)
-    both = lax.all_gather(own, "core", axis=0)
+    mixed = lax.all_to_all(mixed, "ctx", 0, 0, tiled=True, axis_index_groups=order)
+    activated = pl.pallas_call(
+        activate_kernel,
+        out_shape=pltpu.VMEM((2 * length, width), jnp.bfloat16),
+        in_specs=[vmem] * 2,
+        out_specs=vmem,
+        compiler_params=pltpu.CompilerParams(vmem_limit_bytes=4 * MIB),
+        cost_estimate=pl.CostEstimate(flops=1000000, bytes_accessed=300000, transcendentals=0),
+        interpret=INTERPRET,
+    )(mixed, query)
+    both = lax.all_gather(activated, "core", axis=0)
     partial = pl.pallas_call(
         project_kernel,
         out_shape=pltpu.VMEM((chips, 2 * length, width), jnp.bfloat16),
@@ -269,10 +310,10 @@
         compiler_params=pltpu.CompilerParams(vmem_limit_bytes=8 * MIB),
         cost_estimate=pl.CostEstimate(flops=268435456, bytes_accessed=3300000, transcendentals=0),
         interpret=INTERPRET,
-    )(core, both, out_weight, other_weight)
+    )(index, both, out_weight, other_weight)
     shares = lax.all_to_all(partial, "chip", 0, 0, tiled=True)
-    mixed = jnp.sum(shares.astype(jnp.float32), axis=0).astype(jnp.bfloat16)
-    return mixed.reshape(2, 1, length, width)
+    result = jnp.sum(shares.astype(jnp.float32), axis=0).astype(jnp.bfloat16)
+    return result.reshape(2, 1, length, width)
 
 
 def solution(mesh):

time: 79.5 us -> 77.5 us (0.975)
  blocking collectives: 25.9 us -> 61.6 us
  starting transfers between devices: 33.9 us -> 8.87 us
  waiting for transfers between devices: 12.5 us -> 0.01 us
    all_to_all x0 -> x2, blocking collectives: none -> 36.5 us  [the longest x1 21.3 us: local(): lax.all_to_all(packed, 'ctx', 0, 0, tiled=True, axis_index_groups=order)]
    all_to_all x2 -> x0, starting transfers between devices: 30.7 us -> none  [the longest x1 19.1 us: local(): lax.all_to_all(packed, 'ctx', 0, 0, tiled=True, axis_index_groups=order)]
    all_to_all x2 -> x0, waiting for transfers between devices: 12.5 us -> none  [the longest x1 9.34 us: local(): lax.all_to_all(packed, 'ctx', 0, 0, tiled=True, axis_index_groups=order)]
    ppermute x1, starting transfers between devices: 3.13 us -> 8.87 us  [local(): other_weight = lax.ppermute(out_weight, 'core', [(0, 1), (1, 0)])]
    pallas_call x1, Pallas kernels: 3.12 us -> 2.27 us  [local(): pl.pallas_call(mix_kernel, out_shape=pltpu.VMEM((pairs, 2, channels, leng...]
    all_gather x1, blocking collectives: 3.38 us -> 2.57 us  [local(): both = lax.all_gather(activated, 'core', axis=0)]
    pallas_call x1 -> x2, Pallas kernels: 2.04 us -> 2.16 us  [the longest x1 2.06 us: local(): pl.pallas_call(pack_kernel, out_shape=(pltpu.VMEM((pairs, 5, channels, le...]
  transfers between devices with their start and end apart: 3 -> 1, of which waited for: 2 -> 0; matrix products, arithmetic and copies ran while one was open for 0% -> 0% of each run, Pallas kernels for 4% -> 6%
where the time goes in v4:
time: 77.5 us; the launch traced here: 77.1 us
  blocking collectives  61.6 us (79%)
  starting transfers between devices  8.87 us (11%)
  Pallas kernels  5.73 us (7%)
  other arithmetic  0.85 us (1%)
    all_to_all x1, blocking collectives, local(): shares = lax.all_to_all(partial, 'chip', 0, 0, tiled=True)  22.6 us
    all_to_all x1, blocking collectives, local(): lax.all_to_all(packed, 'ctx', 0, 0, tiled=True, axis_index_groups=order)  21.3 us
    all_to_all x1, blocking collectives, local(): lax.all_to_all(mixed, 'ctx', 0, 0, tiled=True, axis_index_groups=order)  15.2 us
    ppermute x1, starting transfers between devices, local(): other_weight = lax.ppermute(out_weight, 'core', [(0, 1), (1, 0)])  8.87 us
    all_gather x1, blocking collectives, local(): both = lax.all_gather(activated, 'core', axis=0)  2.57 us
    pallas_call x1, Pallas kernels, local(): pl.pallas_call(mix_kernel, out_shape=pltpu.VMEM((pairs, 2, channels, leng...  2.27 us
    pallas_call x1, Pallas kernels, local(): pl.pallas_call(pack_kernel, out_shape=(pltpu.VMEM((pairs, 5, channels, le...  2.06 us
  transfers between devices with their start and end apart: 1, of which 0 were waited for; matrix products, arithmetic and copies ran while one was open for 0% of the time, Pallas kernels for 6%

profile of v4, /device:TPU:1, one launch (start us, length us, event | category | flops | bytes accessed | tf_op | source)
XLA Modules:
  0.0 77.1 jit_solution(10110564702558642228)
XLA Ops:
  0.0 0.0 copy-start
  0.0 8.9 %collective-permute-start = (bf16[128,4096]{1,0:T(8,128)(2,1)}, bf16[128,4096]{1,0:T(8,128)(2,1)S(1)}, u32[]{:S(2)}, u32[]{:S(2)}) collective-permute-start(bf16[128,4096]{1,0:T(8,128)(2,1)} %own_weight_ref.1), channel_id=1, source_target_pairs={{0,1},{1,0},{2,3},{3,2},{4,5},{5,4},{6,7},{7,6},{8,9},{9,8},{10,11... | collective-permute-start | bytes 3145736 | tf_op jit(solution)/shard_map/ppermute | solution.py:265
  8.9 0.1 pad_add_fusion.index_ref
  9.0 2.1 %shard_map.73 = (bf16[16,5,8,128]{3,2,1,0:T(8,128)(2,1)S(1)}, f32[8,128]{1,0:T(8,128)S(1)}, f32[2,128,128]{2,1,0:T(8,128)S(1)}) custom-call(s32[2]{0:T(128)S(1)} %pad_add_fusion.index_ref, bf16[2,3,128,128]{3,2,1,0:T(8,128)(2,1)} %bitcast.13, bf16[2,128,128]{2,1,0:T(8,128)(2,1)} %bitcast.14, bf16[3,7,128]{2,1,0:T(8,128)(2,1)} %bitcast.15, f32[1,128]{1,0:T(1,128)} %bitcast.16), custom_call_target="tpu_custom_call" | custom-call | flops 1000000 | bytes 600000 | tf_op jit(solution)/shard_map/pallas_call | solution.py:234
  11.0 21.3 %all_to_all.15.packed_ref = bf16[16,5,8,128]{3,2,1,0:T(8,128)(2,1)S(1)} all-to-all(bf16[16,5,8,128]{3,2,1,0:T(8,128)(2,1)S(1)} %get-tuple-element.8), channel_id=1, replica_groups={{256,288,320,352,384,416,448,480,0,32,64,96,128,160,192,224},{257,289,3..., dimensions={0} | all-to-all | bytes 327680 | tf_op jit(solution)/shard_map/all_to_all | solution.py:264
  32.4 2.3 %shard_map.74 = bf16[16,2,8,128]{3,2,1,0:T(8,128)(2,1)S(1)} custom-call(bf16[16,5,8,128]{3,2,1,0:T(8,128)(2,1)S(1)} %all_to_all.15.packed_ref, f32[8,128]{1,0:T(8,128)S(1)} %get-tuple-element.9.weights_ref, bf16[2,128,256]{2,1,0:T(8,128)(2,1)} %constant.32.clone.forward_hbm, f32[256,128]{1,0:T(8,128)} %constant.33.clone.inverse_hbm), custom_call_target="tpu_custom_call" | custom-call | flops 100000000 | bytes 600000 | tf_op jit(solution)/shard_map/pallas_call | solution.py:268
  34.6 15.2 %all_to_all.16.mixed_ref = bf16[16,2,8,128]{3,2,1,0:T(8,128)(2,1)S(1)} all-to-all(bf16[16,2,8,128]{3,2,1,0:T(8,128)(2,1)S(1)} %shard_map.74), channel_id=1, replica_groups={{256,288,320,352,384,416,448,480,0,32,64,96,128,160,192,224},{257,289,3..., dimensions={0} | all-to-all | bytes 131072 | tf_op jit(solution)/shard_map/all_to_all | solution.py:294
  49.8 0.1 shard_map.75
  49.9 2.6 %all-gather = bf16[512,128]{1,0:T(8,128)(2,1)S(1)} all-gather(bf16[256,128]{1,0:T(8,128)(2,1)S(1)} %shard_map.75), channel_id=2, replica_groups=mesh['ctx'=16,'chip'=16,'core'=2] {'core'}, dimensions={0}, use_global_device_ids=true | all-gather | bytes 196608 | tf_op jit(solution)/shard_map/all_gather | solution.py:304
  52.5 0.0 collective-permute-done.other_weight_ref
  52.5 0.0 copy-done
  52.5 1.3 %shard_map.76 = bf16[16,256,128]{2,1,0:T(8,128)(2,1)S(1)} custom-call(s32[2]{0:T(128)S(1)} %pad_add_fusion.index_ref, bf16[2,256,128]{2,1,0:T(8,128)(2,1)S(1)} %bitcast.12, bf16[128,4096]{1,0:T(8,128)(2,1)S(1)} %copy-done, bf16[128,4096]{1,0:T(8,128)(2,1)S(1)} %collective-permute-done.other_weight_ref), custom_call_target="tpu_custom_call" | custom-call | flops 268435456 | bytes 3300000 | tf_op jit(solution)/shard_map/pallas_call | solution.py:305
  53.8 22.6 %all_to_all.17 = bf16[16,256,128]{2,1,0:T(8,128)(2,1)S(1)} all-to-all(bf16[16,256,128]{2,1,0:T(8,128)(2,1)S(1)} %shard_map.76), channel_id=1, replica_groups=mesh['ctx'=16,'chip'=16,'core'=2] {'chip'}, dimensions={0} | all-to-all | bytes 2097152 | tf_op jit(solution)/shard_map/all_to_all | solution.py:314
  76.4 0.8 %reduce_sum.12 = bf16[256,128]{1,0:T(8,128)(2,1)} reduce(bf16[16,256,128]{2,1,0:T(8,128)(2,1)S(1)} %all_to_all.17, bf16[]{:T(256)} %constant.31.clone.1), dimensions={0}, to_apply=%region_0.1 | reduce | flops 491520 | bytes 1114114 | tf_op jit(solution)/shard_map/reduce_sum | solution.py:315
Async XLA Ops:
  0.0 52.5 %copy-start = (bf16[128,4096]{1,0:T(8,128)(2,1)S(1)}, bf16[128,4096]{1,0:T(8,128)(2,1)}, u32[]{:S(2)}) copy-start(bf16[128,4096]{1,0:T(8,128)(2,1)} %own_weight_ref.1) | copy-start | bytes 3145732
  0.0 52.5 %collective-permute-start = (bf16[128,4096]{1,0:T(8,128)(2,1)}, bf16[128,4096]{1,0:T(8,128)(2,1)S(1)}, u32[]{:S(2)}, u32[]{:S(2)}) collective-permute-start(bf16[128,4096]{1,0:T(8,128)(2,1)} %own_weight_ref.1), channel_id=1, source_target_pairs={{0,1},{1,0},{2,3},{3,2},{4,5},{5,4},{6,7},{7,6},{8,9},{9,8},{10,11... | collective-permute-start | bytes 3145736 | tf_op jit(solution)/shard_map/ppermute | solution.py:265

commit v5 on v4

--- a/solution.py
+++ b/solution.py
@@ -10,6 +10,8 @@
 
 INTERPRET = False
 MIB = 2**20
+CTX_FIRST = 11
+CHIP_FIRST = 14
 LANES = 128
 PERIOD = 2 * LANES
 
@@ -107,7 +109,7 @@
 
     def place(block):
         owner, half = (block, 0) if block < pairs else (blocks - 1 - block, 1)
-        return (owner + pairs // 2) % pairs, half
+        return (owner - CTX_FIRST) % pairs, half
 
     def span(block):
         return slice(block * channels, (block + 1) * channels)
@@ -212,7 +214,8 @@
     core = index_ref[1]
     lhs = jnp.concatenate([both_ref[core], both_ref[1 - core]], axis=1)
     for chip in range(chips):
-        columns = pl.ds(pl.multiple_of((2 * chip + core) * width, width), width)
+        block = 2 * ((chip + CHIP_FIRST) % chips) + core
+        columns = pl.ds(pl.multiple_of(block * width, width), width)
         weight = jnp.concatenate([own_weight_ref[:, columns], other_weight_ref[:, columns]], axis=0)
         out_ref[chip] = jnp.dot(lhs, weight, preferred_element_type=jnp.float32).astype(jnp.bfloat16)
 
@@ -223,8 +226,9 @@
     length = features.shape[2]
     width = features.shape[4]
     channels = width // pairs
-    order = [[(place + pairs // 2) % pairs for place in range(pairs)]]
-    position = (lax.axis_index("ctx") + pairs // 2) % pairs
+    order = [[(place + CTX_FIRST) % pairs for place in range(pairs)]]
+    chip_order = [[(place + CHIP_FIRST) % chips for place in range(chips)]]
+    position = (lax.axis_index("ctx") + pairs - CTX_FIRST) % pairs
     index = jnp.stack([position, lax.axis_index("core")]).astype(jnp.int32)
     tiles = jnp.transpose(features, (0, 1, 3, 2, 4)).reshape(2, 3, length, width)
     taps = jnp.transpose(short_weight, (1, 0, 2))
@@ -311,7 +315,7 @@
         cost_estimate=pl.CostEstimate(flops=268435456, bytes_accessed=3300000, transcendentals=0),
         interpret=INTERPRET,
     )(index, both, out_weight, other_weight)
-    shares = lax.all_to_all(partial, "chip", 0, 0, tiled=True)
+    shares = lax.all_to_all(partial, "chip", 0, 0, tiled=True, axis_index_groups=chip_order)
     result = jnp.sum(shares.astype(jnp.float32), axis=0).astype(jnp.bfloat16)
     return result.reshape(2, 1, length, width)
 

time: 77.5 us -> 75.3 us (0.972); the launches traced: 77.1 us -> 74 us
  blocking collectives: 61.6 us -> 58.5 us
    all_to_all x1, blocking collectives: 22.6 us -> 19.5 us  [local(): lax.all_to_all(partial, 'chip', 0, 0, tiled=True, axis_index_groups=chip_...]
where the time goes in v5:
time: 75.3 us; the launch traced here: 74 us
  blocking collectives  58.5 us (78%)
  starting transfers between devices  8.87 us (12%)
  Pallas kernels  5.71 us (8%)
  other arithmetic  0.85 us (1%)
    all_to_all x1, blocking collectives, local(): lax.all_to_all(packed, 'ctx', 0, 0, tiled=True, axis_index_groups=order)  20.7 us
    all_to_all x1, blocking collectives, local(): lax.all_to_all(partial, 'chip', 0, 0, tiled=True, axis_index_groups=chip_...  19.5 us
    all_to_all x1, blocking collectives, local(): lax.all_to_all(mixed, 'ctx', 0, 0, tiled=True, axis_index_groups=order)  15.1 us
    ppermute x1, starting transfers between devices, local(): other_weight = lax.ppermute(out_weight, 'core', [(0, 1), (1, 0)])  8.87 us
    all_gather x1, blocking collectives, local(): both = lax.all_gather(activated, 'core', axis=0)  3.2 us
    pallas_call x1, Pallas kernels, local(): pl.pallas_call(mix_kernel, out_shape=pltpu.VMEM((pairs, 2, channels, leng...  2.27 us
    pallas_call x1, Pallas kernels, local(): pl.pallas_call(pack_kernel, out_shape=(pltpu.VMEM((pairs, 5, channels, le...  2.06 us
  transfers between devices with their start and end apart: 1, of which 0 were waited for; matrix products, arithmetic and copies ran while one was open for 0% of the time, Pallas kernels for 6%

profile of v5, /device:TPU:1, one launch (start us, length us, event | category | flops | bytes accessed | tf_op | source)
XLA Modules:
  0.0 74.0 jit_solution(8895051465769454097)
XLA Ops:
  0.0 0.0 copy-start
  0.0 8.9 %collective-permute-start = (bf16[128,4096]{1,0:T(8,128)(2,1)}, bf16[128,4096]{1,0:T(8,128)(2,1)S(1)}, u32[]{:S(2)}, u32[]{:S(2)}) collective-permute-start(bf16[128,4096]{1,0:T(8,128)(2,1)} %own_weight_ref.1), channel_id=1, source_target_pairs={{0,1},{1,0},{2,3},{3,2},{4,5},{5,4},{6,7},{7,6},{8,9},{9,8},{10,11... | collective-permute-start | bytes 3145736 | tf_op jit(solution)/shard_map/ppermute | solution.py:269
  8.9 0.1 pad_add_fusion.index_ref
  9.0 2.1 %shard_map.73 = (bf16[16,5,8,128]{3,2,1,0:T(8,128)(2,1)S(1)}, f32[8,128]{1,0:T(8,128)S(1)}, f32[2,128,128]{2,1,0:T(8,128)S(1)}) custom-call(s32[2]{0:T(128)S(1)} %pad_add_fusion.index_ref, bf16[2,3,128,128]{3,2,1,0:T(8,128)(2,1)} %bitcast.13, bf16[2,128,128]{2,1,0:T(8,128)(2,1)} %bitcast.14, bf16[3,7,128]{2,1,0:T(8,128)(2,1)} %bitcast.15, f32[1,128]{1,0:T(1,128)} %bitcast.16), custom_call_target="tpu_custom_call" | custom-call | flops 1000000 | bytes 600000 | tf_op jit(solution)/shard_map/pallas_call | solution.py:238
  11.0 20.7 %all_to_all.15.packed_ref = bf16[16,5,8,128]{3,2,1,0:T(8,128)(2,1)S(1)} all-to-all(bf16[16,5,8,128]{3,2,1,0:T(8,128)(2,1)S(1)} %get-tuple-element.8), channel_id=1, replica_groups={{352,384,416,448,480,0,32,64,96,128,160,192,224,256,288,320},{353,385,4..., dimensions={0} | all-to-all | bytes 327680 | tf_op jit(solution)/shard_map/all_to_all | solution.py:268
  31.8 2.3 %shard_map.74 = bf16[16,2,8,128]{3,2,1,0:T(8,128)(2,1)S(1)} custom-call(bf16[16,5,8,128]{3,2,1,0:T(8,128)(2,1)S(1)} %all_to_all.15.packed_ref, f32[8,128]{1,0:T(8,128)S(1)} %get-tuple-element.9.weights_ref, bf16[2,128,256]{2,1,0:T(8,128)(2,1)} %constant.34.clone.forward_hbm, f32[256,128]{1,0:T(8,128)} %constant.35.clone.inverse_hbm), custom_call_target="tpu_custom_call" | custom-call | flops 100000000 | bytes 600000 | tf_op jit(solution)/shard_map/pallas_call | solution.py:272
  34.1 15.1 %all_to_all.16.mixed_ref = bf16[16,2,8,128]{3,2,1,0:T(8,128)(2,1)S(1)} all-to-all(bf16[16,2,8,128]{3,2,1,0:T(8,128)(2,1)S(1)} %shard_map.74), channel_id=1, replica_groups={{352,384,416,448,480,0,32,64,96,128,160,192,224,256,288,320},{353,385,4..., dimensions={0} | all-to-all | bytes 131072 | tf_op jit(solution)/shard_map/all_to_all | solution.py:298
  49.1 0.1 shard_map.75
  49.3 3.2 %all-gather = bf16[512,128]{1,0:T(8,128)(2,1)S(1)} all-gather(bf16[256,128]{1,0:T(8,128)(2,1)S(1)} %shard_map.75), channel_id=2, replica_groups=mesh['ctx'=16,'chip'=16,'core'=2] {'core'}, dimensions={0}, use_global_device_ids=true | all-gather | bytes 196608 | tf_op jit(solution)/shard_map/all_gather | solution.py:308
  52.5 0.0 collective-permute-done.other_weight_ref
  52.5 0.0 copy-done
  52.5 1.3 %shard_map.76 = bf16[16,256,128]{2,1,0:T(8,128)(2,1)S(1)} custom-call(s32[2]{0:T(128)S(1)} %pad_add_fusion.index_ref, bf16[2,256,128]{2,1,0:T(8,128)(2,1)S(1)} %bitcast.12, bf16[128,4096]{1,0:T(8,128)(2,1)S(1)} %copy-done, bf16[128,4096]{1,0:T(8,128)(2,1)S(1)} %collective-permute-done.other_weight_ref), custom_call_target="tpu_custom_call" | custom-call | flops 268435456 | bytes 3300000 | tf_op jit(solution)/shard_map/pallas_call | solution.py:309
  53.7 19.5 %all_to_all.17 = bf16[16,256,128]{2,1,0:T(8,128)(2,1)S(1)} all-to-all(bf16[16,256,128]{2,1,0:T(8,128)(2,1)S(1)} %shard_map.76), channel_id=1, replica_groups={{28,30,0,2,4,6,8,10,12,14,16,18,20,22,24,26},{29,31,1,3,5,7,9,11,13,15,..., dimensions={0} | all-to-all | bytes 2097152 | tf_op jit(solution)/shard_map/all_to_all | solution.py:318
  73.3 0.8 %reduce_sum.12 = bf16[256,128]{1,0:T(8,128)(2,1)} reduce(bf16[16,256,128]{2,1,0:T(8,128)(2,1)S(1)} %all_to_all.17, bf16[]{:T(256)} %constant.33.clone.1), dimensions={0}, to_apply=%region_0.1 | reduce | flops 491520 | bytes 1114114 | tf_op jit(solution)/shard_map/reduce_sum | solution.py:319
Async XLA Ops:
  0.0 52.5 %copy-start = (bf16[128,4096]{1,0:T(8,128)(2,1)S(1)}, bf16[128,4096]{1,0:T(8,128)(2,1)}, u32[]{:S(2)}) copy-start(bf16[128,4096]{1,0:T(8,128)(2,1)} %own_weight_ref.1) | copy-start | bytes 3145732
  0.0 52.5 %collective-permute-start = (bf16[128,4096]{1,0:T(8,128)(2,1)}, bf16[128,4096]{1,0:T(8,128)(2,1)S(1)}, u32[]{:S(2)}, u32[]{:S(2)}) collective-permute-start(bf16[128,4096]{1,0:T(8,128)(2,1)} %own_weight_ref.1), channel_id=1, source_target_pairs={{0,1},{1,0},{2,3},{3,2},{4,5},{5,4},{6,7},{7,6},{8,9},{9,8},{10,11... | collective-permute-start | bytes 3145736 | tf_op jit(solution)/shard_map/ppermute | solution.py:269

commit v6 on v5

--- a/solution.py
+++ b/solution.py
@@ -31,9 +31,13 @@
     inverse = np.concatenate(
         [cosine * scale, np.where(k == 0, sign / PERIOD, sine * scale)], axis=1
     ).T
-    high = forward.astype(jnp.bfloat16)
-    low = (forward - high.astype(np.float64)).astype(jnp.bfloat16)
-    return np.stack([high, low]), inverse.astype(np.float32)
+
+    def split(table, axis):
+        high = table.astype(jnp.bfloat16)
+        low = (table - high.astype(np.float64)).astype(jnp.bfloat16)
+        return np.concatenate([high, low], axis=axis)
+
+    return split(forward, 0), split(inverse, 1)
 
 
 def pack_kernel(
@@ -92,13 +96,21 @@
 
 
 def mix_kernel(
-    packed_ref, weights_ref, forward_hbm, inverse_hbm, out_ref,
+    index_ref, packed_ref, weights_ref, forward_hbm, inverse_hbm, matrix_hbm, out_ref, matrix_ref,
     query, keys, lags, key_spec, lag_spec, resp, total, forward_ref, inverse_ref, sems,
 ):
     forward_copy = pltpu.make_async_copy(forward_hbm, forward_ref, sems.at[0])
     inverse_copy = pltpu.make_async_copy(inverse_hbm, inverse_ref, sems.at[1])
     forward_copy.start()
     inverse_copy.start()
+    chips = matrix_ref.shape[0]
+    matrix_copies = []
+    for chip in range(chips):
+        block = 2 * ((chip + CHIP_FIRST) % chips) + index_ref[1]
+        columns = pl.ds(pl.multiple_of(block * LANES, LANES), LANES)
+        copy = pltpu.make_async_copy(matrix_hbm.at[:, columns], matrix_ref.at[chip], sems.at[2 + chip])
+        copy.start()
+        matrix_copies.append(copy)
     pairs = packed_ref.shape[0]
     blocks = 2 * pairs
     channels = packed_ref.shape[2]
@@ -148,8 +160,8 @@
             query[span(block)] = pltpu.roll(summed, LANES - first, 1)
 
     def transform(values):
-        return jnp.dot(values, forward_ref[0], preferred_element_type=jnp.float32) + jnp.dot(
-            values, forward_ref[1], preferred_element_type=jnp.float32
+        return jnp.dot(
+            jnp.concatenate([values, values], axis=1), forward_ref[...], preferred_element_type=jnp.float32
         )
 
     forward_copy.wait()
@@ -162,41 +174,45 @@
         if block:
             real = real + parity * lag_spec[span(block - 1), :LANES]
             imag = imag + parity * lag_spec[span(block - 1), LANES:]
-        resp[0, span(block)] = real
-        resp[1, span(block)] = jnp.where(lane == 0, 0.0, imag)
-        resp[2, span(block)] = jnp.where(lane == 0, imag, real)
+        cross = jnp.where(lane == 0, 0.0, imag)
+        resp[0, span(block)] = real + cross
+        resp[1, span(block)] = cross
+        resp[2, span(block)] = jnp.where(lane == 0, imag, real) - cross
     group = 4
     for base in range(0, blocks, group):
-        sums = [[None, None] for _ in range(group)]
+        sums = [None] * group
         for block in range(base + group):
             real = key_spec[span(block), :LANES]
             imag = key_spec[span(block), LANES:]
+            both = real + imag
             for j in range(group):
                 gap = base + j - block
                 if gap < 0:
                     continue
-                first = resp[0, span(gap)]
-                cross = resp[1, span(gap)]
-                second = resp[2, span(gap)]
-                out_real = real * first - imag * cross
-                out_imag = real * cross + imag * second
-                if sums[j][0] is None:
-                    sums[j] = [out_real, out_imag]
-                else:
-                    sums[j] = [sums[j][0] + out_real, sums[j][1] + out_imag]
+                terms = [
+                    real * resp[0, span(gap)],
+                    both * resp[1, span(gap)],
+                    imag * resp[2, span(gap)],
+                ]
+                if sums[j] is not None:
+                    terms = [one + other for one, other in zip(sums[j], terms)]
+                sums[j] = terms
         for j in range(group):
-            total[span(base + j), :LANES] = sums[j][0]
-            total[span(base + j), LANES:] = sums[j][1]
+            total[span(base + j), :LANES] = sums[j][0] - sums[j][1]
+            total[span(base + j), LANES:] = sums[j][1] + sums[j][2]
     inverse_copy.wait()
-    convolved = jnp.dot(
-        total[...], inverse_ref[...], preferred_element_type=jnp.float32, precision=lax.Precision.HIGHEST
-    )
-    total[:, :LANES] = convolved
+    high = total[...].astype(jnp.bfloat16)
+    low = (total[...] - high.astype(jnp.float32)).astype(jnp.bfloat16)
+    wide = jnp.dot(high, inverse_ref[...], preferred_element_type=jnp.float32)
+    narrow = jnp.dot(low, inverse_ref[:, :LANES], preferred_element_type=jnp.float32)
+    total[:, :LANES] = wide[:, :LANES] + (wide[:, LANES:] + narrow)
     gain = column(24)
     for block in range(blocks):
         target, half = place(block)
         inner = total[span(block), :LANES] + gain * keys[span(block)].astype(jnp.float32)
         out_ref[target, half] = jnp.where(head, query[span(block)] * inner, inner).astype(jnp.bfloat16)
+    for copy in matrix_copies:
+        copy.wait()
 
 
 def activate_kernel(mixed_ref, query_ref, out_ref):
@@ -213,11 +229,18 @@
     chips, _, width = out_ref.shape
     core = index_ref[1]
     lhs = jnp.concatenate([both_ref[core], both_ref[1 - core]], axis=1)
-    for chip in range(chips):
+
+    def columns(chip):
         block = 2 * ((chip + CHIP_FIRST) % chips) + core
-        columns = pl.ds(pl.multiple_of(block * width, width), width)
-        weight = jnp.concatenate([own_weight_ref[:, columns], other_weight_ref[:, columns]], axis=0)
-        out_ref[chip] = jnp.dot(lhs, weight, preferred_element_type=jnp.float32).astype(jnp.bfloat16)
+        other = other_weight_ref[:, pl.ds(pl.multiple_of(block * width, width), width)]
+        return jnp.concatenate([own_weight_ref[chip], other], axis=0)
+
+    step = math.gcd(chips, 2)
+    for first in range(0, chips, step):
+        weight = jnp.concatenate([columns(first + i) for i in range(step)], axis=1)
+        product = jnp.dot(lhs, weight, preferred_element_type=jnp.float32).astype(jnp.bfloat16)
+        for i in range(step):
+            out_ref[first + i] = product[:, i * width : (i + 1) * width]
 
 
 def local(features, short_weight, long_filter, skip_gain, out_weight):
@@ -269,11 +292,14 @@
     other_weight = lax.ppermute(out_weight, "core", [(0, 1), (1, 0)])
     forward, inverse = tables()
     rows = 2 * pairs * channels
-    mixed = pl.pallas_call(
+    mixed, own_weight = pl.pallas_call(
         mix_kernel,
-        out_shape=pltpu.VMEM((pairs, 2, channels, length), jnp.bfloat16),
-        in_specs=[vmem] * 2 + [hbm] * 2,
-        out_specs=vmem,
+        out_shape=(
+            pltpu.VMEM((pairs, 2, channels, length), jnp.bfloat16),
+            pltpu.VMEM((chips, width, width), jnp.bfloat16),
+        ),
+        in_specs=[scalars] + [vmem] * 2 + [hbm] * 3,
+        out_specs=(vmem, vmem),
         scratch_shapes=[
             pltpu.VMEM((rows, LANES), jnp.float32),
             pltpu.VMEM((rows, LANES), jnp.bfloat16),
@@ -283,17 +309,19 @@
             pltpu.VMEM((3, rows, LANES), jnp.float32),
             pltpu.VMEM((rows, PERIOD), jnp.float32),
             pltpu.VMEM(forward.shape, jnp.bfloat16),
-            pltpu.VMEM(inverse.shape, jnp.float32),
-            pltpu.SemaphoreType.DMA((2,)),
+            pltpu.VMEM(inverse.shape, jnp.bfloat16),
+            pltpu.SemaphoreType.DMA((2 + chips,)),
         ],
         compiler_params=pltpu.CompilerParams(vmem_limit_bytes=6 * MIB),
         cost_estimate=pl.CostEstimate(flops=100000000, bytes_accessed=600000, transcendentals=0),
         interpret=INTERPRET,
     )(
+        index,
         packed,
         weights,
         in_hbm(jnp.asarray(forward)),
         in_hbm(jnp.asarray(inverse)),
+        in_hbm(out_weight),
     )
     mixed = lax.all_to_all(mixed, "ctx", 0, 0, tiled=True, axis_index_groups=order)
     activated = pl.pallas_call(
@@ -314,7 +342,7 @@
         compiler_params=pltpu.CompilerParams(vmem_limit_bytes=8 * MIB),
         cost_estimate=pl.CostEstimate(flops=268435456, bytes_accessed=3300000, transcendentals=0),
         interpret=INTERPRET,
-    )(index, both, out_weight, other_weight)
+    )(index, both, own_weight, other_weight)
     shares = lax.all_to_all(partial, "chip", 0, 0, tiled=True, axis_index_groups=chip_order)
     result = jnp.sum(shares.astype(jnp.float32), axis=0).astype(jnp.bfloat16)
     return result.reshape(2, 1, length, width)

time: 75.3 us -> 75.3 us (level)
  transfers between devices with their start and end apart: 1 -> 1, of which waited for: 0 -> 0; matrix products, arithmetic and copies ran while one was open for 0% -> 0% of each run, Pallas kernels for 6% -> 7%
where the time goes in v6:
time: 75.3 us; the launch traced here: 74 us
  blocking collectives  58.5 us (78%)
  starting transfers between devices  8.74 us (12%)
  Pallas kernels  5.84 us (8%)
  other arithmetic  0.85 us (1%)
    all_to_all x1, blocking collectives, local(): lax.all_to_all(packed, 'ctx', 0, 0, tiled=True, axis_index_groups=order)  20.7 us
    all_to_all x1, blocking collectives, local(): lax.all_to_all(partial, 'chip', 0, 0, tiled=True, axis_index_groups=chip_...  19.5 us
    all_to_all x1, blocking collectives, local(): lax.all_to_all(mixed, 'ctx', 0, 0, tiled=True, axis_index_groups=order)  15.1 us
    ppermute x1, starting transfers between devices, local(): other_weight = lax.ppermute(out_weight, 'core', [(0, 1), (1, 0)])  8.74 us
    all_gather x1, blocking collectives, local(): both = lax.all_gather(activated, 'core', axis=0)  3.2 us
    pallas_call x1, Pallas kernels, local(): pl.pallas_call(mix_kernel, out_shape=(pltpu.VMEM((pairs, 2, channels, len...  2.68 us
    pallas_call x1, Pallas kernels, local(): pl.pallas_call(pack_kernel, out_shape=(pltpu.VMEM((pairs, 5, channels, le...  2.06 us
  transfers between devices with their start and end apart: 1, of which 0 were waited for; matrix products, arithmetic and copies ran while one was open for 0% of the time, Pallas kernels for 7%

profile of v6, /device:TPU:1, one launch (start us, length us, event | category | flops | bytes accessed | tf_op | source)
XLA Modules:
  0.0 74.0 jit_solution(8711544762702830509)
XLA Ops:
  0.0 8.7 %collective-permute-start = (bf16[128,4096]{1,0:T(8,128)(2,1)}, bf16[128,4096]{1,0:T(8,128)(2,1)S(1)}, u32[]{:S(2)}, u32[]{:S(2)}) collective-permute-start(bf16[128,4096]{1,0:T(8,128)(2,1)} %matrix_hbm.1), channel_id=1, source_target_pairs={{0,1},{1,0},{2,3},{3,2},{4,5},{5,4},{6,7},{7,6},{8,9},{9,8},{10,11... | collective-permute-start | bytes 3145736 | tf_op jit(solution)/shard_map/ppermute | solution.py:292
  8.8 0.1 pad_add_fusion.index_ref
  8.8 2.1 %shard_map.73 = (bf16[16,5,8,128]{3,2,1,0:T(8,128)(2,1)S(1)}, f32[8,128]{1,0:T(8,128)S(1)}, f32[2,128,128]{2,1,0:T(8,128)S(1)}) custom-call(s32[2]{0:T(128)S(1)} %pad_add_fusion.index_ref, bf16[2,3,128,128]{3,2,1,0:T(8,128)(2,1)} %bitcast.13, bf16[2,128,128]{2,1,0:T(8,128)(2,1)} %bitcast.14, bf16[3,7,128]{2,1,0:T(8,128)(2,1)} %bitcast.15, f32[1,128]{1,0:T(1,128)} %bitcast.16), custom_call_target="tpu_custom_call" | custom-call | flops 1000000 | bytes 600000 | tf_op jit(solution)/shard_map/pallas_call | solution.py:261
  10.9 20.7 %all_to_all.15.packed_ref = bf16[16,5,8,128]{3,2,1,0:T(8,128)(2,1)S(1)} all-to-all(bf16[16,5,8,128]{3,2,1,0:T(8,128)(2,1)S(1)} %get-tuple-element.10), channel_id=1, replica_groups={{352,384,416,448,480,0,32,64,96,128,160,192,224,256,288,320},{353,385,4..., dimensions={0} | all-to-all | bytes 327680 | tf_op jit(solution)/shard_map/all_to_all | solution.py:291
  31.7 2.7 %shard_map.74 = (bf16[16,2,8,128]{3,2,1,0:T(8,128)(2,1)S(1)}, bf16[16,128,128]{2,1,0:T(8,128)(2,1)S(1)}) custom-call(s32[2]{0:T(128)S(1)} %pad_add_fusion.index_ref, bf16[16,5,8,128]{3,2,1,0:T(8,128)(2,1)S(1)} %all_to_all.15.packed_ref, f32[8,128]{1,0:T(8,128)S(1)} %get-tuple-element.11.weights_ref, bf16[256,256]{1,0:T(8,128)(2,1)} %constant.34.clone.forward_hbm, ...), custom_call_target="tpu_custom_call" | custom-call | flops 100000000 | bytes 600000 | tf_op jit(solution)/shard_map/pallas_call | solution.py:295
  34.3 15.1 %all_to_all.16.mixed_ref = bf16[16,2,8,128]{3,2,1,0:T(8,128)(2,1)S(1)} all-to-all(bf16[16,2,8,128]{3,2,1,0:T(8,128)(2,1)S(1)} %get-tuple-element.12), channel_id=1, replica_groups={{352,384,416,448,480,0,32,64,96,128,160,192,224,256,288,320},{353,385,4..., dimensions={0} | all-to-all | bytes 131072 | tf_op jit(solution)/shard_map/all_to_all | solution.py:326
  49.4 0.1 shard_map.75
  49.5 3.2 %all-gather = bf16[512,128]{1,0:T(8,128)(2,1)S(1)} all-gather(bf16[256,128]{1,0:T(8,128)(2,1)S(1)} %shard_map.75), channel_id=2, replica_groups=mesh['ctx'=16,'chip'=16,'core'=2] {'core'}, dimensions={0}, use_global_device_ids=true | all-gather | bytes 196608 | tf_op jit(solution)/shard_map/all_gather | solution.py:336
  52.7 0.0 collective-permute-done.other_weight_ref
  52.7 1.0 %shard_map.76 = bf16[16,256,128]{2,1,0:T(8,128)(2,1)S(1)} custom-call(s32[2]{0:T(128)S(1)} %pad_add_fusion.index_ref, bf16[2,256,128]{2,1,0:T(8,128)(2,1)S(1)} %bitcast.12, bf16[16,128,128]{2,1,0:T(8,128)(2,1)S(1)} %get-tuple-element.14.own_weight_ref, bf16[128,4096]{1,0:T(8,128)(2,1)S(1)} %collective-permute-done.other_weight_ref), custom_call_target="tpu_custom_call" | custom-call | flops 268435456 | bytes 3300000 | tf_op jit(solution)/shard_map/pallas_call | solution.py:337
  53.7 19.5 %all_to_all.17 = bf16[16,256,128]{2,1,0:T(8,128)(2,1)S(1)} all-to-all(bf16[16,256,128]{2,1,0:T(8,128)(2,1)S(1)} %shard_map.76), channel_id=1, replica_groups={{28,30,0,2,4,6,8,10,12,14,16,18,20,22,24,26},{29,31,1,3,5,7,9,11,13,15,..., dimensions={0} | all-to-all | bytes 2097152 | tf_op jit(solution)/shard_map/all_to_all | solution.py:346
  73.3 0.8 %reduce_sum.12 = bf16[256,128]{1,0:T(8,128)(2,1)} reduce(bf16[16,256,128]{2,1,0:T(8,128)(2,1)S(1)} %all_to_all.17, bf16[]{:T(256)} %constant.33.clone.1), dimensions={0}, to_apply=%region_0.1 | reduce | flops 491520 | bytes 1114114 | tf_op jit(solution)/shard_map/reduce_sum | solution.py:347
Async XLA Ops:
  0.0 52.7 %collective-permute-start = (bf16[128,4096]{1,0:T(8,128)(2,1)}, bf16[128,4096]{1,0:T(8,128)(2,1)S(1)}, u32[]{:S(2)}, u32[]{:S(2)}) collective-permute-start(bf16[128,4096]{1,0:T(8,128)(2,1)} %matrix_hbm.1), channel_id=1, source_target_pairs={{0,1},{1,0},{2,3},{3,2},{4,5},{5,4},{6,7},{7,6},{8,9},{9,8},{10,11... | collective-permute-start | bytes 3145736 | tf_op jit(solution)/shard_map/ppermute | solution.py:292

commit v7 on v6

--- a/solution.py
+++ b/solution.py
@@ -11,9 +11,20 @@
 INTERPRET = False
 MIB = 2**20
 CTX_FIRST = 11
-CHIP_FIRST = 14
 LANES = 128
 PERIOD = 2 * LANES
+
+
+def row_first(side):
+    return side - 1
+
+
+def part_first(parts):
+    return parts - 2
+
+
+def rotated(first, count):
+    return [[(place + first) % count for place in range(count)]]
 
 
 def in_hbm(value):
@@ -96,21 +107,13 @@
 
 
 def mix_kernel(
-    index_ref, packed_ref, weights_ref, forward_hbm, inverse_hbm, matrix_hbm, out_ref, matrix_ref,
+    packed_ref, weights_ref, forward_hbm, inverse_hbm, out_ref,
     query, keys, lags, key_spec, lag_spec, resp, total, forward_ref, inverse_ref, sems,
 ):
     forward_copy = pltpu.make_async_copy(forward_hbm, forward_ref, sems.at[0])
     inverse_copy = pltpu.make_async_copy(inverse_hbm, inverse_ref, sems.at[1])
     forward_copy.start()
     inverse_copy.start()
-    chips = matrix_ref.shape[0]
-    matrix_copies = []
-    for chip in range(chips):
-        block = 2 * ((chip + CHIP_FIRST) % chips) + index_ref[1]
-        columns = pl.ds(pl.multiple_of(block * LANES, LANES), LANES)
-        copy = pltpu.make_async_copy(matrix_hbm.at[:, columns], matrix_ref.at[chip], sems.at[2 + chip])
-        copy.start()
-        matrix_copies.append(copy)
     pairs = packed_ref.shape[0]
     blocks = 2 * pairs
     channels = packed_ref.shape[2]
@@ -211,8 +214,6 @@
         target, half = place(block)
         inner = total[span(block), :LANES] + gain * keys[span(block)].astype(jnp.float32)
         out_ref[target, half] = jnp.where(head, query[span(block)] * inner, inner).astype(jnp.bfloat16)
-    for copy in matrix_copies:
-        copy.wait()
 
 
 def activate_kernel(mixed_ref, query_ref, out_ref):
@@ -222,37 +223,55 @@
     for half in range(halves):
         inner = mixed_ref[:, half].reshape(groups * channels, length).astype(jnp.float32).T
         product = jnp.where(token < rim, inner, query_ref[half] * inner)
-        out_ref[half * length : (half + 1) * length] = product.astype(jnp.bfloat16)
-
-
-def project_kernel(index_ref, both_ref, own_weight_ref, other_weight_ref, out_ref):
-    chips, _, width = out_ref.shape
-    core = index_ref[1]
-    lhs = jnp.concatenate([both_ref[core], both_ref[1 - core]], axis=1)
-
-    def columns(chip):
-        block = 2 * ((chip + CHIP_FIRST) % chips) + core
-        other = other_weight_ref[:, pl.ds(pl.multiple_of(block * width, width), width)]
-        return jnp.concatenate([own_weight_ref[chip], other], axis=0)
-
-    step = math.gcd(chips, 2)
-    for first in range(0, chips, step):
-        weight = jnp.concatenate([columns(first + i) for i in range(step)], axis=1)
+        for copy in range(out_ref.shape[0]):
+            out_ref[copy, half * length : (half + 1) * length] = product.astype(jnp.bfloat16)
+
+
+def divide_kernel(index_ref, weight_hbm, *refs):
+    pieces, sems = refs[:-1], refs[-1]
+    side = len(pieces)
+    share = pieces[0].shape[1]
+    copies = []
+    for step, piece in enumerate(pieces):
+        columns = pl.ds(pl.multiple_of((index_ref[1] + step) % side * share, share), share)
+        copies.append(pltpu.make_async_copy(weight_hbm.at[:, columns], piece, sems.at[step]))
+    for copy in copies:
+        copy.start()
+    for copy in copies:
+        copy.wait()
+
+
+def arrange_kernel(index_ref, row_ref, out_ref):
+    side, _, width = row_ref.shape
+    shift = row_first(side)
+    for step in range(side):
+        source = (index_ref[1] + (2 * side - step - shift)) % side
+        out_ref[:, step * width : (step + 1) * width] = row_ref[source]
+
+
+def project_kernel(lhs_ref, *refs):
+    weights, out_ref = refs[:-1], refs[-1]
+    parts, _, width = out_ref.shape
+    lhs = lhs_ref[...]
+    for part in range(0, parts, 2):
+        columns = slice(part * width, (part + 2) * width)
+        weight = jnp.concatenate([piece[:, columns] for piece in weights], axis=0)
         product = jnp.dot(lhs, weight, preferred_element_type=jnp.float32).astype(jnp.bfloat16)
-        for i in range(step):
-            out_ref[first + i] = product[:, i * width : (i + 1) * width]
+        for i in range(2):
+            place = (part + i - part_first(parts)) % parts
+            out_ref[place] = product[:, i * width : (i + 1) * width]
 
 
 def local(features, short_weight, long_filter, skip_gain, out_weight):
     pairs = lax.axis_size("ctx")
-    chips = lax.axis_size("chip")
+    side = lax.axis_size("x")
+    parts = 2 * lax.axis_size("y")
     length = features.shape[2]
     width = features.shape[4]
     channels = width // pairs
-    order = [[(place + CTX_FIRST) % pairs for place in range(pairs)]]
-    chip_order = [[(place + CHIP_FIRST) % chips for place in range(chips)]]
+    order = rotated(CTX_FIRST, pairs)
     position = (lax.axis_index("ctx") + pairs - CTX_FIRST) % pairs
-    index = jnp.stack([position, lax.axis_index("core")]).astype(jnp.int32)
+    index = jnp.stack([position, lax.axis_index("x")]).astype(jnp.int32)
     tiles = jnp.transpose(features, (0, 1, 3, 2, 4)).reshape(2, 3, length, width)
     taps = jnp.transpose(short_weight, (1, 0, 2))
     scalars = pl.BlockSpec(memory_space=pltpu.SMEM)
@@ -289,17 +308,27 @@
         in_hbm(skip_gain.reshape(1, width)),
     )
     packed = lax.all_to_all(packed, "ctx", 0, 0, tiled=True, axis_index_groups=order)
-    other_weight = lax.ppermute(out_weight, "core", [(0, 1), (1, 0)])
+    pieces = pl.pallas_call(
+        divide_kernel,
+        out_shape=(jax.ShapeDtypeStruct((width, parts * width), jnp.bfloat16),) * side,
+        in_specs=[scalars, hbm],
+        out_specs=(vmem,) * side,
+        scratch_shapes=[pltpu.SemaphoreType.DMA((side,))],
+        compiler_params=pltpu.CompilerParams(vmem_limit_bytes=4 * MIB),
+        cost_estimate=pl.CostEstimate(flops=0, bytes_accessed=2 * MIB, transcendentals=0),
+        interpret=INTERPRET,
+    )(index, in_hbm(out_weight))
+    pieces = [pieces[0]] + [
+        lax.ppermute(pieces[step], "x", [(source, (source + step) % side) for source in range(side)])
+        for step in range(1, side)
+    ]
     forward, inverse = tables()
     rows = 2 * pairs * channels
-    mixed, own_weight = pl.pallas_call(
+    mixed = pl.pallas_call(
         mix_kernel,
-        out_shape=(
-            pltpu.VMEM((pairs, 2, channels, length), jnp.bfloat16),
-            pltpu.VMEM((chips, width, width), jnp.bfloat16),
-        ),
-        in_specs=[scalars] + [vmem] * 2 + [hbm] * 3,
-        out_specs=(vmem, vmem),
+        out_shape=pltpu.VMEM((pairs, 2, channels, length), jnp.bfloat16),
+        in_specs=[vmem] * 2 + [hbm] * 2,
+        out_specs=vmem,
         scratch_shapes=[
             pltpu.VMEM((rows, LANES), jnp.float32),
             pltpu.VMEM((rows, LANES), jnp.bfloat16),
@@ -310,48 +339,60 @@
             pltpu.VMEM((rows, PERIOD), jnp.float32),
             pltpu.VMEM(forward.shape, jnp.bfloat16),
             pltpu.VMEM(inverse.shape, jnp.bfloat16),
-            pltpu.SemaphoreType.DMA((2 + chips,)),
+            pltpu.SemaphoreType.DMA((2,)),
         ],
         compiler_params=pltpu.CompilerParams(vmem_limit_bytes=6 * MIB),
         cost_estimate=pl.CostEstimate(flops=100000000, bytes_accessed=600000, transcendentals=0),
         interpret=INTERPRET,
     )(
-        index,
         packed,
         weights,
         in_hbm(jnp.asarray(forward)),
         in_hbm(jnp.asarray(inverse)),
-        in_hbm(out_weight),
     )
     mixed = lax.all_to_all(mixed, "ctx", 0, 0, tiled=True, axis_index_groups=order)
     activated = pl.pallas_call(
         activate_kernel,
-        out_shape=pltpu.VMEM((2 * length, width), jnp.bfloat16),
+        out_shape=pltpu.VMEM((side, 2 * length, width), jnp.bfloat16),
         in_specs=[vmem] * 2,
         out_specs=vmem,
         compiler_params=pltpu.CompilerParams(vmem_limit_bytes=4 * MIB),
         cost_estimate=pl.CostEstimate(flops=1000000, bytes_accessed=300000, transcendentals=0),
         interpret=INTERPRET,
     )(mixed, query)
-    both = lax.all_gather(activated, "core", axis=0)
+    row = lax.all_to_all(
+        activated, "x", 0, 0, tiled=True, axis_index_groups=rotated(row_first(side), side)
+    )
+    lhs = pl.pallas_call(
+        arrange_kernel,
+        out_shape=pltpu.VMEM((2 * length, side * width), jnp.bfloat16),
+        in_specs=[scalars, vmem],
+        out_specs=vmem,
+        compiler_params=pltpu.CompilerParams(vmem_limit_bytes=4 * MIB),
+        cost_estimate=pl.CostEstimate(flops=0, bytes_accessed=500000, transcendentals=0),
+        interpret=INTERPRET,
+    )(index, row)
     partial = pl.pallas_call(
         project_kernel,
-        out_shape=pltpu.VMEM((chips, 2 * length, width), jnp.bfloat16),
-        in_specs=[scalars] + [vmem] * 3,
+        out_shape=pltpu.VMEM((parts, 2 * length, width), jnp.bfloat16),
+        in_specs=[vmem] * (1 + side),
         out_specs=vmem,
         compiler_params=pltpu.CompilerParams(vmem_limit_bytes=8 * MIB),
         cost_estimate=pl.CostEstimate(flops=268435456, bytes_accessed=3300000, transcendentals=0),
         interpret=INTERPRET,
-    )(index, both, own_weight, other_weight)
-    shares = lax.all_to_all(partial, "chip", 0, 0, tiled=True, axis_index_groups=chip_order)
+    )(lhs, *pieces)
+    shares = lax.all_to_all(
+        partial, ("y", "core"), 0, 0, tiled=True, axis_index_groups=rotated(part_first(parts), parts)
+    )
     result = jnp.sum(shares.astype(jnp.float32), axis=0).astype(jnp.bfloat16)
     return result.reshape(2, 1, length, width)
 
 
 def solution(mesh):
     pairs, parts = mesh.shape["ctx"], mesh.shape["ch"]
-    split = Mesh(mesh.devices.reshape(pairs, parts // 2, 2), ("ctx", "chip", "core"))
-    ch = ("chip", "core")
+    side = math.isqrt(parts // 2)
+    split = Mesh(mesh.devices.reshape(pairs, side, side, 2), ("ctx", "x", "y", "core"))
+    ch = ("x", "y", "core")
     in_specs = (
         P(None, "ctx", None, None, ch),
         P(None, None, ch),

time: 75.3 us -> 81 us (1.076)
  starting transfers between devices: 8.74 us -> 20.6 us
  blocking collectives: 58.5 us -> 50.6 us
  Pallas kernels: 5.84 us -> 7.58 us
    all_to_all x2, blocking collectives: 34.6 us -> 24.4 us  [the longest x1 15.3 us: local(): lax.all_to_all(partial, ('y', 'core'), 0, 0, tiled=True, axis_index_group...]
    all_to_all x0 -> x1, starting transfers between devices: none -> 10.1 us  [local(): lax.all_to_all(mixed, 'ctx', 0, 0, tiled=True, axis_index_groups=order)]
    all_to_all x1, blocking collectives: 20.7 us -> 26.2 us  [local(): lax.all_to_all(packed, 'ctx', 0, 0, tiled=True, axis_index_groups=order)]
    all_gather x1 -> x0, blocking collectives: 3.2 us -> none  [local(): both = lax.all_gather(activated, 'core', axis=0)]
    ppermute x1 -> x3, starting transfers between devices: 8.74 us -> 10.5 us  [local(): lax.ppermute(pieces[step], 'x', [(source, (source + step) % side) for sou...]
    pallas_call x3 -> x5, Pallas kernels: 3.78 us -> 5.52 us  [the longest x1 2.6 us: local(): pl.pallas_call(mix_kernel, out_shape=pltpu.VMEM((pairs, 2, channels, leng...]
  transfers between devices with their start and end apart: 1 -> 4, of which waited for: 0 -> 0; matrix products, arithmetic and copies ran while one was open for 0% -> 0% of each run, Pallas kernels for 7% -> 3%
where the time goes in v7:
time: 81 us; the launch traced here: 79.7 us
  blocking collectives  50.6 us (62%)
  starting transfers between devices  20.6 us (25%)
  Pallas kernels  7.58 us (9%)
    all_to_all x1, blocking collectives, local(): lax.all_to_all(packed, 'ctx', 0, 0, tiled=True, axis_index_groups=order)  26.2 us
    all_to_all x1, blocking collectives, local(): lax.all_to_all(partial, ('y', 'core'), 0, 0, tiled=True, axis_index_group...  15.3 us
    ppermute x3, starting transfers between devices, local(): lax.ppermute(pieces[step], 'x', [(source, (source + step) % side) for sou...  10.5 us
    all_to_all x1, starting transfers between devices, local(): lax.all_to_all(mixed, 'ctx', 0, 0, tiled=True, axis_index_groups=order)  10.1 us
    all_to_all x1, blocking collectives, local(): lax.all_to_all(activated, 'x', 0, 0, tiled=True, axis_index_groups=rotate...  9.14 us
    pallas_call x1, Pallas kernels, local(): pl.pallas_call(mix_kernel, out_shape=pltpu.VMEM((pairs, 2, channels, leng...  2.6 us
    pallas_call x1, Pallas kernels, local(): pl.pallas_call(pack_kernel, out_shape=(pltpu.VMEM((pairs, 5, channels, le...  2.06 us
    pallas_call x1, Pallas kernels, local(): pl.pallas_call(divide_kernel, out_shape=(jax.ShapeDtypeStruct((width, par...  1.77 us
  transfers between devices with their start and end apart: 4, of which 0 were waited for; matrix products, arithmetic and copies ran while one was open for 0% of the time, Pallas kernels for 3%

profile of v7, /device:TPU:1, one launch (start us, length us, event | category | flops | bytes accessed | tf_op | source)
XLA Modules:
  0.0 79.7 jit_solution(12199939897973057959)
XLA Ops:
  0.0 0.1 pad_add_fusion.index_ref
  0.1 2.1 %shard_map.73 = (bf16[16,5,8,128]{3,2,1,0:T(8,128)(2,1)S(1)}, f32[8,128]{1,0:T(8,128)S(1)}, f32[2,128,128]{2,1,0:T(8,128)S(1)}) custom-call(s32[2]{0:T(128)S(1)} %pad_add_fusion.index_ref, bf16[2,3,128,128]{3,2,1,0:T(8,128)(2,1)} %bitcast.11, bf16[2,128,128]{2,1,0:T(8,128)(2,1)} %bitcast.12, bf16[3,7,128]{2,1,0:T(8,128)(2,1)} %bitcast.13, f32[1,128]{1,0:T(1,128)} %bitcast.14), custom_call_target="tpu_custom_call" | custom-call | flops 1000000 | bytes 600000 | tf_op jit(solution)/shard_map/pallas_call | solution.py:280
  2.1 26.2 %all_to_all.20.packed_ref = bf16[16,5,8,128]{3,2,1,0:T(8,128)(2,1)S(1)} all-to-all(bf16[16,5,8,128]{3,2,1,0:T(8,128)(2,1)S(1)} %get-tuple-element.12), channel_id=1, replica_groups={{352,384,416,448,480,0,32,64,96,128,160,192,224,256,288,320},{353,385,4..., dimensions={0} | all-to-all | bytes 327680 | tf_op jit(solution)/shard_map/all_to_all | solution.py:310
  28.3 2.6 %shard_map.74 = bf16[16,2,8,128]{3,2,1,0:T(8,128)(2,1)} custom-call(bf16[16,5,8,128]{3,2,1,0:T(8,128)(2,1)S(1)} %all_to_all.20.packed_ref, f32[8,128]{1,0:T(8,128)S(1)} %get-tuple-element.13.weights_ref, bf16[256,256]{1,0:T(8,128)(2,1)} %constant.35.clone.forward_hbm, bf16[256,256]{1,0:T(8,128)(2,1)} %constant.36.clone.inverse_hbm), custom_call_target="tpu_custom_call" | custom-call | flops 100000000 | bytes 600000 | tf_op jit(solution)/shard_map/pallas_call | solution.py:327
  31.0 10.1 %all-to-all-start.1 = ((bf16[16,2,8,128]{3,2,1,0:T(8,128)(2,1)}), bf16[16,2,8,128]{3,2,1,0:T(8,128)(2,1)S(1)}, u32[]{:S(2)}, u32[]{:S(2)}) async-start(bf16[16,2,8,128]{3,2,1,0:T(8,128)(2,1)} %shard_map.74), calls=%async_computation.1 | async-start | bytes 131072 | tf_op jit(solution)/shard_map/all_to_all | solution.py:353
  41.0 1.8 %shard_map.77 = (bf16[128,1024]{1,0:T(8,128)(2,1)S(1)}, bf16[128,1024]{1,0:T(8,128)(2,1)S(1)}, bf16[128,1024]{1,0:T(8,128)(2,1)S(1)}, bf16[128,1024]{1,0:T(8,128)(2,1)S(1)}) custom-call(s32[2]{0:T(128)S(1)} %pad_add_fusion.index_ref, bf16[128,4096]{1,0:T(8,128)(2,1)} %weight_hbm.1), custom_call_target="tpu_custom_call" | custom-call | bytes 2097152 | tf_op jit(solution)/shard_map/pallas_call | solution.py:311
  42.8 3.1 %collective-permute-start = (bf16[128,1024]{1,0:T(8,128)(2,1)S(1)}, bf16[128,1024]{1,0:T(8,128)(2,1)S(1)}, u32[]{:S(2)}, u32[]{:S(2)}) collective-permute-start(bf16[128,1024]{1,0:T(8,128)(2,1)S(1)} %get-tuple-element.16), channel_id=1, source_target_pairs={{0,8},{8,16},{16,24},{24,0},{1,9},{9,17},{17,25},{25,1},{2,10},{10... | collective-permute-start | bytes 786440 | tf_op jit(solution)/shard_map/ppermute | solution.py:322
  45.9 4.4 %collective-permute-start.1 = (bf16[128,1024]{1,0:T(8,128)(2,1)S(1)}, bf16[128,1024]{1,0:T(8,128)(2,1)S(1)}, u32[]{:S(2)}, u32[]{:S(2)}) collective-permute-start(bf16[128,1024]{1,0:T(8,128)(2,1)S(1)} %get-tuple-element.17), channel_id=1, source_target_pairs={{0,16},{8,24},{16,0},{24,8},{1,17},{9,25},{17,1},{25,9},{2,18},{10... | collective-permute-start | bytes 786440 | tf_op jit(solution)/shard_map/ppermute | solution.py:322
  50.3 3.1 %collective-permute-start.2 = (bf16[128,1024]{1,0:T(8,128)(2,1)S(1)}, bf16[128,1024]{1,0:T(8,128)(2,1)S(1)}, u32[]{:S(2)}, u32[]{:S(2)}) collective-permute-start(bf16[128,1024]{1,0:T(8,128)(2,1)S(1)} %get-tuple-element.18), channel_id=1, source_target_pairs={{0,24},{8,0},{16,8},{24,16},{1,25},{9,1},{17,9},{25,17},{2,26},{10... | collective-permute-start | bytes 786440 | tf_op jit(solution)/shard_map/ppermute | solution.py:322
  53.4 0.0 all-to-all-done.1.mixed_ref
  53.4 0.1 shard_map.75
  53.5 9.1 %all_to_all.21.row_ref = bf16[4,256,128]{2,1,0:T(8,128)(2,1)S(1)} all-to-all(bf16[4,256,128]{2,1,0:T(8,128)(2,1)S(1)} %shard_map.75), channel_id=1, replica_groups={{24,0,8,16},{25,1,9,17},{26,2,10,18},{27,3,11,19},{28,4,12,20},{29,5,13..., dimensions={0} | all-to-all | bytes 524288 | tf_op jit(solution)/shard_map/all_to_all | solution.py:363
  62.6 0.6 shard_map.76.lhs_ref
  63.2 0.0 collective-permute-done.refs_1_
  63.3 0.0 collective-permute-done.1.refs_2_
  63.3 0.0 collective-permute-done.2.refs_3_
  63.3 0.4 shard_map.78
  63.7 15.3 %all_to_all.22 = bf16[8,256,128]{2,1,0:T(8,128)(2,1)S(1)} all-to-all(bf16[8,256,128]{2,1,0:T(8,128)(2,1)S(1)} %shard_map.78), channel_id=1, replica_groups={{6,7,0,1,2,3,4,5},{14,15,8,9,10,11,12,13},{22,23,16,17,18,19,20,21},{30..., dimensions={0} | all-to-all | bytes 1048576 | tf_op jit(solution)/shard_map/all_to_all | solution.py:384
  79.0 0.7 reduce_sum.12
Async XLA Ops:
  31.0 22.4 %all-to-all-start.1 = ((bf16[16,2,8,128]{3,2,1,0:T(8,128)(2,1)}), bf16[16,2,8,128]{3,2,1,0:T(8,128)(2,1)S(1)}, u32[]{:S(2)}, u32[]{:S(2)}) async-start(bf16[16,2,8,128]{3,2,1,0:T(8,128)(2,1)} %shard_map.74), calls=%async_computation.1 | async-start | bytes 131072 | tf_op jit(solution)/shard_map/all_to_all | solution.py:353
  42.8 20.4 %collective-permute-start = (bf16[128,1024]{1,0:T(8,128)(2,1)S(1)}, bf16[128,1024]{1,0:T(8,128)(2,1)S(1)}, u32[]{:S(2)}, u32[]{:S(2)}) collective-permute-start(bf16[128,1024]{1,0:T(8,128)(2,1)S(1)} %get-tuple-element.16), channel_id=1, source_target_pairs={{0,8},{8,16},{16,24},{24,0},{1,9},{9,17},{17,25},{25,1},{2,10},{10... | collective-permute-start | bytes 786440 | tf_op jit(solution)/shard_map/ppermute | solution.py:322
  45.9 17.3 %collective-permute-start.1 = (bf16[128,1024]{1,0:T(8,128)(2,1)S(1)}, bf16[128,1024]{1,0:T(8,128)(2,1)S(1)}, u32[]{:S(2)}, u32[]{:S(2)}) collective-permute-start(bf16[128,1024]{1,0:T(8,128)(2,1)S(1)} %get-tuple-element.17), channel_id=1, source_target_pairs={{0,16},{8,24},{16,0},{24,8},{1,17},{9,25},{17,1},{25,9},{2,18},{10... | collective-permute-start | bytes 786440 | tf_op jit(solution)/shard_map/ppermute | solution.py:322
  50.3 13.0 %collective-permute-start.2 = (bf16[128,1024]{1,0:T(8,128)(2,1)S(1)}, bf16[128,1024]{1,0:T(8,128)(2,1)S(1)}, u32[]{:S(2)}, u32[]{:S(2)}) collective-permute-start(bf16[128,1024]{1,0:T(8,128)(2,1)S(1)} %get-tuple-element.18), channel_id=1, source_target_pairs={{0,24},{8,0},{16,8},{24,16},{1,25},{9,1},{17,9},{25,17},{2,26},{10... | collective-permute-start | bytes 786440 | tf_op jit(solution)/shard_map/ppermute | solution.py:322

commit v8 on v6

--- a/solution.py
+++ b/solution.py
@@ -41,10 +41,10 @@
 
 
 def pack_kernel(
-    index_ref, features_hbm, filter_hbm, taps_hbm, gain_hbm, out_ref, weights_ref, query_ref,
-    features_ref, filter_ref, taps_ref, gain_ref, extended, edges, rows, turned, sems,
+    index_ref, features_hbm, filter_hbm, taps_hbm, gain_hbm, out_hbm, weights_ref, query_ref,
+    features_ref, filter_ref, taps_ref, gain_ref, extended, edges, rows, turned, packed, sems, out_sems,
 ):
-    groups = out_ref.shape[0]
+    groups = out_hbm.shape[0]
     channels = LANES // groups
     streams = features_ref.shape[1]
     taps = taps_ref.shape[1]
@@ -59,8 +59,13 @@
     for copy in copies:
         copy.start()
 
+    sent = []
+
     def put(row, tile):
-        out_ref[:, row] = tile.T.astype(jnp.bfloat16).reshape(groups, channels, LANES)
+        packed[row] = tile.T.astype(jnp.bfloat16).reshape(groups, channels, LANES)
+        copy = pltpu.make_async_copy(packed.at[row], out_hbm.at[:, row], out_sems.at[row])
+        copy.start()
+        sent.append(copy)
 
     extended[:, :8] = jnp.zeros((streams, 8, LANES), jnp.float32)
     edges[...] = jnp.zeros_like(edges)
@@ -93,24 +98,18 @@
     turned[...] = rows[...].T
     first = pl.multiple_of(index_ref[0] * channels, channels)
     weights_ref[...] = turned[pl.ds(first, channels)]
+    for copy in sent:
+        copy.wait()
 
 
 def mix_kernel(
-    index_ref, packed_ref, weights_ref, forward_hbm, inverse_hbm, matrix_hbm, out_ref, matrix_ref,
+    packed_ref, weights_ref, forward_hbm, inverse_hbm, out_ref,
     query, keys, lags, key_spec, lag_spec, resp, total, forward_ref, inverse_ref, sems,
 ):
     forward_copy = pltpu.make_async_copy(forward_hbm, forward_ref, sems.at[0])
     inverse_copy = pltpu.make_async_copy(inverse_hbm, inverse_ref, sems.at[1])
     forward_copy.start()
     inverse_copy.start()
-    chips = matrix_ref.shape[0]
-    matrix_copies = []
-    for chip in range(chips):
-        block = 2 * ((chip + CHIP_FIRST) % chips) + index_ref[1]
-        columns = pl.ds(pl.multiple_of(block * LANES, LANES), LANES)
-        copy = pltpu.make_async_copy(matrix_hbm.at[:, columns], matrix_ref.at[chip], sems.at[2 + chip])
-        copy.start()
-        matrix_copies.append(copy)
     pairs = packed_ref.shape[0]
     blocks = 2 * pairs
     channels = packed_ref.shape[2]
@@ -181,6 +180,7 @@
     group = 4
     for base in range(0, blocks, group):
         sums = [None] * group
+        held = {}
         for block in range(base + group):
             real = key_spec[span(block), :LANES]
             imag = key_spec[span(block), LANES:]
@@ -189,11 +189,9 @@
                 gap = base + j - block
                 if gap < 0:
                     continue
-                terms = [
-                    real * resp[0, span(gap)],
-                    both * resp[1, span(gap)],
-                    imag * resp[2, span(gap)],
-                ]
+                if gap not in held:
+                    held[gap] = [resp[i, span(gap)] for i in range(3)]
+                terms = [one * other for one, other in zip((real, both, imag), held[gap])]
                 if sums[j] is not None:
                     terms = [one + other for one, other in zip(sums[j], terms)]
                 sums[j] = terms
@@ -211,8 +209,6 @@
         target, half = place(block)
         inner = total[span(block), :LANES] + gain * keys[span(block)].astype(jnp.float32)
         out_ref[target, half] = jnp.where(head, query[span(block)] * inner, inner).astype(jnp.bfloat16)
-    for copy in matrix_copies:
-        copy.wait()
 
 
 def activate_kernel(mixed_ref, query_ref, out_ref):
@@ -225,22 +221,33 @@
         out_ref[half * length : (half + 1) * length] = product.astype(jnp.bfloat16)
 
 
-def project_kernel(index_ref, both_ref, own_weight_ref, other_weight_ref, out_ref):
-    chips, _, width = out_ref.shape
+def regroup_kernel(index_ref, own_hbm, other_hbm, out_ref, sems):
+    chips = out_ref.shape[0] * out_ref.shape[2] // LANES
+    step = chips // out_ref.shape[0]
+    depth = own_hbm.shape[0]
+    copies = []
+    for chip in range(chips):
+        block = 2 * ((chip + CHIP_FIRST) % chips) + index_ref[1]
+        source = pl.ds(pl.multiple_of(block * LANES, LANES), LANES)
+        columns = slice(chip % step * LANES, (chip % step + 1) * LANES)
+        for i, weight in enumerate((own_hbm, other_hbm)):
+            target = out_ref.at[chip // step, i * depth : (i + 1) * depth, columns]
+            copies.append(pltpu.make_async_copy(weight.at[:, source], target, sems.at[i, chip]))
+    for copy in copies:
+        copy.start()
+    for copy in copies:
+        copy.wait()
+
+
+def project_kernel(index_ref, both_ref, weight_ref, out_ref):
+    width = out_ref.shape[2]
     core = index_ref[1]
     lhs = jnp.concatenate([both_ref[core], both_ref[1 - core]], axis=1)
-
-    def columns(chip):
-        block = 2 * ((chip + CHIP_FIRST) % chips) + core
-        other = other_weight_ref[:, pl.ds(pl.multiple_of(block * width, width), width)]
-        return jnp.concatenate([own_weight_ref[chip], other], axis=0)
-
-    step = math.gcd(chips, 2)
-    for first in range(0, chips, step):
-        weight = jnp.concatenate([columns(first + i) for i in range(step)], axis=1)
-        product = jnp.dot(lhs, weight, preferred_element_type=jnp.float32).astype(jnp.bfloat16)
+    step = weight_ref.shape[2] // width
+    for group in range(weight_ref.shape[0]):
+        product = jnp.dot(lhs, weight_ref[group], preferred_element_type=jnp.float32).astype(jnp.bfloat16)
         for i in range(step):
-            out_ref[first + i] = product[:, i * width : (i + 1) * width]
+            out_ref[group * step + i] = product[:, i * width : (i + 1) * width]
 
 
 def local(features, short_weight, long_filter, skip_gain, out_weight):
@@ -261,12 +268,12 @@
     packed, weights, query = pl.pallas_call(
         pack_kernel,
         out_shape=(
-            pltpu.VMEM((pairs, 5, channels, length), jnp.bfloat16),
+            pltpu.HBM((pairs, 5, channels, length), jnp.bfloat16),
             pltpu.VMEM((channels, LANES), jnp.float32),
             pltpu.VMEM((2, length, width), jnp.float32),
         ),
         in_specs=[scalars] + [hbm] * 4,
-        out_specs=(vmem, vmem, vmem),
+        out_specs=(hbm, vmem, vmem),
         scratch_shapes=[
             pltpu.VMEM((2, 3, length, width), jnp.bfloat16),
             pltpu.VMEM((2, length, width), jnp.bfloat16),
@@ -276,6 +283,8 @@
             pltpu.VMEM((LANES, LANES), jnp.float32),
             pltpu.VMEM((LANES, LANES), jnp.float32),
             pltpu.VMEM((LANES, LANES), jnp.float32),
+            pltpu.VMEM((5, pairs, channels, length), jnp.bfloat16),
+            pltpu.SemaphoreType.DMA((5,)),
             pltpu.SemaphoreType.DMA((5,)),
         ],
         compiler_params=pltpu.CompilerParams(vmem_limit_bytes=4 * MIB),
@@ -290,16 +299,24 @@
     )
     packed = lax.all_to_all(packed, "ctx", 0, 0, tiled=True, axis_index_groups=order)
     other_weight = lax.ppermute(out_weight, "core", [(0, 1), (1, 0)])
+    step = math.gcd(chips, 2)
+    columns = pl.pallas_call(
+        regroup_kernel,
+        out_shape=pltpu.VMEM((chips // step, 2 * width, step * width), jnp.bfloat16),
+        in_specs=[scalars, hbm, pl.BlockSpec(memory_space=pl.ANY)],
+        out_specs=vmem,
+        scratch_shapes=[pltpu.SemaphoreType.DMA((2, chips))],
+        compiler_params=pltpu.CompilerParams(vmem_limit_bytes=4 * MIB),
+        cost_estimate=pl.CostEstimate(flops=0, bytes_accessed=2 * MIB, transcendentals=0),
+        interpret=INTERPRET,
+    )(index, in_hbm(out_weight), other_weight)
     forward, inverse = tables()
     rows = 2 * pairs * channels
-    mixed, own_weight = pl.pallas_call(
+    mixed = pl.pallas_call(
         mix_kernel,
-        out_shape=(
-            pltpu.VMEM((pairs, 2, channels, length), jnp.bfloat16),
-            pltpu.VMEM((chips, width, width), jnp.bfloat16),
-        ),
-        in_specs=[scalars] + [vmem] * 2 + [hbm] * 3,
-        out_specs=(vmem, vmem),
+        out_shape=pltpu.VMEM((pairs, 2, channels, length), jnp.bfloat16),
+        in_specs=[vmem] * 2 + [hbm] * 2,
+        out_specs=vmem,
         scratch_shapes=[
             pltpu.VMEM((rows, LANES), jnp.float32),
             pltpu.VMEM((rows, LANES), jnp.bfloat16),
@@ -310,18 +327,16 @@
             pltpu.VMEM((rows, PERIOD), jnp.float32),
             pltpu.VMEM(forward.shape, jnp.bfloat16),
             pltpu.VMEM(inverse.shape, jnp.bfloat16),
-            pltpu.SemaphoreType.DMA((2 + chips,)),
+            pltpu.SemaphoreType.DMA((2,)),
         ],
         compiler_params=pltpu.CompilerParams(vmem_limit_bytes=6 * MIB),
         cost_estimate=pl.CostEstimate(flops=100000000, bytes_accessed=600000, transcendentals=0),
         interpret=INTERPRET,
     )(
-        index,
         packed,
         weights,
         in_hbm(jnp.asarray(forward)),
         in_hbm(jnp.asarray(inverse)),
-        in_hbm(out_weight),
     )
     mixed = lax.all_to_all(mixed, "ctx", 0, 0, tiled=True, axis_index_groups=order)
     activated = pl.pallas_call(
@@ -337,12 +352,12 @@
     partial = pl.pallas_call(
         project_kernel,
         out_shape=pltpu.VMEM((chips, 2 * length, width), jnp.bfloat16),
-        in_specs=[scalars] + [vmem] * 3,
+        in_specs=[scalars] + [vmem] * 2,
         out_specs=vmem,
         compiler_params=pltpu.CompilerParams(vmem_limit_bytes=8 * MIB),
         cost_estimate=pl.CostEstimate(flops=268435456, bytes_accessed=3300000, transcendentals=0),
         interpret=INTERPRET,
-    )(index, both, own_weight, other_weight)
+    )(index, both, columns)
     shares = lax.all_to_all(partial, "chip", 0, 0, tiled=True, axis_index_groups=chip_order)
     result = jnp.sum(shares.astype(jnp.float32), axis=0).astype(jnp.bfloat16)
     return result.reshape(2, 1, length, width)

time: 75.3 us -> 77.3 us (1.027)
  Pallas kernels: 5.84 us -> 7.58 us
    pallas_call x2 -> x3, Pallas kernels: 4.74 us -> 6.5 us  [the longest x1 2.65 us: local(): pl.pallas_call(pack_kernel, out_shape=(pltpu.HBM((pairs, 5, channels, len...]
  transfers between devices with their start and end apart: 1 -> 1, of which waited for: 0 -> 0; matrix products, arithmetic and copies ran while one was open for 0% -> 0% of each run, Pallas kernels for 7% -> 6%
where the time goes in v8:
time: 77.3 us; the launch traced here: 76 us
  blocking collectives  58.8 us (76%)
  starting transfers between devices  8.74 us (11%)
  Pallas kernels  7.58 us (10%)
  other arithmetic  0.85 us (1%)
    all_to_all x1, blocking collectives, local(): lax.all_to_all(packed, 'ctx', 0, 0, tiled=True, axis_index_groups=order)  21 us
    all_to_all x1, blocking collectives, local(): lax.all_to_all(partial, 'chip', 0, 0, tiled=True, axis_index_groups=chip_...  19.5 us
    all_to_all x1, blocking collectives, local(): lax.all_to_all(mixed, 'ctx', 0, 0, tiled=True, axis_index_groups=order)  15.1 us
    ppermute x1, starting transfers between devices, local(): other_weight = lax.ppermute(out_weight, 'core', [(0, 1), (1, 0)])  8.74 us
    all_gather x1, blocking collectives, local(): both = lax.all_gather(activated, 'core', axis=0)  3.2 us
    pallas_call x1, Pallas kernels, local(): pl.pallas_call(pack_kernel, out_shape=(pltpu.HBM((pairs, 5, channels, len...  2.65 us
    pallas_call x1, Pallas kernels, local(): pl.pallas_call(mix_kernel, out_shape=pltpu.VMEM((pairs, 2, channels, leng...  1.98 us
    pallas_call x1, Pallas kernels, local(): pl.pallas_call(regroup_kernel, out_shape=pltpu.VMEM((chips // step, 2 * w...  1.88 us
  transfers between devices with their start and end apart: 1, of which 0 were waited for; matrix products, arithmetic and copies ran while one was open for 0% of the time, Pallas kernels for 6%

profile of v8, /device:TPU:1, one launch (start us, length us, event | category | flops | bytes accessed | tf_op | source)
XLA Modules:
  0.0 76.0 jit_solution(14635133029991484472)
XLA Ops:
  0.0 8.7 %collective-permute-start = (bf16[128,4096]{1,0:T(8,128)(2,1)}, bf16[128,4096]{1,0:T(8,128)(2,1)S(1)}, u32[]{:S(2)}, u32[]{:S(2)}) collective-permute-start(bf16[128,4096]{1,0:T(8,128)(2,1)} %own_hbm.1), channel_id=1, source_target_pairs={{0,1},{1,0},{2,3},{3,2},{4,5},{5,4},{6,7},{7,6},{8,9},{9,8},{10,11... | collective-permute-start | bytes 3145736 | tf_op jit(solution)/shard_map/ppermute | solution.py:301
  8.8 0.1 pad_add_fusion.index_ref
  8.8 2.6 %shard_map.73 = (bf16[16,5,8,128]{3,2,1,0:T(8,128)(2,1)}, f32[8,128]{1,0:T(8,128)S(1)}, f32[2,128,128]{2,1,0:T(8,128)S(1)}) custom-call(s32[2]{0:T(128)S(1)} %pad_add_fusion.index_ref, bf16[2,3,128,128]{3,2,1,0:T(8,128)(2,1)} %bitcast.13, bf16[2,128,128]{2,1,0:T(8,128)(2,1)} %bitcast.14, bf16[3,7,128]{2,1,0:T(8,128)(2,1)} %bitcast.15, f32[1,128]{1,0:T(1,128)} %bitcast.16), custom_call_target="tpu_custom_call" | custom-call | flops 1000000 | bytes 600000 | tf_op jit(solution)/shard_map/pallas_call | solution.py:268
  11.5 21.0 %all_to_all.15.packed_ref = bf16[16,5,8,128]{3,2,1,0:T(8,128)(2,1)S(1)} all-to-all(bf16[16,5,8,128]{3,2,1,0:T(8,128)(2,1)} %get-tuple-element.8), channel_id=1, replica_groups={{352,384,416,448,480,0,32,64,96,128,160,192,224,256,288,320},{353,385,4..., dimensions={0} | all-to-all | bytes 327680 | tf_op jit(solution)/shard_map/all_to_all | solution.py:300
  32.5 2.0 %shard_map.74 = bf16[16,2,8,128]{3,2,1,0:T(8,128)(2,1)S(1)} custom-call(bf16[16,5,8,128]{3,2,1,0:T(8,128)(2,1)S(1)} %all_to_all.15.packed_ref, f32[8,128]{1,0:T(8,128)S(1)} %get-tuple-element.9.weights_ref, bf16[256,256]{1,0:T(8,128)(2,1)} %constant.34.clone.forward_hbm, bf16[256,256]{1,0:T(8,128)(2,1)} %constant.35.clone.inverse_hbm), custom_call_target="tpu_custom_call" | custom-call | flops 100000000 | bytes 600000 | tf_op jit(solution)/shard_map/pallas_call | solution.py:315
  34.5 15.1 %all_to_all.16.mixed_ref = bf16[16,2,8,128]{3,2,1,0:T(8,128)(2,1)S(1)} all-to-all(bf16[16,2,8,128]{3,2,1,0:T(8,128)(2,1)S(1)} %shard_map.74), channel_id=1, replica_groups={{352,384,416,448,480,0,32,64,96,128,160,192,224,256,288,320},{353,385,4..., dimensions={0} | all-to-all | bytes 131072 | tf_op jit(solution)/shard_map/all_to_all | solution.py:341
  49.5 0.1 shard_map.75
  49.6 3.2 %all-gather = bf16[512,128]{1,0:T(8,128)(2,1)S(1)} all-gather(bf16[256,128]{1,0:T(8,128)(2,1)S(1)} %shard_map.75), channel_id=2, replica_groups=mesh['ctx'=16,'chip'=16,'core'=2] {'core'}, dimensions={0}, use_global_device_ids=true | all-gather | bytes 196608 | tf_op jit(solution)/shard_map/all_gather | solution.py:351
  52.8 0.0 collective-permute-done.other_hbm
  52.8 1.9 %shard_map.76.weight_ref = bf16[8,256,256]{2,1,0:T(8,128)(2,1)S(1)} custom-call(s32[2]{0:T(128)S(1)} %pad_add_fusion.index_ref, bf16[128,4096]{1,0:T(8,128)(2,1)} %own_hbm.1, bf16[128,4096]{1,0:T(8,128)(2,1)S(1)} %collective-permute-done.other_hbm), custom_call_target="tpu_custom_call" | custom-call | bytes 2097152 | tf_op jit(solution)/shard_map/pallas_call | solution.py:303
  54.7 1.0 %shard_map.77 = bf16[16,256,128]{2,1,0:T(8,128)(2,1)S(1)} custom-call(s32[2]{0:T(128)S(1)} %pad_add_fusion.index_ref, bf16[2,256,128]{2,1,0:T(8,128)(2,1)S(1)} %bitcast.12, bf16[8,256,256]{2,1,0:T(8,128)(2,1)S(1)} %shard_map.76.weight_ref), custom_call_target="tpu_custom_call" | custom-call | flops 268435456 | bytes 3300000 | tf_op jit(solution)/shard_map/pallas_call | solution.py:352
  55.7 19.5 %all_to_all.17 = bf16[16,256,128]{2,1,0:T(8,128)(2,1)S(1)} all-to-all(bf16[16,256,128]{2,1,0:T(8,128)(2,1)S(1)} %shard_map.77), channel_id=1, replica_groups={{28,30,0,2,4,6,8,10,12,14,16,18,20,22,24,26},{29,31,1,3,5,7,9,11,13,15,..., dimensions={0} | all-to-all | bytes 2097152 | tf_op jit(solution)/shard_map/all_to_all | solution.py:361
  75.2 0.8 %reduce_sum.12 = bf16[256,128]{1,0:T(8,128)(2,1)} reduce(bf16[16,256,128]{2,1,0:T(8,128)(2,1)S(1)} %all_to_all.17, bf16[]{:T(256)} %constant.33.clone.1), dimensions={0}, to_apply=%region_0.1 | reduce | flops 491520 | bytes 1114114 | tf_op jit(solution)/shard_map/reduce_sum | solution.py:362
Async XLA Ops:
  0.0 52.8 %collective-permute-start = (bf16[128,4096]{1,0:T(8,128)(2,1)}, bf16[128,4096]{1,0:T(8,128)(2,1)S(1)}, u32[]{:S(2)}, u32[]{:S(2)}) collective-permute-start(bf16[128,4096]{1,0:T(8,128)(2,1)} %own_hbm.1), channel_id=1, source_target_pairs={{0,1},{1,0},{2,3},{3,2},{4,5},{5,4},{6,7},{7,6},{8,9},{9,8},{10,11... | collective-permute-start | bytes 3145736 | tf_op jit(solution)/shard_map/ppermute | solution.py:301

commit v9 on v8

--- a/solution.py
+++ b/solution.py
@@ -41,7 +41,7 @@
 
 
 def pack_kernel(
-    index_ref, features_hbm, filter_hbm, taps_hbm, gain_hbm, out_hbm, weights_ref, query_ref,
+    features_hbm, filter_hbm, taps_hbm, gain_hbm, out_hbm, weights_ref, query_ref,
     features_ref, filter_ref, taps_ref, gain_ref, extended, edges, rows, turned, packed, sems, out_sems,
 ):
     groups = out_hbm.shape[0]
@@ -96,20 +96,17 @@
         rows[stream * 8 : stream * 8 + taps] = taps_ref[stream].astype(jnp.float32)
     rows[streams * 8 : streams * 8 + 1] = gain_ref[...]
     turned[...] = rows[...].T
-    first = pl.multiple_of(index_ref[0] * channels, channels)
+    position = (lax.axis_index("ctx") + groups - CTX_FIRST) % groups
+    first = pl.multiple_of(position * channels, channels)
     weights_ref[...] = turned[pl.ds(first, channels)]
     for copy in sent:
         copy.wait()
 
 
 def mix_kernel(
-    packed_ref, weights_ref, forward_hbm, inverse_hbm, out_ref,
-    query, keys, lags, key_spec, lag_spec, resp, total, forward_ref, inverse_ref, sems,
+    packed_ref, weights_ref, forward_ref, inverse_ref, out_ref,
+    query, keys, lags, key_spec, lag_spec, resp, total,
 ):
-    forward_copy = pltpu.make_async_copy(forward_hbm, forward_ref, sems.at[0])
-    inverse_copy = pltpu.make_async_copy(inverse_hbm, inverse_ref, sems.at[1])
-    forward_copy.start()
-    inverse_copy.start()
     pairs = packed_ref.shape[0]
     blocks = 2 * pairs
     channels = packed_ref.shape[2]
@@ -163,7 +160,6 @@
             jnp.concatenate([values, values], axis=1), forward_ref[...], preferred_element_type=jnp.float32
         )
 
-    forward_copy.wait()
     key_spec[...] = transform(keys[...])
     lag_spec[...] = transform(lags[...])
     parity = jnp.where(lane % 2 == 0, 1.0, -1.0).astype(jnp.float32)
@@ -198,7 +194,6 @@
         for j in range(group):
             total[span(base + j), :LANES] = sums[j][0] - sums[j][1]
             total[span(base + j), LANES:] = sums[j][1] + sums[j][2]
-    inverse_copy.wait()
     high = total[...].astype(jnp.bfloat16)
     low = (total[...] - high.astype(jnp.float32)).astype(jnp.bfloat16)
     wide = jnp.dot(high, inverse_ref[...], preferred_element_type=jnp.float32)
@@ -221,17 +216,24 @@
         out_ref[half * length : (half + 1) * length] = product.astype(jnp.bfloat16)
 
 
-def regroup_kernel(index_ref, own_hbm, other_hbm, out_ref, sems):
+def regroup_kernel(
+    own_hbm, other_hbm, forward_hbm, inverse_hbm, out_ref, forward_ref, inverse_ref, sems, table_sems
+):
     chips = out_ref.shape[0] * out_ref.shape[2] // LANES
     step = chips // out_ref.shape[0]
     depth = own_hbm.shape[0]
-    copies = []
+    core = lax.axis_index("core")
+    copies = [
+        pltpu.make_async_copy(forward_hbm, forward_ref, table_sems.at[0]),
+        pltpu.make_async_copy(inverse_hbm, inverse_ref, table_sems.at[1]),
+    ]
     for chip in range(chips):
-        block = 2 * ((chip + CHIP_FIRST) % chips) + index_ref[1]
+        block = 2 * ((chip + CHIP_FIRST) % chips) + core
         source = pl.ds(pl.multiple_of(block * LANES, LANES), LANES)
         columns = slice(chip % step * LANES, (chip % step + 1) * LANES)
         for i, weight in enumerate((own_hbm, other_hbm)):
-            target = out_ref.at[chip // step, i * depth : (i + 1) * depth, columns]
+            rows = pl.ds(pl.multiple_of((core + i) % 2 * depth, depth), depth)
+            target = out_ref.at[chip // step, rows, columns]
             copies.append(pltpu.make_async_copy(weight.at[:, source], target, sems.at[i, chip]))
     for copy in copies:
         copy.start()
@@ -239,10 +241,9 @@
         copy.wait()
 
 
-def project_kernel(index_ref, both_ref, weight_ref, out_ref):
+def project_kernel(both_ref, weight_ref, out_ref):
     width = out_ref.shape[2]
-    core = index_ref[1]
-    lhs = jnp.concatenate([both_ref[core], both_ref[1 - core]], axis=1)
+    lhs = jnp.concatenate([both_ref[0], both_ref[1]], axis=1)
     step = weight_ref.shape[2] // width
     for group in range(weight_ref.shape[0]):
         product = jnp.dot(lhs, weight_ref[group], preferred_element_type=jnp.float32).astype(jnp.bfloat16)
@@ -258,11 +259,8 @@
     channels = width // pairs
     order = [[(place + CTX_FIRST) % pairs for place in range(pairs)]]
     chip_order = [[(place + CHIP_FIRST) % chips for place in range(chips)]]
-    position = (lax.axis_index("ctx") + pairs - CTX_FIRST) % pairs
-    index = jnp.stack([position, lax.axis_index("core")]).astype(jnp.int32)
     tiles = jnp.transpose(features, (0, 1, 3, 2, 4)).reshape(2, 3, length, width)
     taps = jnp.transpose(short_weight, (1, 0, 2))
-    scalars = pl.BlockSpec(memory_space=pltpu.SMEM)
     vmem = pl.BlockSpec(memory_space=pltpu.VMEM)
     hbm = pl.BlockSpec(memory_space=pltpu.HBM)
     packed, weights, query = pl.pallas_call(
@@ -272,7 +270,7 @@
             pltpu.VMEM((channels, LANES), jnp.float32),
             pltpu.VMEM((2, length, width), jnp.float32),
         ),
-        in_specs=[scalars] + [hbm] * 4,
+        in_specs=[hbm] * 4,
         out_specs=(hbm, vmem, vmem),
         scratch_shapes=[
             pltpu.VMEM((2, 3, length, width), jnp.bfloat16),
@@ -291,7 +289,6 @@
         cost_estimate=pl.CostEstimate(flops=1000000, bytes_accessed=600000, transcendentals=0),
         interpret=INTERPRET,
     )(
-        index,
         in_hbm(tiles),
         in_hbm(long_filter.reshape(2, length, width)),
         in_hbm(taps),
@@ -300,22 +297,26 @@
     packed = lax.all_to_all(packed, "ctx", 0, 0, tiled=True, axis_index_groups=order)
     other_weight = lax.ppermute(out_weight, "core", [(0, 1), (1, 0)])
     step = math.gcd(chips, 2)
-    columns = pl.pallas_call(
+    forward, inverse = tables()
+    columns, forward, inverse = pl.pallas_call(
         regroup_kernel,
-        out_shape=pltpu.VMEM((chips // step, 2 * width, step * width), jnp.bfloat16),
-        in_specs=[scalars, hbm, pl.BlockSpec(memory_space=pl.ANY)],
-        out_specs=vmem,
-        scratch_shapes=[pltpu.SemaphoreType.DMA((2, chips))],
+        out_shape=(
+            pltpu.VMEM((chips // step, 2 * width, step * width), jnp.bfloat16),
+            pltpu.VMEM(forward.shape, jnp.bfloat16),
+            pltpu.VMEM(inverse.shape, jnp.bfloat16),
+        ),
+        in_specs=[hbm, pl.BlockSpec(memory_space=pl.ANY), hbm, hbm],
+        out_specs=(vmem, vmem, vmem),
+        scratch_shapes=[pltpu.SemaphoreType.DMA((2, chips)), pltpu.SemaphoreType.DMA((2,))],
         compiler_params=pltpu.CompilerParams(vmem_limit_bytes=4 * MIB),
         cost_estimate=pl.CostEstimate(flops=0, bytes_accessed=2 * MIB, transcendentals=0),
         interpret=INTERPRET,
-    )(index, in_hbm(out_weight), other_weight)
-    forward, inverse = tables()
+    )(in_hbm(out_weight), other_weight, in_hbm(jnp.asarray(forward)), in_hbm(jnp.asarray(inverse)))
     rows = 2 * pairs * channels
     mixed = pl.pallas_call(
         mix_kernel,
         out_shape=pltpu.VMEM((pairs, 2, channels, length), jnp.bfloat16),
-        in_specs=[vmem] * 2 + [hbm] * 2,
+        in_specs=[vmem] * 4,
         out_specs=vmem,
         scratch_shapes=[
             pltpu.VMEM((rows, LANES), jnp.float32),
@@ -325,9 +326,6 @@
             pltpu.VMEM((rows, PERIOD), jnp.float32),
             pltpu.VMEM((3, rows, LANES), jnp.float32),
             pltpu.VMEM((rows, PERIOD), jnp.float32),
-            pltpu.VMEM(forward.shape, jnp.bfloat16),
-            pltpu.VMEM(inverse.shape, jnp.bfloat16),
-            pltpu.SemaphoreType.DMA((2,)),
         ],
         compiler_params=pltpu.CompilerParams(vmem_limit_bytes=6 * MIB),
         cost_estimate=pl.CostEstimate(flops=100000000, bytes_accessed=600000, transcendentals=0),
@@ -335,8 +333,8 @@
     )(
         packed,
         weights,
-        in_hbm(jnp.asarray(forward)),
-        in_hbm(jnp.asarray(inverse)),
+        forward,
+        inverse,
     )
     mixed = lax.all_to_all(mixed, "ctx", 0, 0, tiled=True, axis_index_groups=order)
     activated = pl.pallas_call(
@@ -352,12 +350,12 @@
     partial = pl.pallas_call(
         project_kernel,
         out_shape=pltpu.VMEM((chips, 2 * length, width), jnp.bfloat16),
-        in_specs=[scalars] + [vmem] * 2,
+        in_specs=[vmem] * 2,
         out_specs=vmem,
         compiler_params=pltpu.CompilerParams(vmem_limit_bytes=8 * MIB),
         cost_estimate=pl.CostEstimate(flops=268435456, bytes_accessed=3300000, transcendentals=0),
         interpret=INTERPRET,
-    )(index, both, columns)
+    )(both, columns)
     shares = lax.all_to_all(partial, "chip", 0, 0, tiled=True, axis_index_groups=chip_order)
     result = jnp.sum(shares.astype(jnp.float32), axis=0).astype(jnp.bfloat16)
     return result.reshape(2, 1, length, width)

time: 77.3 us -> 73.3 us (0.948)
  blocking collectives: 58.8 us -> 37.8 us
  starting transfers between devices: 8.74 us -> 19 us
  waiting for transfers between devices: 0.01 us -> 9.29 us
  Pallas kernels: 7.58 us -> 5.1 us
    all_to_all x1 -> x0, blocking collectives: 21 us -> none  [local(): lax.all_to_all(packed, 'ctx', 0, 0, tiled=True, axis_index_groups=order)]
    all_to_all x0 -> x1, starting transfers between devices: none -> 10.3 us  [local(): lax.all_to_all(packed, 'ctx', 0, 0, tiled=True, axis_index_groups=order)]
    all_to_all x0 -> x1, waiting for transfers between devices: none -> 9.29 us  [local(): lax.all_to_all(packed, 'ctx', 0, 0, tiled=True, axis_index_groups=order)]
    pallas_call x1, Pallas kernels: 1.98 us -> 1.01 us  [local(): pl.pallas_call(mix_kernel, out_shape=pltpu.VMEM((pairs, 2, channels, leng...]
  transfers between devices with their start and end apart: 1 -> 2, of which waited for: 0 -> 1; matrix products, arithmetic and copies ran while one was open for 0% -> 0% of each run, Pallas kernels for 6% -> 5%
where the time goes in v9:
time: 73.3 us; the launch traced here: 72 us
  blocking collectives  37.8 us (52%)
  starting transfers between devices  19 us (26%)
  waiting for transfers between devices  9.29 us (13%)
  Pallas kernels  5.1 us (7%)
  other arithmetic  0.77 us (1%)
    all_to_all x1, blocking collectives, local(): lax.all_to_all(partial, 'chip', 0, 0, tiled=True, axis_index_groups=chip_...  19.5 us
    all_to_all x1, blocking collectives, local(): lax.all_to_all(mixed, 'ctx', 0, 0, tiled=True, axis_index_groups=order)  15.1 us
    all_to_all x1, starting transfers between devices, local(): lax.all_to_all(packed, 'ctx', 0, 0, tiled=True, axis_index_groups=order)  10.3 us
    all_to_all x1, waiting for transfers between devices, local(): lax.all_to_all(packed, 'ctx', 0, 0, tiled=True, axis_index_groups=order)  9.29 us
    ppermute x1, starting transfers between devices, local(): other_weight = lax.ppermute(out_weight, 'core', [(0, 1), (1, 0)])  8.74 us
    all_gather x1, blocking collectives, local(): both = lax.all_gather(activated, 'core', axis=0)  3.2 us
    pallas_call x1, Pallas kernels, local(): pl.pallas_call(pack_kernel, out_shape=(pltpu.HBM((pairs, 5, channels, len...  2.12 us
  transfers between devices with their start and end apart: 2, of which 1 were waited for; matrix products, arithmetic and copies ran while one was open for 0% of the time, Pallas kernels for 5%

profile of v9, /device:TPU:1, one launch (start us, length us, event | category | flops | bytes accessed | tf_op | source)
XLA Modules:
  0.0 72.0 jit_solution(8684129698873530844)
XLA Ops:
  0.0 8.7 %collective-permute-start = (bf16[128,4096]{1,0:T(8,128)(2,1)}, bf16[128,4096]{1,0:T(8,128)(2,1)S(1)}, u32[]{:S(2)}, u32[]{:S(2)}) collective-permute-start(bf16[128,4096]{1,0:T(8,128)(2,1)} %own_hbm.1), channel_id=1, source_target_pairs={{0,1},{1,0},{2,3},{3,2},{4,5},{5,4},{6,7},{7,6},{8,9},{9,8},{10,11... | collective-permute-start | bytes 3145736 | tf_op jit(solution)/shard_map/ppermute | solution.py:298
  8.7 2.1 %shard_map.73 = (bf16[16,5,8,128]{3,2,1,0:T(8,128)(2,1)}, f32[8,128]{1,0:T(8,128)S(1)}, f32[2,128,128]{2,1,0:T(8,128)S(1)}) custom-call(bf16[2,3,128,128]{3,2,1,0:T(8,128)(2,1)} %bitcast.11, bf16[2,128,128]{2,1,0:T(8,128)(2,1)} %bitcast.12, bf16[3,7,128]{2,1,0:T(8,128)(2,1)} %bitcast.13, f32[1,128]{1,0:T(1,128)} %bitcast.14), custom_call_target="tpu_custom_call" | custom-call | flops 1000000 | bytes 600000 | tf_op jit(solution)/shard_map/pallas_call | solution.py:266
  10.9 10.3 %all-to-all-start = ((bf16[16,5,8,128]{3,2,1,0:T(8,128)(2,1)}), bf16[16,5,8,128]{3,2,1,0:T(8,128)(2,1)S(1)}, u32[]{:S(2)}, u32[]{:S(2)}) async-start(bf16[16,5,8,128]{3,2,1,0:T(8,128)(2,1)} %get-tuple-element.11), calls=%async_computation | async-start | bytes 327680 | tf_op jit(solution)/shard_map/all_to_all | solution.py:297
  21.1 0.0 collective-permute-done.other_hbm
  21.1 1.4 %shard_map.74 = (bf16[8,256,256]{2,1,0:T(8,128)(2,1)S(1)}, bf16[256,256]{1,0:T(8,128)(2,1)S(1)}, bf16[256,256]{1,0:T(8,128)(2,1)S(1)}) custom-call(bf16[128,4096]{1,0:T(8,128)(2,1)} %own_hbm.1, bf16[128,4096]{1,0:T(8,128)(2,1)S(1)} %collective-permute-done.other_hbm, bf16[256,256]{1,0:T(8,128)(2,1)} %constant.7.clone.forward_hbm, ...), custom_call_target="tpu_custom_call" | custom-call | bytes 2097152 | tf_op jit(solution)/shard_map/pallas_call | solution.py:301
  22.6 9.3 %all-to-all-done.packed_ref = bf16[16,5,8,128]{3,2,1,0:T(8,128)(2,1)S(1)} async-done(((bf16[16,5,8,128]{3,2,1,0:T(8,128)(2,1)}), bf16[16,5,8,128]{3,2,1,0:T(8,128)(2,1)S(1)}, u32[]{:S(2)}, u32[]{:S(2)}) %all-to-all-start) | async-done | bytes 163872 | tf_op jit(solution)/shard_map/all_to_all | solution.py:297
  31.9 1.0 %shard_map.75 = bf16[16,2,8,128]{3,2,1,0:T(8,128)(2,1)S(1)} custom-call(bf16[16,5,8,128]{3,2,1,0:T(8,128)(2,1)S(1)} %all-to-all-done.packed_ref, f32[8,128]{1,0:T(8,128)S(1)} %get-tuple-element.12.weights_ref, bf16[256,256]{1,0:T(8,128)(2,1)S(1)} %get-tuple-element.13.forward_ref, bf16[256,256]{1,0:T(8,128)(2,1)S(1)} %get-tuple-element.14.inverse_ref), custom_call_target="tpu_custom_call" | custom-call | flops 100000000 | bytes 600000 | tf_op jit(solution)/shard_map/pallas_call | solution.py:316
  32.9 15.1 %all_to_all.15.mixed_ref = bf16[16,2,8,128]{3,2,1,0:T(8,128)(2,1)S(1)} all-to-all(bf16[16,2,8,128]{3,2,1,0:T(8,128)(2,1)S(1)} %shard_map.75), channel_id=1, replica_groups={{352,384,416,448,480,0,32,64,96,128,160,192,224,256,288,320},{353,385,4..., dimensions={0} | all-to-all | bytes 131072 | tf_op jit(solution)/shard_map/all_to_all | solution.py:339
  47.9 0.1 shard_map.76
  48.1 3.2 %all-gather = bf16[512,128]{1,0:T(8,128)(2,1)S(1)} all-gather(bf16[256,128]{1,0:T(8,128)(2,1)S(1)} %shard_map.76), channel_id=2, replica_groups=mesh['ctx'=16,'chip'=16,'core'=2] {'core'}, dimensions={0}, use_global_device_ids=true | all-gather | bytes 196608 | tf_op jit(solution)/shard_map/all_gather | solution.py:349
  51.3 0.4 shard_map.77
  51.7 19.5 %all_to_all.16 = bf16[16,256,128]{2,1,0:T(8,128)(2,1)S(1)} all-to-all(bf16[16,256,128]{2,1,0:T(8,128)(2,1)S(1)} %shard_map.77), channel_id=1, replica_groups={{28,30,0,2,4,6,8,10,12,14,16,18,20,22,24,26},{29,31,1,3,5,7,9,11,13,15,..., dimensions={0} | all-to-all | bytes 2097152 | tf_op jit(solution)/shard_map/all_to_all | solution.py:359
  71.2 0.8 %reduce_sum.12 = bf16[256,128]{1,0:T(8,128)(2,1)} reduce(bf16[16,256,128]{2,1,0:T(8,128)(2,1)S(1)} %all_to_all.16, bf16[]{:T(256)} %constant.6.clone.1), dimensions={0}, to_apply=%region_0.0 | reduce | flops 491520 | bytes 1114114 | tf_op jit(solution)/shard_map/reduce_sum | solution.py:360
Async XLA Ops:
  0.0 21.1 %collective-permute-start = (bf16[128,4096]{1,0:T(8,128)(2,1)}, bf16[128,4096]{1,0:T(8,128)(2,1)S(1)}, u32[]{:S(2)}, u32[]{:S(2)}) collective-permute-start(bf16[128,4096]{1,0:T(8,128)(2,1)} %own_hbm.1), channel_id=1, source_target_pairs={{0,1},{1,0},{2,3},{3,2},{4,5},{5,4},{6,7},{7,6},{8,9},{9,8},{10,11... | collective-permute-start | bytes 3145736 | tf_op jit(solution)/shard_map/ppermute | solution.py:298
  10.9 21.0 %all-to-all-start = ((bf16[16,5,8,128]{3,2,1,0:T(8,128)(2,1)}), bf16[16,5,8,128]{3,2,1,0:T(8,128)(2,1)S(1)}, u32[]{:S(2)}, u32[]{:S(2)}) async-start(bf16[16,5,8,128]{3,2,1,0:T(8,128)(2,1)} %get-tuple-element.11), calls=%async_computation | async-start | bytes 327680 | tf_op jit(solution)/shard_map/all_to_all | solution.py:297

commit v10 on v9

--- a/solution.py
+++ b/solution.py
@@ -11,7 +11,8 @@
 INTERPRET = False
 MIB = 2**20
 CTX_FIRST = 11
-CHIP_FIRST = 14
+BACK_FIRST = 9
+CHIP_FIRST = 10
 LANES = 128
 PERIOD = 2 * LANES
 
@@ -201,17 +202,20 @@
     total[:, :LANES] = wide[:, :LANES] + (wide[:, LANES:] + narrow)
     gain = column(24)
     for block in range(blocks):
-        target, half = place(block)
+        owner, half = (block, 0) if block < pairs else (blocks - 1 - block, 1)
+        target = (owner - BACK_FIRST) % pairs
         inner = total[span(block), :LANES] + gain * keys[span(block)].astype(jnp.float32)
         out_ref[target, half] = jnp.where(head, query[span(block)] * inner, inner).astype(jnp.bfloat16)
 
 
 def activate_kernel(mixed_ref, query_ref, out_ref):
     groups, halves, channels, length = mixed_ref.shape
+    start = (CTX_FIRST - BACK_FIRST) % groups
     rim = 6
     token = lax.broadcasted_iota(jnp.int32, (length, LANES), 0)
     for half in range(halves):
-        inner = mixed_ref[:, half].reshape(groups * channels, length).astype(jnp.float32).T
+        parts = [mixed_ref[start:, half], mixed_ref[:start, half]]
+        inner = jnp.concatenate(parts, axis=0).reshape(groups * channels, length).astype(jnp.float32).T
         product = jnp.where(token < rim, inner, query_ref[half] * inner)
         out_ref[half * length : (half + 1) * length] = product.astype(jnp.bfloat16)
 
@@ -258,6 +262,7 @@
     width = features.shape[4]
     channels = width // pairs
     order = [[(place + CTX_FIRST) % pairs for place in range(pairs)]]
+    back_order = [[(place + BACK_FIRST) % pairs for place in range(pairs)]]
     chip_order = [[(place + CHIP_FIRST) % chips for place in range(chips)]]
     tiles = jnp.transpose(features, (0, 1, 3, 2, 4)).reshape(2, 3, length, width)
     taps = jnp.transpose(short_weight, (1, 0, 2))
@@ -311,7 +316,12 @@
         compiler_params=pltpu.CompilerParams(vmem_limit_bytes=4 * MIB),
         cost_estimate=pl.CostEstimate(flops=0, bytes_accessed=2 * MIB, transcendentals=0),
         interpret=INTERPRET,
-    )(in_hbm(out_weight), other_weight, in_hbm(jnp.asarray(forward)), in_hbm(jnp.asarray(inverse)))
+    )(
+        in_hbm(out_weight),
+        other_weight,
+        in_hbm(jnp.asarray(forward)),
+        in_hbm(jnp.asarray(inverse)),
+    )
     rows = 2 * pairs * channels
     mixed = pl.pallas_call(
         mix_kernel,
@@ -336,7 +346,7 @@
         forward,
         inverse,
     )
-    mixed = lax.all_to_all(mixed, "ctx", 0, 0, tiled=True, axis_index_groups=order)
+    mixed = lax.all_to_all(mixed, "ctx", 0, 0, tiled=True, axis_index_groups=back_order)
     activated = pl.pallas_call(
         activate_kernel,
         out_shape=pltpu.VMEM((2 * length, width), jnp.bfloat16),
@@ -372,6 +382,4 @@
         P(ch),
         P(ch, None),
     )
-    return jax.shard_map(
-        local, mesh=split, in_specs=in_specs, out_specs=P(None, "ctx", None, ch), check_vma=False
-    )
+    return jax.shard_map(local, mesh=split, in_specs=in_specs, out_specs=P(None, "ctx", None, ch), check_vma=False)

time: 73.3 us -> 73.4 us (level); the launches traced: 72 us -> 73 us
  blocking collectives: 37.8 us -> 38.8 us
    all_to_all x1, blocking collectives: 19.5 us -> 20.7 us  [local(): lax.all_to_all(partial, 'chip', 0, 0, tiled=True, axis_index_groups=chip_...]
where the time goes in v10:
time: 73.4 us; the launch traced here: 73 us
  blocking collectives  38.8 us (53%)
  starting transfers between devices  19 us (26%)
  waiting for transfers between devices  9.29 us (13%)
  Pallas kernels  5.1 us (7%)
  other arithmetic  0.77 us (1%)
    all_to_all x1, blocking collectives, local(): lax.all_to_all(partial, 'chip', 0, 0, tiled=True, axis_index_groups=chip_...  20.7 us
    all_to_all x1, blocking collectives, local(): lax.all_to_all(mixed, 'ctx', 0, 0, tiled=True, axis_index_groups=back_order)  14.4 us
    all_to_all x1, starting transfers between devices, local(): lax.all_to_all(packed, 'ctx', 0, 0, tiled=True, axis_index_groups=order)  10.3 us
    all_to_all x1, waiting for transfers between devices, local(): lax.all_to_all(packed, 'ctx', 0, 0, tiled=True, axis_index_groups=order)  9.29 us
    ppermute x1, starting transfers between devices, local(): other_weight = lax.ppermute(out_weight, 'core', [(0, 1), (1, 0)])  8.74 us
    all_gather x1, blocking collectives, local(): both = lax.all_gather(activated, 'core', axis=0)  3.68 us
    pallas_call x1, Pallas kernels, local(): pl.pallas_call(pack_kernel, out_shape=(pltpu.HBM((pairs, 5, channels, len...  2.12 us
  transfers between devices with their start and end apart: 2, of which 1 were waited for; matrix products, arithmetic and copies ran while one was open for 0% of the time, Pallas kernels for 5%

profile of v10, /device:TPU:1, one launch (start us, length us, event | category | flops | bytes accessed | tf_op | source)
XLA Modules:
  0.0 73.0 jit_solution(12741656677194992253)
XLA Ops:
  0.0 8.7 %collective-permute-start = (bf16[128,4096]{1,0:T(8,128)(2,1)}, bf16[128,4096]{1,0:T(8,128)(2,1)S(1)}, u32[]{:S(2)}, u32[]{:S(2)}) collective-permute-start(bf16[128,4096]{1,0:T(8,128)(2,1)} %own_hbm.1), channel_id=1, source_target_pairs={{0,1},{1,0},{2,3},{3,2},{4,5},{5,4},{6,7},{7,6},{8,9},{9,8},{10,11... | collective-permute-start | bytes 3145736 | tf_op jit(solution)/shard_map/ppermute | solution.py:303
  8.7 2.1 %shard_map.73 = (bf16[16,5,8,128]{3,2,1,0:T(8,128)(2,1)}, f32[8,128]{1,0:T(8,128)S(1)}, f32[2,128,128]{2,1,0:T(8,128)S(1)}) custom-call(bf16[2,3,128,128]{3,2,1,0:T(8,128)(2,1)} %bitcast.11, bf16[2,128,128]{2,1,0:T(8,128)(2,1)} %bitcast.12, bf16[3,7,128]{2,1,0:T(8,128)(2,1)} %bitcast.13, f32[1,128]{1,0:T(1,128)} %bitcast.14), custom_call_target="tpu_custom_call" | custom-call | flops 1000000 | bytes 600000 | tf_op jit(solution)/shard_map/pallas_call | solution.py:271
  10.9 10.3 %all-to-all-start = ((bf16[16,5,8,128]{3,2,1,0:T(8,128)(2,1)}), bf16[16,5,8,128]{3,2,1,0:T(8,128)(2,1)S(1)}, u32[]{:S(2)}, u32[]{:S(2)}) async-start(bf16[16,5,8,128]{3,2,1,0:T(8,128)(2,1)} %get-tuple-element.11), calls=%async_computation | async-start | bytes 327680 | tf_op jit(solution)/shard_map/all_to_all | solution.py:302
  21.1 0.0 collective-permute-done.other_hbm
  21.1 1.4 %shard_map.74 = (bf16[8,256,256]{2,1,0:T(8,128)(2,1)S(1)}, bf16[256,256]{1,0:T(8,128)(2,1)S(1)}, bf16[256,256]{1,0:T(8,128)(2,1)S(1)}) custom-call(bf16[128,4096]{1,0:T(8,128)(2,1)} %own_hbm.1, bf16[128,4096]{1,0:T(8,128)(2,1)S(1)} %collective-permute-done.other_hbm, bf16[256,256]{1,0:T(8,128)(2,1)} %constant.7.clone.forward_hbm, ...), custom_call_target="tpu_custom_call" | custom-call | bytes 2097152 | tf_op jit(solution)/shard_map/pallas_call | solution.py:306
  22.6 9.3 %all-to-all-done.packed_ref = bf16[16,5,8,128]{3,2,1,0:T(8,128)(2,1)S(1)} async-done(((bf16[16,5,8,128]{3,2,1,0:T(8,128)(2,1)}), bf16[16,5,8,128]{3,2,1,0:T(8,128)(2,1)S(1)}, u32[]{:S(2)}, u32[]{:S(2)}) %all-to-all-start) | async-done | bytes 163872 | tf_op jit(solution)/shard_map/all_to_all | solution.py:302
  31.9 1.0 %shard_map.75 = bf16[16,2,8,128]{3,2,1,0:T(8,128)(2,1)S(1)} custom-call(bf16[16,5,8,128]{3,2,1,0:T(8,128)(2,1)S(1)} %all-to-all-done.packed_ref, f32[8,128]{1,0:T(8,128)S(1)} %get-tuple-element.12.weights_ref, bf16[256,256]{1,0:T(8,128)(2,1)S(1)} %get-tuple-element.13.forward_ref, bf16[256,256]{1,0:T(8,128)(2,1)S(1)} %get-tuple-element.14.inverse_ref), custom_call_target="tpu_custom_call" | custom-call | flops 100000000 | bytes 600000 | tf_op jit(solution)/shard_map/pallas_call | solution.py:326
  32.9 14.4 %all_to_all.15.mixed_ref = bf16[16,2,8,128]{3,2,1,0:T(8,128)(2,1)S(1)} all-to-all(bf16[16,2,8,128]{3,2,1,0:T(8,128)(2,1)S(1)} %shard_map.75), channel_id=1, replica_groups={{288,320,352,384,416,448,480,0,32,64,96,128,160,192,224,256},{289,321,3..., dimensions={0} | all-to-all | bytes 131072 | tf_op jit(solution)/shard_map/all_to_all | solution.py:349
  47.3 0.1 shard_map.76
  47.4 3.7 %all-gather = bf16[512,128]{1,0:T(8,128)(2,1)S(1)} all-gather(bf16[256,128]{1,0:T(8,128)(2,1)S(1)} %shard_map.76), channel_id=2, replica_groups=mesh['ctx'=16,'chip'=16,'core'=2] {'core'}, dimensions={0}, use_global_device_ids=true | all-gather | bytes 196608 | tf_op jit(solution)/shard_map/all_gather | solution.py:359
  51.1 0.4 shard_map.77
  51.5 20.7 %all_to_all.16 = bf16[16,256,128]{2,1,0:T(8,128)(2,1)S(1)} all-to-all(bf16[16,256,128]{2,1,0:T(8,128)(2,1)S(1)} %shard_map.77), channel_id=1, replica_groups={{20,22,24,26,28,30,0,2,4,6,8,10,12,14,16,18},{21,23,25,27,29,31,1,3,5,7..., dimensions={0} | all-to-all | bytes 2097152 | tf_op jit(solution)/shard_map/all_to_all | solution.py:369
  72.2 0.8 %reduce_sum.12 = bf16[256,128]{1,0:T(8,128)(2,1)} reduce(bf16[16,256,128]{2,1,0:T(8,128)(2,1)S(1)} %all_to_all.16, bf16[]{:T(256)} %constant.6.clone.1), dimensions={0}, to_apply=%region_0.0 | reduce | flops 491520 | bytes 1114114 | tf_op jit(solution)/shard_map/reduce_sum | solution.py:370
Async XLA Ops:
  0.0 21.1 %collective-permute-start = (bf16[128,4096]{1,0:T(8,128)(2,1)}, bf16[128,4096]{1,0:T(8,128)(2,1)S(1)}, u32[]{:S(2)}, u32[]{:S(2)}) collective-permute-start(bf16[128,4096]{1,0:T(8,128)(2,1)} %own_hbm.1), channel_id=1, source_target_pairs={{0,1},{1,0},{2,3},{3,2},{4,5},{5,4},{6,7},{7,6},{8,9},{9,8},{10,11... | collective-permute-start | bytes 3145736 | tf_op jit(solution)/shard_map/ppermute | solution.py:303
  10.9 21.0 %all-to-all-start = ((bf16[16,5,8,128]{3,2,1,0:T(8,128)(2,1)}), bf16[16,5,8,128]{3,2,1,0:T(8,128)(2,1)S(1)}, u32[]{:S(2)}, u32[]{:S(2)}) async-start(bf16[16,5,8,128]{3,2,1,0:T(8,128)(2,1)} %get-tuple-element.11), calls=%async_computation | async-start | bytes 327680 | tf_op jit(solution)/shard_map/all_to_all | solution.py:302

commit v11 on v10

--- a/solution.py
+++ b/solution.py
@@ -11,8 +11,8 @@
 INTERPRET = False
 MIB = 2**20
 CTX_FIRST = 11
-BACK_FIRST = 9
-CHIP_FIRST = 10
+BACK_FIRST = 8
+CHIP_FIRST = 14
 LANES = 128
 PERIOD = 2 * LANES
 
@@ -57,8 +57,8 @@
         pltpu.make_async_copy(filter_hbm, filter_ref, sems.at[2]),
         pltpu.make_async_copy(gain_hbm, gain_ref, sems.at[4]),
     ]
-    for copy in copies:
-        copy.start()
+    for place in (3, 0, 1, 2, 4):
+        copies[place].start()
 
     sent = []
 
@@ -71,6 +71,9 @@
     extended[:, :8] = jnp.zeros((streams, 8, LANES), jnp.float32)
     edges[...] = jnp.zeros_like(edges)
     rows[...] = jnp.zeros_like(rows)
+    copies[3].wait()
+    for half in range(2):
+        put(2 + half, filter_ref[half].astype(jnp.float32))
     copies[0].wait()
     for half in range(2):
         copies[1 + half].wait()
@@ -88,9 +91,6 @@
             featured.append(summed)
         query_ref[half] = featured[0]
         put(half, featured[1] * featured[2])
-    copies[3].wait()
-    for half in range(2):
-        put(2 + half, filter_ref[half].astype(jnp.float32))
     put(4, edges[...])
     copies[4].wait()
     for stream in range(streams):

time: 73.4 us -> 73 us (level); the launches traced: 73 us -> 71.7 us
  blocking collectives: 38.8 us -> 37.6 us
    all_to_all x1, blocking collectives: 20.7 us -> 19.5 us  [local(): lax.all_to_all(partial, 'chip', 0, 0, tiled=True, axis_index_groups=chip_...]
where the time goes in v11:
time: 73 us; the launch traced here: 71.7 us
  blocking collectives  37.6 us (52%)
  starting transfers between devices  19 us (26%)
  waiting for transfers between devices  9.29 us (13%)
  Pallas kernels  5.02 us (7%)
  other arithmetic  0.77 us (1%)
    all_to_all x1, blocking collectives, local(): lax.all_to_all(partial, 'chip', 0, 0, tiled=True, axis_index_groups=chip_...  19.5 us
    all_to_all x1, blocking collectives, local(): lax.all_to_all(mixed, 'ctx', 0, 0, tiled=True, axis_index_groups=back_order)  14.4 us
    all_to_all x1, starting transfers between devices, local(): lax.all_to_all(packed, 'ctx', 0, 0, tiled=True, axis_index_groups=order)  10.3 us
    all_to_all x1, waiting for transfers between devices, local(): lax.all_to_all(packed, 'ctx', 0, 0, tiled=True, axis_index_groups=order)  9.29 us
    ppermute x1, starting transfers between devices, local(): other_weight = lax.ppermute(out_weight, 'core', [(0, 1), (1, 0)])  8.74 us
    all_gather x1, blocking collectives, local(): both = lax.all_gather(activated, 'core', axis=0)  3.68 us
    pallas_call x1, Pallas kernels, local(): pl.pallas_call(pack_kernel, out_shape=(pltpu.HBM((pairs, 5, channels, len...  2.04 us
  transfers between devices with their start and end apart: 2, of which 1 were waited for; matrix products, arithmetic and copies ran while one was open for 0% of the time, Pallas kernels for 5%

profile of v11, /device:TPU:1, one launch (start us, length us, event | category | flops | bytes accessed | tf_op | source)
XLA Modules:
  0.0 71.7 jit_solution(13739692211010182677)
XLA Ops:
  0.0 8.7 %collective-permute-start = (bf16[128,4096]{1,0:T(8,128)(2,1)}, bf16[128,4096]{1,0:T(8,128)(2,1)S(1)}, u32[]{:S(2)}, u32[]{:S(2)}) collective-permute-start(bf16[128,4096]{1,0:T(8,128)(2,1)} %own_hbm.1), channel_id=1, source_target_pairs={{0,1},{1,0},{2,3},{3,2},{4,5},{5,4},{6,7},{7,6},{8,9},{9,8},{10,11... | collective-permute-start | bytes 3145736 | tf_op jit(solution)/shard_map/ppermute | solution.py:303
  8.7 2.0 %shard_map.73 = (bf16[16,5,8,128]{3,2,1,0:T(8,128)(2,1)}, f32[8,128]{1,0:T(8,128)S(1)}, f32[2,128,128]{2,1,0:T(8,128)S(1)}) custom-call(bf16[2,3,128,128]{3,2,1,0:T(8,128)(2,1)} %bitcast.11, bf16[2,128,128]{2,1,0:T(8,128)(2,1)} %bitcast.12, bf16[3,7,128]{2,1,0:T(8,128)(2,1)} %bitcast.13, f32[1,128]{1,0:T(1,128)} %bitcast.14), custom_call_target="tpu_custom_call" | custom-call | flops 1000000 | bytes 600000 | tf_op jit(solution)/shard_map/pallas_call | solution.py:271
  10.8 10.3 %all-to-all-start = ((bf16[16,5,8,128]{3,2,1,0:T(8,128)(2,1)}), bf16[16,5,8,128]{3,2,1,0:T(8,128)(2,1)S(1)}, u32[]{:S(2)}, u32[]{:S(2)}) async-start(bf16[16,5,8,128]{3,2,1,0:T(8,128)(2,1)} %get-tuple-element.11), calls=%async_computation | async-start | bytes 327680 | tf_op jit(solution)/shard_map/all_to_all | solution.py:302
  21.1 0.0 collective-permute-done.other_hbm
  21.1 1.4 %shard_map.74 = (bf16[8,256,256]{2,1,0:T(8,128)(2,1)S(1)}, bf16[256,256]{1,0:T(8,128)(2,1)S(1)}, bf16[256,256]{1,0:T(8,128)(2,1)S(1)}) custom-call(bf16[128,4096]{1,0:T(8,128)(2,1)} %own_hbm.1, bf16[128,4096]{1,0:T(8,128)(2,1)S(1)} %collective-permute-done.other_hbm, bf16[256,256]{1,0:T(8,128)(2,1)} %constant.7.clone.forward_hbm, ...), custom_call_target="tpu_custom_call" | custom-call | bytes 2097152 | tf_op jit(solution)/shard_map/pallas_call | solution.py:306
  22.5 9.3 %all-to-all-done.packed_ref = bf16[16,5,8,128]{3,2,1,0:T(8,128)(2,1)S(1)} async-done(((bf16[16,5,8,128]{3,2,1,0:T(8,128)(2,1)}), bf16[16,5,8,128]{3,2,1,0:T(8,128)(2,1)S(1)}, u32[]{:S(2)}, u32[]{:S(2)}) %all-to-all-start) | async-done | bytes 163872 | tf_op jit(solution)/shard_map/all_to_all | solution.py:302
  31.8 1.0 %shard_map.75 = bf16[16,2,8,128]{3,2,1,0:T(8,128)(2,1)S(1)} custom-call(bf16[16,5,8,128]{3,2,1,0:T(8,128)(2,1)S(1)} %all-to-all-done.packed_ref, f32[8,128]{1,0:T(8,128)S(1)} %get-tuple-element.12.weights_ref, bf16[256,256]{1,0:T(8,128)(2,1)S(1)} %get-tuple-element.13.forward_ref, bf16[256,256]{1,0:T(8,128)(2,1)S(1)} %get-tuple-element.14.inverse_ref), custom_call_target="tpu_custom_call" | custom-call | flops 100000000 | bytes 600000 | tf_op jit(solution)/shard_map/pallas_call | solution.py:326
  32.8 14.4 %all_to_all.15.mixed_ref = bf16[16,2,8,128]{3,2,1,0:T(8,128)(2,1)S(1)} all-to-all(bf16[16,2,8,128]{3,2,1,0:T(8,128)(2,1)S(1)} %shard_map.75), channel_id=1, replica_groups={{256,288,320,352,384,416,448,480,0,32,64,96,128,160,192,224},{257,289,3..., dimensions={0} | all-to-all | bytes 131072 | tf_op jit(solution)/shard_map/all_to_all | solution.py:349
  47.2 0.1 shard_map.76
  47.3 3.7 %all-gather = bf16[512,128]{1,0:T(8,128)(2,1)S(1)} all-gather(bf16[256,128]{1,0:T(8,128)(2,1)S(1)} %shard_map.76), channel_id=2, replica_groups=mesh['ctx'=16,'chip'=16,'core'=2] {'core'}, dimensions={0}, use_global_device_ids=true | all-gather | bytes 196608 | tf_op jit(solution)/shard_map/all_gather | solution.py:359
  51.0 0.4 shard_map.77
  51.4 19.5 %all_to_all.16 = bf16[16,256,128]{2,1,0:T(8,128)(2,1)S(1)} all-to-all(bf16[16,256,128]{2,1,0:T(8,128)(2,1)S(1)} %shard_map.77), channel_id=1, replica_groups={{28,30,0,2,4,6,8,10,12,14,16,18,20,22,24,26},{29,31,1,3,5,7,9,11,13,15,..., dimensions={0} | all-to-all | bytes 2097152 | tf_op jit(solution)/shard_map/all_to_all | solution.py:369
  70.9 0.8 %reduce_sum.12 = bf16[256,128]{1,0:T(8,128)(2,1)} reduce(bf16[16,256,128]{2,1,0:T(8,128)(2,1)S(1)} %all_to_all.16, bf16[]{:T(256)} %constant.6.clone.1), dimensions={0}, to_apply=%region_0.0 | reduce | flops 491520 | bytes 1114114 | tf_op jit(solution)/shard_map/reduce_sum | solution.py:370
Async XLA Ops:
  0.0 21.1 %collective-permute-start = (bf16[128,4096]{1,0:T(8,128)(2,1)}, bf16[128,4096]{1,0:T(8,128)(2,1)S(1)}, u32[]{:S(2)}, u32[]{:S(2)}) collective-permute-start(bf16[128,4096]{1,0:T(8,128)(2,1)} %own_hbm.1), channel_id=1, source_target_pairs={{0,1},{1,0},{2,3},{3,2},{4,5},{5,4},{6,7},{7,6},{8,9},{9,8},{10,11... | collective-permute-start | bytes 3145736 | tf_op jit(solution)/shard_map/ppermute | solution.py:303
  10.8 21.0 %all-to-all-start = ((bf16[16,5,8,128]{3,2,1,0:T(8,128)(2,1)}), bf16[16,5,8,128]{3,2,1,0:T(8,128)(2,1)S(1)}, u32[]{:S(2)}, u32[]{:S(2)}) async-start(bf16[16,5,8,128]{3,2,1,0:T(8,128)(2,1)} %get-tuple-element.11), calls=%async_computation | async-start | bytes 327680 | tf_op jit(solution)/shard_map/all_to_all | solution.py:302
